TPU v7x, 128 devices: a whole 4x4x4 slice. The times are simulated.
128 devices in a mesh: dp: 4 (over y), ctx: 32 (over z, x, core).
Axes of the slice: x: 4, y: 4, z: 4, core: 2. Of those that a mesh axis runs over, the one named last changes fastest.
Arguments:
- tokens: bfloat16 [16384, 1536], P(('dp', 'ctx')), may hold values from -6 to 6
- segment_ids: int32 [4, 4096], P('dp', 'ctx'), may hold values from 0 to 15, never falling along the last dimension, each value on 1 to 3072 neighbouring positions
- expert_ids: int32 [16384, 2], P(('dp', 'ctx')), may hold values from 0 to 15, all different within a row
- w_query: bfloat16 [1536, 1536], P(('dp', 'ctx')), may hold values from -0.15625 to 0.15625
- w_key: bfloat16 [1536, 512], P(('dp', 'ctx')), may hold values from -0.3125 to 0.3125
- w_value: bfloat16 [1536, 512], P(('dp', 'ctx')), may hold values from -0.3125 to 0.3125
- w_out: bfloat16 [1536, 1536], P(None, ('dp', 'ctx')), may hold values from -0.625 to 0.625
- w_router: bfloat16 [1536, 16], P(('dp', 'ctx')), may hold values from -0.15625 to 0.15625
- gain_attn: bfloat16 [1536], P(('dp', 'ctx')), may hold values from 0.5 to 1.5
- gain_moe: bfloat16 [1536], P(('dp', 'ctx')), may hold values from 0.5 to 1.5
- w_gate: bfloat16 [1536, 16384], P('dp', 'ctx'), may hold values from -0.15625 to 0.15625
- w_up: bfloat16 [1536, 16384], P('dp', 'ctx'), may hold values from -0.15625 to 0.15625
- w_down: bfloat16 [16384, 1536], P('ctx', 'dp'), may hold values from -0.1875 to 0.1875
- cotangent: bfloat16 [16384, 1536], P(('dp', 'ctx')), may hold values from -6 to 6
Outputs:
- block_out: bfloat16 [16384, 1536], P(('dp', 'ctx'))
- grad_tokens: float32 [16384, 1536], P(('dp', 'ctx'))
- grad_w_query: float32 [1536, 1536], P(('dp', 'ctx'))
- grad_w_key: float32 [1536, 512], P(('dp', 'ctx'))
- grad_w_value: float32 [1536, 512], P(('dp', 'ctx'))
- grad_w_out: float32 [1536, 1536], P(None, ('dp', 'ctx'))
- grad_w_router: float32 [1536, 16], P(('dp', 'ctx'))
- grad_gain_attn: float32 [1536], P(('dp', 'ctx'))
- grad_gain_moe: float32 [1536], P(('dp', 'ctx'))
- grad_w_gate: float32 [1536, 16384], P('dp', 'ctx')
- grad_w_up: float32 [1536, 16384], P('dp', 'ctx')
- grad_w_down: float32 [16384, 1536], P('ctx', 'dp')
Inputs may be any that keep to these rules, and one draw needn't show every extreme that they name: `expert_ids`: each token names two different experts. `segment_ids`: within a sequence the ids never fall.
All inputs are finite; a program needn't handle non-finite values.
Results may differ from a plain program's by a relative error of at most 0.017.
The roundings to bfloat16 on the way count: a program that leaves them out, or rounds other values in their place, can miss the bound.
Values may be sent and summed in bfloat16 or wider, within the bound.
A program may use at most 192 MiB of HBM per device.

v0:
```python
import math

import jax
import jax.numpy as jnp
from jax import lax
from jax.sharding import PartitionSpec as P

MODEL_WIDTH = 1536
HEADS = 24
KV = 8
HD = 64
EXPERT_COUNT = 16
FF = 1024
EXPERT_CAPACITY = 20


EPS = 1e-05
SCALE_QK = 0.125
NEGATIVE = -1e30
HIGH_PRECISION = lax.Precision.HIGHEST


def norm_forward(values, gain):
    inverse = lax.rsqrt(jnp.mean(values * values, axis=-1, keepdims=True) + EPS)
    return (values * inverse * gain, inverse)


def norm_backward(values, inverse, gain, grad_out):
    scaled = grad_out * gain
    grad_in = inverse * scaled - values * inverse**3 * jnp.mean(
        values * scaled, axis=-1, keepdims=True
    )
    grad_gain = jnp.sum(grad_out * values * inverse, axis=0)
    return (grad_in, grad_gain)


def block_scores(q_heads, key_block):
    key_heads = key_block.reshape(key_block.shape[0], KV, HD)
    return (
        jnp.einsum("qkgd,skd->kgqs", q_heads, key_heads, preferred_element_type=jnp.float32)
        * SCALE_QK
    )


def local(
    tokens,
    segment_ids,
    expert_ids,
    w_query,
    w_key,
    w_value,
    w_out,
    w_router,
    gain_attn,
    gain_moe,
    w_gate,
    w_up,
    w_down,
    cotangent,
):
    dense_full = (
        lax.all_gather(w_query, ("dp", "ctx"), axis=0, tiled=True),
        lax.all_gather(w_key, ("dp", "ctx"), axis=0, tiled=True),
        lax.all_gather(w_value, ("dp", "ctx"), axis=0, tiled=True),
        lax.all_gather(w_out, ("dp", "ctx"), axis=1, tiled=True),
        lax.all_gather(w_router, ("dp", "ctx"), axis=0, tiled=True),
        lax.all_gather(gain_attn, ("dp", "ctx"), axis=0, tiled=True),
        lax.all_gather(gain_moe, ("dp", "ctx"), axis=0, tiled=True),
    )
    expert_full = (
        lax.all_gather(w_gate, "dp", axis=0, tiled=True),
        lax.all_gather(w_up, "dp", axis=0, tiled=True),
        lax.all_gather(w_down, "dp", axis=1, tiled=True),
    )
    full_query, full_key, full_value, full_out, full_router, full_gain_a, full_gain_m = dense_full
    rows_loc = tokens.shape[0]
    per_group = HEADS // KV
    n_ctx = lax.axis_size("ctx")
    hid_dev = w_gate.shape[1]
    exp_loc = max(1, hid_dev // FF)
    split_count = max(1, FF // hid_dev)
    ff_dev = hid_dev // exp_loc
    slot_count = EXPERT_CAPACITY * exp_loc
    inputs = tokens.astype(jnp.float32)
    normed_f, inverse_a = norm_forward(inputs, full_gain_a.astype(jnp.float32))
    normed = normed_f.astype(jnp.bfloat16)
    queries = jnp.dot(normed, full_query, preferred_element_type=jnp.float32).astype(jnp.bfloat16)
    keys_loc = jnp.dot(normed, full_key, preferred_element_type=jnp.float32).astype(jnp.bfloat16)
    values_loc = jnp.dot(normed, full_value, preferred_element_type=jnp.float32).astype(
        jnp.bfloat16
    )
    key_all, value_all, seg_all = (
        lax.all_gather(keys_loc, "ctx", axis=0, tiled=True),
        lax.all_gather(values_loc, "ctx", axis=0, tiled=True),
        lax.all_gather(segment_ids[0], "ctx", axis=0, tiled=True),
    )
    seq_len = key_all.shape[0]
    block_rows = math.gcd(seq_len, 512)
    block_count = seq_len // block_rows
    first_row = lax.axis_index("ctx") * rows_loc
    row_pos = first_row + jnp.arange(rows_loc, dtype=jnp.int32)
    row_seg = segment_ids[0]
    q_heads = queries.reshape(rows_loc, KV, per_group, HD)

    def block_view(block_index):
        offset = block_index * block_rows
        key_block = lax.dynamic_slice_in_dim(key_all, offset, block_rows, 0)
        value_block = lax.dynamic_slice_in_dim(value_all, offset, block_rows, 0)
        seg_block = lax.dynamic_slice_in_dim(seg_all, offset, block_rows, 0)
        col_pos = offset + jnp.arange(block_rows, dtype=jnp.int32)
        allowed = (row_pos[:, None] >= col_pos[None, :]) & (row_seg[:, None] == seg_block[None, :])
        is_live = (
            (offset <= first_row + rows_loc - 1)
            & (seg_block[-1] >= row_seg[0])
            & (seg_block[0] <= row_seg[-1])
        )
        return (key_block, value_block, allowed, is_live)

    def stats_step(running, block_index):
        key_block, value_block, allowed, is_live = block_view(block_index)

        def stats_compute(state_in):
            top_old, total_old = state_in
            scores = jnp.where(allowed, block_scores(q_heads, key_block), NEGATIVE)
            top_new = jnp.maximum(top_old, jnp.max(scores, axis=-1))
            exponent = jnp.where(allowed, jnp.exp(scores - top_new[..., None]), 0.0)
            return (top_new, total_old * jnp.exp(top_old - top_new) + jnp.sum(exponent, axis=-1))

        return (lax.cond(is_live, stats_compute, lambda state_in: state_in, running), None)

    stat_shape = (KV, per_group, rows_loc)
    (top_all, total_all), _ = lax.scan(
        stats_step,
        (jnp.full(stat_shape, NEGATIVE, jnp.float32), jnp.zeros(stat_shape, jnp.float32)),
        jnp.arange(block_count),
    )
    log_total = top_all + jnp.log(total_all)

    def mix_step(accum, block_index):
        key_block, value_block, allowed, is_live = block_view(block_index)

        def mix_compute(acc_in):
            scores = block_scores(q_heads, key_block)
            prob_low = jnp.where(allowed, jnp.exp(scores - log_total[..., None]), 0.0).astype(
                jnp.bfloat16
            )
            value_heads = value_block.reshape(block_rows, KV, HD)
            return acc_in + jnp.einsum(
                "kgqs,skd->qkgd", prob_low, value_heads, preferred_element_type=jnp.float32
            )

        return (lax.cond(is_live, mix_compute, lambda acc_in: acc_in, accum), None)

    attn_heads, _ = lax.scan(
        mix_step, jnp.zeros((rows_loc, KV, per_group, HD), jnp.float32), jnp.arange(block_count)
    )
    attn_low = attn_heads.reshape(rows_loc, HEADS * HD).astype(jnp.bfloat16)
    middle = inputs + jnp.dot(attn_low, full_out, preferred_element_type=jnp.float32)
    moe_f, inverse_m = norm_forward(middle, full_gain_m.astype(jnp.float32))
    mixture_input = moe_f.astype(jnp.bfloat16)
    logits = jnp.dot(mixture_input, full_router, preferred_element_type=jnp.float32)
    chosen = (
        expert_ids[:, :, None] == jnp.arange(EXPERT_COUNT, dtype=jnp.int32)[None, None, :]
    ).astype(jnp.float32)
    picked = jnp.sum(chosen * logits[:, None, :], axis=-1)
    gates = jax.nn.softmax(picked, axis=-1)
    gate_e = jnp.sum(chosen * gates[:, :, None], axis=1)
    used = jnp.sum(chosen, axis=1)
    earlier = (jnp.arange(rows_loc)[:, None] > jnp.arange(rows_loc)[None, :]).astype(jnp.bfloat16)
    before = jnp.dot(earlier, used.astype(jnp.bfloat16), preferred_element_type=jnp.float32)
    slot_hit = (used[..., None] > 0.5) & (
        before[..., None] == jnp.arange(EXPERT_CAPACITY, dtype=jnp.float32)
    )
    routing_choice = slot_hit.astype(jnp.float32).reshape(rows_loc, EXPERT_COUNT * EXPERT_CAPACITY)
    route_low = routing_choice.astype(jnp.bfloat16)
    weight_tokens = routing_choice * jnp.repeat(gate_e, EXPERT_CAPACITY, axis=1)
    slots_in = jnp.einsum(
        "tk,td->kd", route_low, mixture_input, preferred_element_type=jnp.float32
    ).astype(jnp.bfloat16)

    def spread_out(per_expert):
        grouped = jnp.repeat(
            per_expert.reshape(EXPERT_COUNT, EXPERT_CAPACITY, MODEL_WIDTH), split_count, axis=0
        )
        return grouped

    def gather_back(returned):
        return jnp.sum(
            returned.reshape(EXPERT_COUNT, split_count, EXPERT_CAPACITY, MODEL_WIDTH), axis=1
        ).reshape(EXPERT_COUNT * EXPERT_CAPACITY, MODEL_WIDTH)

    received = lax.all_to_all(spread_out(slots_in), "ctx", split_axis=0, concat_axis=0, tiled=True)
    expert_input = received.reshape(n_ctx, exp_loc, EXPERT_CAPACITY, MODEL_WIDTH)
    gate_w = expert_full[0].reshape(MODEL_WIDTH, exp_loc, ff_dev)
    up_w = expert_full[1].reshape(MODEL_WIDTH, exp_loc, ff_dev)
    down_w = expert_full[2].reshape(exp_loc, ff_dev, MODEL_WIDTH)
    gate_val = jnp.einsum(
        "slcd,dlf->slcf", expert_input, gate_w, preferred_element_type=jnp.float32
    )
    up_val = jnp.einsum("slcd,dlf->slcf", expert_input, up_w, preferred_element_type=jnp.float32)
    hidden = (jax.nn.silu(gate_val) * up_val).astype(jnp.bfloat16)
    part_out = jnp.einsum("slcf,lfd->slcd", hidden, down_w, preferred_element_type=jnp.float32)
    returned = lax.all_to_all(
        part_out.reshape(n_ctx, slot_count, MODEL_WIDTH).astype(jnp.bfloat16),
        "ctx",
        split_axis=0,
        concat_axis=0,
        tiled=True,
    ).astype(jnp.float32)
    expert_output = gather_back(returned)
    moe_sum = jnp.dot(weight_tokens, expert_output, precision=HIGH_PRECISION)
    block_out = (middle + moe_sum).astype(jnp.bfloat16)
    dense_back = (
        lax.all_gather(w_query, ("dp", "ctx"), axis=0, tiled=True),
        lax.all_gather(w_key, ("dp", "ctx"), axis=0, tiled=True),
        lax.all_gather(w_value, ("dp", "ctx"), axis=0, tiled=True),
        lax.all_gather(w_out, ("dp", "ctx"), axis=1, tiled=True),
        lax.all_gather(w_router, ("dp", "ctx"), axis=0, tiled=True),
        lax.all_gather(gain_attn, ("dp", "ctx"), axis=0, tiled=True),
        lax.all_gather(gain_moe, ("dp", "ctx"), axis=0, tiled=True),
    )
    expert_back = (
        lax.all_gather(w_gate, "dp", axis=0, tiled=True),
        lax.all_gather(w_up, "dp", axis=0, tiled=True),
        lax.all_gather(w_down, "dp", axis=1, tiled=True),
    )
    back_query, back_key, back_value, back_out, back_router, back_gain_a, back_gain_m = dense_back
    grad_output = cotangent.astype(jnp.float32)
    grad_slots = jnp.einsum(
        "tk,td->kd", weight_tokens, grad_output, precision=HIGH_PRECISION
    ).astype(jnp.bfloat16)
    grad_weigh = jnp.einsum("td,kd->tk", grad_output, expert_output, precision=HIGH_PRECISION)
    grad_gate_e = jnp.sum(
        (grad_weigh * routing_choice).reshape(rows_loc, EXPERT_COUNT, EXPERT_CAPACITY), axis=2
    )
    grad_pair = jnp.sum(chosen * grad_gate_e[:, None, :], axis=-1)
    grad_pick = gates * (grad_pair - jnp.sum(gates * grad_pair, axis=-1, keepdims=True))
    grad_logits = jnp.sum(chosen * grad_pick[:, :, None], axis=1)
    grad_received = lax.all_to_all(
        spread_out(grad_slots), "ctx", split_axis=0, concat_axis=0, tiled=True
    )
    grad_part = grad_received.reshape(n_ctx, exp_loc, EXPERT_CAPACITY, MODEL_WIDTH)
    back_gate_w = expert_back[0].reshape(MODEL_WIDTH, exp_loc, ff_dev)
    back_up_w = expert_back[1].reshape(MODEL_WIDTH, exp_loc, ff_dev)
    back_down_w = expert_back[2].reshape(exp_loc, ff_dev, MODEL_WIDTH)
    grad_hidden = jnp.einsum(
        "slcd,lfd->slcf", grad_part, back_down_w, preferred_element_type=jnp.float32
    )
    sigmoid_g = jax.nn.sigmoid(gate_val)
    grad_gate = (grad_hidden * up_val * sigmoid_g * (1.0 + gate_val * (1.0 - sigmoid_g))).astype(
        jnp.bfloat16
    )
    grad_up = (grad_hidden * gate_val * sigmoid_g).astype(jnp.bfloat16)
    grad_w_down = jnp.einsum(
        "slcf,slcd->lfd", hidden, grad_part, preferred_element_type=jnp.float32
    )
    grad_w_gate = jnp.einsum(
        "slcd,slcf->dlf", expert_input, grad_gate, preferred_element_type=jnp.float32
    )
    grad_w_up = jnp.einsum(
        "slcd,slcf->dlf", expert_input, grad_up, preferred_element_type=jnp.float32
    )
    grad_in_part = jnp.einsum(
        "slcf,dlf->slcd", grad_gate, back_gate_w, preferred_element_type=jnp.float32
    )
    grad_in_part = grad_in_part + jnp.einsum(
        "slcf,dlf->slcd", grad_up, back_up_w, preferred_element_type=jnp.float32
    )
    grad_returned = lax.all_to_all(
        grad_in_part.reshape(n_ctx, slot_count, MODEL_WIDTH).astype(jnp.bfloat16),
        "ctx",
        split_axis=0,
        concat_axis=0,
        tiled=True,
    ).astype(jnp.float32)
    grad_slots_in = gather_back(grad_returned)
    grad_moe_in = jnp.dot(routing_choice, grad_slots_in, precision=HIGH_PRECISION)
    grad_moe_in = grad_moe_in + jnp.einsum(
        "te,de->td", grad_logits, back_router.astype(jnp.float32), precision=HIGH_PRECISION
    )
    grad_w_router = jnp.einsum(
        "td,te->de", mixture_input.astype(jnp.float32), grad_logits, precision=HIGH_PRECISION
    )
    grad_mid_norm, grad_gain_moe = norm_backward(
        middle, inverse_m, back_gain_m.astype(jnp.float32), grad_moe_in
    )
    grad_middle = grad_output + grad_mid_norm
    grad_branch = grad_middle.astype(jnp.bfloat16)
    grad_w_out = jnp.einsum("th,td->hd", attn_low, grad_branch, preferred_element_type=jnp.float32)
    grad_attn = jnp.einsum(
        "td,hd->th", grad_branch, back_out, preferred_element_type=jnp.float32
    ).astype(jnp.bfloat16)
    grad_heads = grad_attn.reshape(rows_loc, KV, per_group, HD)
    delta_rows = jnp.einsum("qkgd,qkgd->kgq", grad_heads.astype(jnp.float32), attn_heads)

    def grad_step(accum, block_index):
        key_block, value_block, allowed, is_live = block_view(block_index)

        def grad_compute(acc_in):
            scores = block_scores(q_heads, key_block)
            prob_rows = jnp.where(allowed, jnp.exp(scores - log_total[..., None]), 0.0)
            prob_low = prob_rows.astype(jnp.bfloat16)
            key_heads = key_block.reshape(block_rows, KV, HD)
            value_heads = value_block.reshape(block_rows, KV, HD)
            grad_prob = jnp.einsum(
                "qkgd,skd->kgqs", grad_heads, value_heads, preferred_element_type=jnp.float32
            )
            grad_score = (prob_rows * (grad_prob - delta_rows[..., None])).astype(jnp.bfloat16)
            new_query = (
                acc_in
                + jnp.einsum(
                    "kgqs,skd->qkgd", grad_score, key_heads, preferred_element_type=jnp.float32
                )
                * SCALE_QK
            )
            grad_key = (
                jnp.einsum(
                    "kgqs,qkgd->skd", grad_score, q_heads, preferred_element_type=jnp.float32
                ).reshape(block_rows, KV * HD)
                * SCALE_QK
            )
            grad_value = jnp.einsum(
                "kgqs,qkgd->skd", prob_low, grad_heads, preferred_element_type=jnp.float32
            ).reshape(block_rows, KV * HD)
            return (new_query, grad_key, grad_value)

        def skipped(acc_in):
            zero_rows = jnp.zeros((block_rows, KV * HD), jnp.float32)
            return (acc_in, zero_rows, zero_rows)

        new_query, grad_key, grad_value = lax.cond(is_live, grad_compute, skipped, accum)
        return (new_query, (grad_key, grad_value))

    grad_q_heads, (grad_key_blocks, grad_value_blocks) = lax.scan(
        grad_step, jnp.zeros((rows_loc, KV, per_group, HD), jnp.float32), jnp.arange(block_count)
    )
    grad_key_seq = grad_key_blocks.reshape(seq_len, KV * HD)
    grad_value_seq = grad_value_blocks.reshape(seq_len, KV * HD)
    grad_key_own, grad_value_own = (
        lax.psum_scatter(
            grad_key_seq.astype(jnp.bfloat16), "ctx", scatter_dimension=0, tiled=True
        ).astype(jnp.float32),
        lax.psum_scatter(
            grad_value_seq.astype(jnp.bfloat16), "ctx", scatter_dimension=0, tiled=True
        ).astype(jnp.float32),
    )
    grad_query_low = grad_q_heads.reshape(rows_loc, HEADS * HD).astype(jnp.bfloat16)
    grad_key_low = grad_key_own.astype(jnp.bfloat16)
    grad_value_low = grad_value_own.astype(jnp.bfloat16)
    grad_normed = jnp.einsum(
        "th,dh->td", grad_query_low, back_query, preferred_element_type=jnp.float32
    )
    grad_normed = grad_normed + jnp.einsum(
        "th,dh->td", grad_key_low, back_key, preferred_element_type=jnp.float32
    )
    grad_normed = grad_normed + jnp.einsum(
        "th,dh->td", grad_value_low, back_value, preferred_element_type=jnp.float32
    )
    grad_w_query = jnp.einsum(
        "td,th->dh", normed, grad_query_low, preferred_element_type=jnp.float32
    )
    grad_w_key = jnp.einsum("td,th->dh", normed, grad_key_low, preferred_element_type=jnp.float32)
    grad_w_value = jnp.einsum(
        "td,th->dh", normed, grad_value_low, preferred_element_type=jnp.float32
    )
    grad_in_norm, grad_gain_attn = norm_backward(
        inputs, inverse_a, back_gain_a.astype(jnp.float32), grad_normed
    )
    grad_tokens = grad_middle + grad_in_norm
    dense_grads = (
        lax.psum_scatter(grad_w_query, ("dp", "ctx"), scatter_dimension=0, tiled=True),
        lax.psum_scatter(grad_w_key, ("dp", "ctx"), scatter_dimension=0, tiled=True),
        lax.psum_scatter(grad_w_value, ("dp", "ctx"), scatter_dimension=0, tiled=True),
        lax.psum_scatter(grad_w_out, ("dp", "ctx"), scatter_dimension=1, tiled=True),
        lax.psum_scatter(grad_w_router, ("dp", "ctx"), scatter_dimension=0, tiled=True),
        lax.psum_scatter(grad_gain_attn, ("dp", "ctx"), scatter_dimension=0, tiled=True),
        lax.psum_scatter(grad_gain_moe, ("dp", "ctx"), scatter_dimension=0, tiled=True),
    )
    expert_grads = (
        lax.psum_scatter(
            grad_w_gate.reshape(MODEL_WIDTH, hid_dev).astype(jnp.bfloat16),
            "dp",
            scatter_dimension=0,
            tiled=True,
        ).astype(jnp.float32),
        lax.psum_scatter(
            grad_w_up.reshape(MODEL_WIDTH, hid_dev).astype(jnp.bfloat16),
            "dp",
            scatter_dimension=0,
            tiled=True,
        ).astype(jnp.float32),
        lax.psum_scatter(
            grad_w_down.reshape(hid_dev, MODEL_WIDTH).astype(jnp.bfloat16),
            "dp",
            scatter_dimension=1,
            tiled=True,
        ).astype(jnp.float32),
    )
    return (
        block_out,
        grad_tokens,
        dense_grads[0],
        dense_grads[1],
        dense_grads[2],
        dense_grads[3],
        dense_grads[4],
        dense_grads[5],
        dense_grads[6],
        expert_grads[0],
        expert_grads[1],
        expert_grads[2],
    )


def solution(mesh):
    placed = (
        P(("dp", "ctx"), None),
        P("dp", "ctx"),
        P(("dp", "ctx"), None),
        P(("dp", "ctx"), None),
        P(("dp", "ctx"), None),
        P(("dp", "ctx"), None),
        P(None, ("dp", "ctx")),
        P(("dp", "ctx"), None),
        P(("dp", "ctx")),
        P(("dp", "ctx")),
        P("dp", "ctx"),
        P("dp", "ctx"),
        P("ctx", "dp"),
        P(("dp", "ctx"), None),
    )
    return jax.shard_map(
        local,
        mesh=mesh,
        in_specs=placed,
        out_specs=(
            P(("dp", "ctx"), None),
            P(("dp", "ctx"), None),
            P(("dp", "ctx"), None),
            P(("dp", "ctx"), None),
            P(("dp", "ctx"), None),
            P(None, ("dp", "ctx")),
            P(("dp", "ctx"), None),
            P(("dp", "ctx")),
            P(("dp", "ctx")),
            P("dp", "ctx"),
            P("dp", "ctx"),
            P("ctx", "dp"),
        ),
        check_vma=False,
    )
```

profile of v0, /device:TPU:1, one launch (start us, length us, event | category | flops | bytes accessed | tf_op | source)
XLA Modules:
  0.0 2198.1 jit_solution(11136203148756179013)
XLA Ops:
  11.8 69.8 %all-reduce.15 = (bf16[1536]{0:T(1024)(128)(2,1)S(1)}, bf16[1536]{0:T(1024)(128)(2,1)S(1)}) all-reduce(bf16[1536]{0:T(1024)(128)(2,1)S(1)} %dynamic-update-slice, bf16[1536]{0:T(1024)(128)(2,1)S(1)} %dynamic-update-slice.1), channel_id=1, replica_groups=mesh['dp'=4,'ctx'=32] {'dp','ctx'}, use_global_device_ids=true, to_apply=%add | all-reduce | flops 3072 | bytes 12288
  87.0 59.1 %all-gather.30.cloned.1.call-done = bf16[128,12,512]{2,1,0:T(8,128)(2,1)} async-done(((bf16[1,12,512]{2,1,0:T(8,128)(2,1)}), bf16[128,12,512]{2,1,0:T(8,128)(2,1)}) %all-gather.30.cloned.1.call-update) | async-done | bytes 1572880 | tf_op jit(solution)/shard_map/all_gather | solution.py:64
  151.6 25.9 %all-gather = s32[1,4096]{1,0:T(1,128)S(1)} all-gather(s32[1,128]{1,0:T(1,128)S(1)} %copy-done.24), channel_id=2, replica_groups=mesh['dp'=4,'ctx'=32] {'ctx'}, dimensions={1}, use_global_device_ids=true | all-gather | bytes 16896 | tf_op jit(solution)/shard_map/all_gather | solution.py:95
  177.8 37.1 %all-gather.28.cloned.1.call-done = bf16[128,12,1536]{2,1,0:T(8,128)(2,1)} async-done(((bf16[1,12,1536]{2,1,0:T(8,128)(2,1)}), bf16[128,12,1536]{2,1,0:T(8,128)(2,1)}) %all-gather.28.cloned.1.call-update) | async-done | bytes 4718608 | tf_op jit(solution)/shard_map/all_gather | solution.py:62
  226.6 57.2 %all-gather.32.cloned.1.call-done = bf16[128,12,1536]{2,1,0:T(8,128)(2,1)} async-done(((bf16[1,12,1536]{2,1,0:T(8,128)(2,1)}), bf16[128,12,1536]{2,1,0:T(8,128)(2,1)}) %all-gather.32.cloned.1.call-update) | async-done | bytes 4718608 | tf_op jit(solution)/shard_map/all_gather | solution.py:65
  292.0 38.5 %all-gather.16.cloned.1.call-done = bf16[4096,512]{1,0:T(8,128)(2,1)} async-done(((bf16[128,512]{1,0:T(8,128)(2,1)}), bf16[4096,512]{1,0:T(8,128)(2,1)}) %all-gather.16.cloned.1.call-update) | async-done | bytes 4194320 | tf_op jit(solution)/shard_map/all_gather | solution.py:93
  337.0 40.9 %while.51 = (s32[]{:T(128)}, f32[8,3,128]{2,1,0:T(4,128)S(1)}, f32[8,3,128]{2,1,0:T(4,128)S(1)}, s32[8]{0:T(128)S(1)}, s32[]{:T(128)}, /*index=5*/s32[4096]{0:T(...) while((s32[]{:T(128)}, f32[8,3,128]{2,1,0:T(4,128)S(1)}, ...), condition=%wide.region_6.7_spmd.clone, body=%wide.region_1.6_spmd.clone.sunk | while | flops 214112912 | bytes 14922661 | solution.py:132
  385.6 40.4 %while.52 = (s32[]{:T(128)}, f32[128,8,3,64]{0,3,2,1:T(8,128)S(1)}, s32[8]{0:T(128)S(1)}, s32[]{:T(128)}, s32[4096]{0:T(1024)S(1)}, /*index=5*/s32[128]{0:T(128)...) while((s32[]{:T(128)}, f32[128,8,3,64]{0,3,2,1:T(8,128)S(1)}, ...), condition=%wide.region_10.11_spmd.clone, body=%wide.region_7.10_spmd.clone.sunk | while | flops 409338496 | bytes 5272469 | solution.py:154
  435.7 52.4 %all-to-all-start = ((bf16[32,20,1536]{2,1,0:T(8,128)(2,1)}), bf16[32,20,1536]{2,1,0:T(8,128)(2,1)S(1)}, u32[]{:S(2)}, u32[]{:S(2)}) async-start(bf16[32,20,1536]{2,1,0:T(8,128)(2,1)} %bitcast.308), calls=%async_computation | async-start | bytes 4718592 | tf_op jit(solution)/shard_map/all_to_all | solution.py:192
  488.8 30.0 %all-to-all-done = bf16[32,20,1536]{2,1,0:T(8,128)(2,1)S(1)} async-done(((bf16[32,20,1536]{2,1,0:T(8,128)(2,1)}), bf16[32,20,1536]{2,1,0:T(8,128)(2,1)S(1)}, u32[]{:S(2)}, u32[]{:S(2)}) %all-to-all-start) | async-done | bytes 1966112 | tf_op jit(solution)/shard_map/all_to_all | solution.py:192
  540.1 57.5 %all-gather.5 = bf16[128,12,16]{2,1,0:T(8,128)(2,1)S(1)} all-gather(bf16[1,12,16]{2,1,0:T(8,128)(2,1)S(1)} %bitcast.340), channel_id=1, replica_groups=mesh['dp'=4,'ctx'=32] {'dp','ctx'}, dimensions={0}, use_global_device_ids=true | all-gather | bytes 49536 | tf_op jit(solution)/shard_map/all_gather | solution.py:66
  615.7 35.5 %all_to_all.20 = bf16[32,20,1536]{2,1,0:T(8,128)(2,1)S(1)} all-to-all(bf16[32,20,1536]{2,1,0:T(8,128)(2,1)S(1)} %bitcast.309), channel_id=1, replica_groups=mesh['dp'=4,'ctx'=32] {'ctx'}, dimensions={0} | all-to-all | bytes 3932160 | tf_op jit(solution)/shard_map/all_to_all | solution.py:239
  663.4 30.6 %all-to-all-done.3 = bf16[32,20,1536]{2,1,0:T(8,128)(2,1)} async-done(((bf16[32,20,1536]{2,1,0:T(8,128)(2,1)}), bf16[32,20,1536]{2,1,0:T(8,128)(2,1)}, u32[]{:S(2)}, u32[]{:S(2)}) %all-to-all-start.3) | async-done | bytes 1966112 | tf_op jit(solution)/shard_map/all_to_all | solution.py:269
  701.6 69.6 %while.53 = (s32[]{:T(128)}, f32[128,8,3,64]{0,3,2,1:T(8,128)S(1)}, bf16[8,512,512]{2,1,0:T(8,128)(2,1)}, bf16[8,512,512]{2,1,0:T(8,128)(2,1)}, s32[8]{0:T(128)S...) while((s32[]{:T(128)}, f32[128,8,3,64]{0,3,2,1:T(8,128)S(1)}, ...), condition=%wide.region_27.28_spmd.clone, body=%wide.region_24.27_spmd.clone.sunk | while | flops 1023476352 | bytes 42243088 | solution.py:334
  801.0 101.1 %reduce-scatter.24.cloned.1.call-done = bf16[128,512]{1,0:T(8,128)(2,1)} async-done(((bf16[4096,512]{1,0:T(8,128)(2,1)}), bf16[128,512]{1,0:T(8,128)(2,1)}) %reduce-scatter.24.cloned.1.call-update) | async-done | bytes 131088 | tf_op jit(solution)/shard_map/reduce_scatter | solution.py:343
  905.3 82.2 %reduce-scatter.22.cloned.1.call-done = bf16[128,512]{1,0:T(8,128)(2,1)} async-done(((bf16[4096,512]{1,0:T(8,128)(2,1)}), bf16[128,512]{1,0:T(8,128)(2,1)}) %reduce-scatter.22.cloned.1.call-update) | async-done | bytes 131088 | tf_op jit(solution)/shard_map/reduce_scatter | solution.py:340
  990.8 416.1 %fusion.122 = (f32[16,1536]{1,0:T(8,128)}, f32[16,512]{1,0:T(8,128)S(1)}, f32[16,512]{1,0:T(8,128)S(1)}, f32[1536,16]{0,1:T(8,128)S(1)}, f32[16,16]{1,0:T(8,128)S(1)}) fusion(f32[1536,1536]{1,0:T(8,128)} %fusion.117, f32[1536,512]{1,0:T(8,128)} %fusion.115, f32[1536,512]{1,0:T(8,128)} %fusion.113, f32[1536,1536]{0,1:T(8,128)} %fusion.92, ...), kind=kCustom, calls=%all-reduce-scatter.5 | all-reduce-scatter fusion | flops 8421377 | bytes 25527296
  1597.6 30.3 %collective-permute-start.60 = (f32[16,512]{1,0:T(8,128)S(1)}, f32[16,512]{1,0:T(8,128)S(1)}, u32[]{:S(2)}, u32[]{:S(2)}) collective-permute-start(f32[16,512]{1,0:T(8,128)S(1)} %get-tuple-element.1169), channel_id=1, source_target_pairs={{0,29},{1,30},{2,31},{3,32},{4,33},{5,34},{6,35},{7,36},{8,37},{9,... | collective-permute-start | bytes 98312
  1927.3 63.6 %all-reduce.14 = (f32[1536]{0:T(1024)S(1)}, f32[1536]{0:T(1024)S(1)}) all-reduce(f32[1536]{0:T(1024)S(1)} %copy-done.147, f32[1536]{0:T(1024)} %get-tuple-element.1073), channel_id=10, replica_groups=mesh['dp'=4,'ctx'=32] {'dp','ctx'}, use_global_device_ids=true, to_apply=%region_37.38.clone | all-reduce | flops 3072 | bytes 24576
  1992.0 24.6 %concatenate.4 = f32[524,16]{1,0:T(8,128)S(1)} concatenate(f32[12,16]{1,0:T(8,128)} %collective-permute-done.159, f32[16,16]{1,0:T(8,128)} %collective-permute-done.158, f32[16,16]{1,0:T(8,128)} %collective-permute-done.157, f32[16,16]{1,0:T(8,128)} %collective-permute-done.156, f32[16,16]{1,0:T(8,128)} %collective-permute-done.155, f32[16,16]{1,0:T(8,128)} %collective-permute-done.154, ...), dimensions={0} | concatenate | bytes 67072
  2037.7 20.2 concatenate.1
  2058.0 21.6 concatenate.2
  2113.4 31.7 %concatenate = f32[524,1536]{1,0:T(8,128)S(1)} concatenate(f32[12,1536]{1,0:T(8,128)S(1)} %copy-done.42, f32[16,1536]{1,0:T(8,128)} %collective-permute-done.30, f32[16,1536]{1,0:T(8,128)} %collective-permute-done.29, f32[16,1536]{1,0:T(8,128)} %collective-permute-done.28, f32[16,1536]{1,0:T(8,128)} %copy-done.43, f32[16,1536]{1,0:T(8,128)} %copy-done.44, ...), dimensions={0} | concatenate | bytes 6438912
  2160.7 30.0 %concatenate.3 = f32[1536,524]{0,1:T(8,128)S(1)} concatenate(f32[1536,12]{0,1:T(8,128)S(1)} %copy-done.40, f32[1536,16]{0,1:T(8,128)} %copy-done.51, f32[1536,16]{0,1:T(8,128)} %copy-done.54, f32[1536,16]{0,1:T(8,128)} %copy-done.56, f32[1536,16]{0,1:T(8,128)} %copy-done.58, f32[1536,16]{0,1:T(8,128)} %copy-done.60, f32[1536,16]{0,1:T(8,128)} %copy-done.62, ...), dimensions={1} | concatenate | bytes 6438912
  (1021 shorter events, 803.3 us)
Async XLA Ops:
  7.2 76.1 %all-gather.26.cloned.1.call-start = ((), (), s32[]{:S(2)}) async-start(), calls=%async_computation.16 | async-start | bytes 2113536 | tf_op jit(solution)/shard_map/all_gather | solution.py:63
  7.9 138.2 %all-gather.30.cloned.1.call-start = ((), (), s32[]{:S(2)}) async-start(), calls=%async_computation.18 | async-start | bytes 2113536 | tf_op jit(solution)/shard_map/all_gather | solution.py:64
  8.7 206.3 %all-gather.28.cloned.1.call-start = ((), (), s32[]{:S(2)}) async-start(), calls=%async_computation.17 | async-start | bytes 6340608 | tf_op jit(solution)/shard_map/all_gather | solution.py:62
  9.4 274.4 %all-gather.32.cloned.1.call-start = ((), (), s32[]{:S(2)}) async-start(), calls=%async_computation.19 | async-start | bytes 6340608 | tf_op jit(solution)/shard_map/all_gather | solution.py:65
  10.0 320.5 %all-gather.16.cloned.1.call-start = ((), (), s32[]{:S(2)}) async-start(), calls=%async_computation.9 | async-start | bytes 4325376 | tf_op jit(solution)/shard_map/all_gather | solution.py:93
  87.0 292.1 %all-gather.18.cloned.1.call-start = ((), (), s32[]{:S(2)}) async-start(), calls=%async_computation.10 | async-start | bytes 4325376 | tf_op jit(solution)/shard_map/all_gather | solution.py:94
  149.8 339.0 %all-gather.20.cloned.1.call-start = ((), (), s32[]{:S(2)}) async-start(), calls=%async_computation.11 | async-start | bytes 1966080 | tf_op jit(solution)/shard_map/all_gather | solution.py:71
  150.6 372.8 %all-gather.22.cloned.1.call-start = ((), (), s32[]{:S(2)}) async-start(), calls=%async_computation.12 | async-start | bytes 1966080 | tf_op jit(solution)/shard_map/all_gather | solution.py:72
  435.7 83.1 %all-to-all-start = ((bf16[32,20,1536]{2,1,0:T(8,128)(2,1)}), bf16[32,20,1536]{2,1,0:T(8,128)(2,1)S(1)}, u32[]{:S(2)}, u32[]{:S(2)}) async-start(bf16[32,20,1536]{2,1,0:T(8,128)(2,1)} %bitcast.308), calls=%async_computation | async-start | bytes 4718592 | tf_op jit(solution)/shard_map/all_to_all | solution.py:192
  533.0 65.6 %all-to-all-start.1 = ((bf16[32,20,1536]{2,1,0:T(8,128)(2,1)}), bf16[32,20,1536]{2,1,0:T(8,128)(2,1)}, u32[]{:S(2)}, u32[]{:S(2)}) async-start(bf16[32,20,1536]{2,1,0:T(8,128)(2,1)} %copy.105), calls=%async_computation.1 | async-start | bytes 4718592 | tf_op jit(solution)/shard_map/all_to_all | solution.py:203
  663.2 239.0 %reduce-scatter.24.cloned.1.call-start = ((), (), s32[]{:S(2)}) async-start(), calls=%async_computation.15 | async-start | bytes 4325376 | tf_op jit(solution)/shard_map/reduce_scatter | solution.py:343
  771.2 216.3 %reduce-scatter.22.cloned.1.call-start = ((), (), s32[]{:S(2)}) async-start(), calls=%async_computation.14 | async-start | bytes 4325376 | tf_op jit(solution)/shard_map/reduce_scatter | solution.py:340
  772.0 1087.8 %reduce-scatter.30.cloned.1.call-start = ((), (), s32[]{:S(2)}) async-start(), calls=%async_computation.22 | async-start | bytes 1966080
  777.2 1084.7 %reduce-scatter.26.cloned.1.call-start = ((), (), s32[]{:S(2)}) async-start(), calls=%async_computation.20 | async-start | bytes 1966080
  782.2 1081.9 %reduce-scatter.28.cloned.1.call-start = ((), (), s32[]{:S(2)}) async-start(), calls=%async_computation.21 | async-start | bytes 1966080
  1423.6 204.3 %collective-permute-start.95 = (f32[12,512]{1,0:T(8,128)S(1)}, f32[12,512]{1,0:T(8,128)S(1)}, u32[]{:S(2)}, u32[]{:S(2)}) collective-permute-start(f32[12,512]{1,0:T(8,128)S(1)} %slice.74), channel_id=1, source_target_pairs={{0,32},{1,33},{2,34},{3,35},{4,36},{5,37},{6,38},{7,39},{8,40},{9,... | collective-permute-start | bytes 73736
  1426.3 204.2 %collective-permute-start.62 = (f32[16,512]{1,0:T(8,128)S(1)}, f32[16,512]{1,0:T(8,128)S(1)}, u32[]{:S(2)}, u32[]{:S(2)}) collective-permute-start(f32[16,512]{1,0:T(8,128)S(1)} %get-tuple-element.1169), channel_id=1, source_target_pairs={{0,31},{1,32},{2,33},{3,34},{4,35},{5,36},{6,37},{7,38},{8,39},{9,... | collective-permute-start | bytes 98312
  1430.0 201.9 %collective-permute-start.61 = (f32[16,512]{1,0:T(8,128)S(1)}, f32[16,512]{1,0:T(8,128)S(1)}, u32[]{:S(2)}, u32[]{:S(2)}) collective-permute-start(f32[16,512]{1,0:T(8,128)S(1)} %get-tuple-element.1169), channel_id=1, source_target_pairs={{0,30},{1,31},{2,32},{3,33},{4,34},{5,35},{6,36},{7,37},{8,38},{9,... | collective-permute-start | bytes 98312
  1491.6 137.7 %collective-permute-start.63 = (f32[12,512]{1,0:T(8,128)S(1)}, f32[12,512]{1,0:T(8,128)S(1)}, u32[]{:S(2)}, u32[]{:S(2)}) collective-permute-start(f32[12,512]{1,0:T(8,128)S(1)} %slice.73), channel_id=1, source_target_pairs={{0,32},{1,33},{2,34},{3,35},{4,36},{5,37},{6,38},{7,39},{8,40},{9,... | collective-permute-start | bytes 73736
  1910.3 106.3 %collective-permute-start.120 = (f32[1536,16]{0,1:T(8,128)S(1)}, f32[1536,16]{0,1:T(8,128)S(1)}, u32[]{:S(2)}, u32[]{:S(2)}) collective-permute-start(f32[1536,16]{0,1:T(8,128)S(1)} %copy-done.26), channel_id=1, source_target_pairs={{0,25},{1,26},{2,27},{3,28},{4,29},{5,30},{6,31},{7,32},{8,33},{9,... | collective-permute-start | bytes 294920
  1912.7 109.2 %collective-permute-start.119 = (f32[1536,16]{0,1:T(8,128)S(1)}, f32[1536,16]{0,1:T(8,128)S(1)}, u32[]{:S(2)}, u32[]{:S(2)}) collective-permute-start(f32[1536,16]{0,1:T(8,128)S(1)} %copy-done.26), channel_id=1, source_target_pairs={{0,24},{1,25},{2,26},{3,27},{4,28},{5,29},{6,30},{7,31},{8,32},{9,... | collective-permute-start | bytes 294920
  1914.6 111.5 %collective-permute-start.118 = (f32[1536,16]{0,1:T(8,128)S(1)}, f32[1536,16]{0,1:T(8,128)S(1)}, u32[]{:S(2)}, u32[]{:S(2)}) collective-permute-start(f32[1536,16]{0,1:T(8,128)S(1)} %copy-done.26), channel_id=1, source_target_pairs={{0,23},{1,24},{2,25},{3,26},{4,27},{5,28},{6,29},{7,30},{8,31},{9,... | collective-permute-start | bytes 294920
  1916.0 114.3 %collective-permute-start.117 = (f32[1536,16]{0,1:T(8,128)S(1)}, f32[1536,16]{0,1:T(8,128)S(1)}, u32[]{:S(2)}, u32[]{:S(2)}) collective-permute-start(f32[1536,16]{0,1:T(8,128)S(1)} %copy-done.26), channel_id=1, source_target_pairs={{0,22},{1,23},{2,24},{3,25},{4,26},{5,27},{6,28},{7,29},{8,30},{9,... | collective-permute-start | bytes 294920
  1924.3 108.8 %collective-permute-start.116 = (f32[1536,16]{0,1:T(8,128)S(1)}, f32[1536,16]{0,1:T(8,128)S(1)}, u32[]{:S(2)}, u32[]{:S(2)}) collective-permute-start(f32[1536,16]{0,1:T(8,128)S(1)} %copy-done.26), channel_id=1, source_target_pairs={{0,21},{1,22},{2,23},{3,24},{4,25},{5,26},{6,27},{7,28},{8,29},{9,... | collective-permute-start | bytes 294920
  (320 other events, 16626.0 us)
Sparse Core Ops, SparseCore 0:
  11.2 69.0 all-gather.25
  83.4 62.7 all-gather.29
  149.3 65.6 all-gather.27
  217.9 65.8 all-gather.31
  286.5 44.0 all-gather.15
  333.2 45.7 all-gather.17
  380.7 25.3 all-gather.19
  407.7 26.5 all-gather.21
  490.6 26.5 all-gather.23
  771.3 130.7 reduce-scatter.23
  906.2 81.2 reduce-scatter.21
  989.8 25.6 reduce-scatter.29
  1017.9 33.4 reduce-scatter.25
  1053.7 38.4 reduce-scatter.27
where the time goes:
time: 2220 us; the launch traced here: 2200 us
  blocking collectives  668 us (30%)
  starting transfers between devices  623 us (28%)
  waiting for transfers between devices  448 us (20%)
  local copies, waits for them, and re-layouts  259 us (12%)
  matrix products  86.3 us (4%)
  loops' own time  80 us (4%)
    unnamed x163, starting transfers between devices  558 us
    unnamed x3, blocking collectives  549 us
    unnamed x366, local copies, waits for them, and re-layouts  186 us
    reduce_scatter x1, waiting for transfers between devices, local(): lax.psum_scatter(grad_value_seq.astype(jnp.bfloat16), 'ctx', scatter_dime...  101 us
    reduce_scatter x1, waiting for transfers between devices, local(): lax.psum_scatter(grad_key_seq.astype(jnp.bfloat16), 'ctx', scatter_dimens...  82.2 us
    all_gather x1, waiting for transfers between devices, local(): lax.all_gather(w_value, ('dp', 'ctx'), axis=0, tiled=True)  59.1 us
    all_gather x1, blocking collectives, local(): lax.all_gather(w_router, ('dp', 'ctx'), axis=0, tiled=True)  57.5 us
    all_gather x1, waiting for transfers between devices, local(): lax.all_gather(w_out, ('dp', 'ctx'), axis=1, tiled=True)  57.2 us
  transfers between devices with their start and end apart: 177, of which 25 were waited for; matrix products, arithmetic and copies ran while one was open for 30% of the time, Pallas kernels for 0%

commit v1 on v0

v1 whole, which is shorter than its diff:
```python
import functools

import jax
import jax.numpy as jnp
from jax import lax
from jax.experimental import pallas as pl
from jax.experimental.pallas import tpu as pltpu
from jax.sharding import PartitionSpec as P

MODEL_WIDTH = 1536
HEADS = 24
KV = 8
HD = 64
EXPERT_COUNT = 16
FF = 1024
EXPERT_CAPACITY = 20
SLOTS = 24
ROWS = 128
PAIR = 256
HEAD_Q = 192
Q_HALF = 768
KV_HALF = 512
EXTRA = 128
PACK = Q_HALF + KV_HALF + EXTRA + Q_HALF

EPS = 1e-05
SCALE_QK = 0.125
NEGATIVE = -1e30
HIGH_PRECISION = lax.Precision.HIGHEST
MESH = pl.DeviceIdType.MESH
ANY = pl.BlockSpec(memory_space=pl.ANY)
IN_VMEM = pl.BlockSpec(memory_space=pltpu.VMEM)
BF = jnp.bfloat16
F32 = jnp.float32


def coords():
    i = lax.axis_index("ctx")
    return lax.axis_index("dp"), i // 8, (i // 2) % 4, i % 2


def dev(y, z, x, c):
    return (y, z * 8 + x * 2 + c)


def signal(target):
    pl.semaphore_signal(
        pltpu.get_barrier_semaphore(), inc=1, device_id=target, device_id_type=MESH
    )


def remote(src, dst, send, recv, target):
    return pltpu.make_async_remote_copy(
        src_ref=src, dst_ref=dst, send_sem=send, recv_sem=recv, device_id=target, device_id_type=MESH
    )


def params(cid, vmem=None):
    return pltpu.CompilerParams(collective_id=cid, has_side_effects=True, vmem_limit_bytes=vmem)


def axis_peer(axis, step):
    y, z, x, c = coords()
    if axis == "y":
        return dev((y + step) % 4, z, x, c)
    if axis == "z":
        return dev(y, (z + step) % 4, x, c)
    return dev(y, z, (x + step) % 4, c)


ORDERS = (("x", "z", "y"), ("y", "x", "z"), ("z", "y", "x"), ("y", "x", "z"))
WIDTHS = (Q_HALF, KV_HALF, Q_HALF, EXTRA)
STARTS = (0, Q_HALF, Q_HALF + KV_HALF, 2 * Q_HALF + KV_HALF)
PARTS = 4
STEPS = (1, 3, 2)


def slab(ref, done, y, z, x):
    return ref.at[
        slice(None) if "y" in done else y,
        slice(None) if "z" in done else z,
        slice(None) if "x" in done else x,
    ]


def gather_kernel(
    pack, tokens, segs, out0, out1, out2, out3, pair, seg_all,
    sib, block, p_send, p_recv, l_sem, s_send, s_recv, sib_send, sib_recv,
):
    y, z, x, c = coords()
    outs = (out0, out1, out2, out3)
    me = z * 8 + x * 2 + c
    sibling = dev(y, z, x, 1 - c)

    def greet(k, carry):
        signal((y, (me + k) % 32))
        return carry

    lax.fori_loop(1, 32, greet, 0)
    for step in STEPS:
        signal(axis_peer("y", step))
    pl.semaphore_wait(pltpu.get_barrier_semaphore(), 34)

    first = remote(pack.at[1 - c], sib, sib_send.at[0], sib_recv.at[0], sibling)
    first.start()
    second = remote(tokens, pair.at[c], sib_send.at[1], sib_recv.at[1], sibling)
    second.start()
    own_rows = pltpu.make_async_copy(tokens, pair.at[c], l_sem.at[4])
    own_rows.start()
    own_segs = pltpu.make_async_copy(segs, seg_all.at[me], l_sem.at[5])
    own_segs.start()

    def spread(k, carry):
        remote(segs, seg_all.at[me], s_send, s_recv, (y, (me + k) % 32)).start()
        return carry

    lax.fori_loop(1, 32, spread, 0)

    first.wait()
    own = pack[c, :12].astype(F32)
    other = sib[:12].astype(F32)
    low = jnp.where(c == 0, own, other)
    high = jnp.where(c == 0, other, own)
    block[...] = jnp.concatenate([low, high], axis=0).astype(BF)

    locals_ = []
    for part in range(PARTS):
        cols = pl.ds(STARTS[part], WIDTHS[part])
        here = pltpu.make_async_copy(block.at[:, cols], outs[part].at[y, z, x], l_sem.at[part])
        here.start()
        locals_.append(here)
    for phase in range(3):
        copies = []
        for part in range(PARTS):
            axis = ORDERS[part][phase]
            done = ORDERS[part][:phase]
            for n, step in enumerate(STEPS):
                dst = slab(outs[part], done, y, z, x)
                src = block.at[:, pl.ds(STARTS[part], WIDTHS[part])] if phase == 0 else dst
                copy = remote(
                    src, dst, p_send.at[phase, part, n], p_recv.at[phase, part, n], axis_peer(axis, step)
                )
                copy.start()
                copies.append(copy)
        if phase == 0:
            for here in locals_:
                here.wait()
        for copy in copies:
            copy.wait()
    second.wait()
    own_rows.wait()
    own_segs.wait()
    drain = remote(
        seg_all.at[pl.ds(0, 31)], seg_all.at[pl.ds(0, 31)], s_send, s_recv, sibling
    )
    drain.wait_send()
    drain.wait_recv()


def gather_weights(pack, tokens, segs):
    return pl.pallas_call(
        gather_kernel,
        out_shape=[jax.ShapeDtypeStruct((4, 4, 4, 24, width), BF) for width in WIDTHS]
        + [
            jax.ShapeDtypeStruct((2, ROWS, MODEL_WIDTH), BF),
            jax.ShapeDtypeStruct((32, 1, 128), jnp.int32),
        ],
        in_specs=[IN_VMEM, ANY, ANY],
        out_specs=[ANY] * 6,
        scratch_shapes=[
            pltpu.VMEM((16, PACK), BF),
            pltpu.VMEM((24, PACK), BF),
            pltpu.SemaphoreType.DMA((3, PARTS, 3)),
            pltpu.SemaphoreType.DMA((3, PARTS, 3)),
            pltpu.SemaphoreType.DMA((6,)),
            pltpu.SemaphoreType.DMA,
            pltpu.SemaphoreType.DMA,
            pltpu.SemaphoreType.DMA((2,)),
            pltpu.SemaphoreType.DMA((2,)),
        ],
        compiler_params=params(1),
        name="gather_weights",
    )(pack, tokens, segs)


def plane_greet(y, me, c, sibling):
    def greet(k, carry):
        t = (me + k) % 16
        signal(dev(y, t // 4, t % 4, c))
        return carry

    lax.fori_loop(1, 16, greet, 0)
    if sibling is not None:
        signal(sibling)
        pl.semaphore_wait(pltpu.get_barrier_semaphore(), 16)
    else:
        pl.semaphore_wait(pltpu.get_barrier_semaphore(), 15)


def heads_out_kernel(q4, kv4, half, q_in, kv_in, half_sib, l_sem, q_send, q_recv, k_send, k_recv, o_send, o_recv):
    y, z, x, c = coords()
    me = z * 4 + x
    sibling = dev(y, z, x, 1 - c)
    plane_greet(y, me, c, sibling)

    def send_kv(k, carry):
        t = (me + k) % 16
        remote(kv4.at[t // 4], kv_in.at[me], k_send, k_recv, dev(y, t // 4, t % 4, c)).start()
        return carry

    q_copies = []
    for n, step in enumerate(STEPS):
        to = (z + step) % 4
        copy = remote(q4.at[to], q_in.at[z], q_send.at[n], q_recv.at[n], dev(y, to, x, c))
        copy.start()
        q_copies.append(copy)
    lax.fori_loop(1, 16, send_kv, 0)
    swap = remote(half, half_sib, o_send, o_recv, sibling)
    swap.start()
    here = [
        pltpu.make_async_copy(q4.at[z], q_in.at[z], l_sem.at[0]),
        pltpu.make_async_copy(kv4.at[z], kv_in.at[me], l_sem.at[1]),
    ]
    for copy in here:
        copy.start()
    for copy in here:
        copy.wait()
    for copy in q_copies:
        copy.wait()
    drain = remote(kv_in.at[pl.ds(0, 15)], kv_in.at[pl.ds(0, 15)], k_send, k_recv, sibling)
    drain.wait_send()
    drain.wait_recv()
    swap.wait()


def heads_out(q4, kv4, half):
    return pl.pallas_call(
        heads_out_kernel,
        out_shape=[
            jax.ShapeDtypeStruct((4, PAIR, HEAD_Q), BF),
            jax.ShapeDtypeStruct((16, PAIR, 128), BF),
            jax.ShapeDtypeStruct((MODEL_WIDTH, Q_HALF), BF),
        ],
        in_specs=[ANY] * 3,
        out_specs=[ANY] * 3,
        scratch_shapes=[
            pltpu.SemaphoreType.DMA((3,)),
            pltpu.SemaphoreType.DMA((3,)),
            pltpu.SemaphoreType.DMA((3,)),
            pltpu.SemaphoreType.DMA,
            pltpu.SemaphoreType.DMA,
            pltpu.SemaphoreType.DMA,
            pltpu.SemaphoreType.DMA,
        ],
        compiler_params=params(2),
        name="heads_out",
    )(q4, kv4, half)


def heads_back_kernel(dq4, dkv, dq_in, dkv_in, l_sem, q_send, q_recv, k_send, k_recv):
    y, z, x, c = coords()
    me = z * 4 + x
    plane_greet(y, me, c, None)

    def send_kv(k, carry):
        t = (me + k) % 16
        remote(dkv.at[t], dkv_in.at[me], k_send, k_recv, dev(y, t // 4, t % 4, c)).start()
        return carry

    q_copies = []
    for n, step in enumerate(STEPS):
        to = (z + step) % 4
        copy = remote(dq4.at[to], dq_in.at[z], q_send.at[n], q_recv.at[n], dev(y, to, x, c))
        copy.start()
        q_copies.append(copy)
    lax.fori_loop(1, 16, send_kv, 0)
    here = [
        pltpu.make_async_copy(dq4.at[z], dq_in.at[z], l_sem.at[0]),
        pltpu.make_async_copy(dkv.at[me], dkv_in.at[me], l_sem.at[1]),
    ]
    for copy in here:
        copy.start()
    for copy in here:
        copy.wait()
    for copy in q_copies:
        copy.wait()
    neighbour = dev(y, (z + 1) % 4, x, c)
    drain = remote(dkv_in.at[pl.ds(0, 15)], dkv_in.at[pl.ds(0, 15)], k_send, k_recv, neighbour)
    drain.wait_send()
    drain.wait_recv()


def heads_back(dq4, dkv):
    return pl.pallas_call(
        heads_back_kernel,
        out_shape=[
            jax.ShapeDtypeStruct((4, PAIR, HEAD_Q), BF),
            jax.ShapeDtypeStruct((16, PAIR, 128), BF),
        ],
        in_specs=[ANY] * 2,
        out_specs=[ANY] * 2,
        scratch_shapes=[
            pltpu.SemaphoreType.DMA((2,)),
            pltpu.SemaphoreType.DMA((3,)),
            pltpu.SemaphoreType.DMA((3,)),
            pltpu.SemaphoreType.DMA,
            pltpu.SemaphoreType.DMA,
        ],
        compiler_params=params(3),
        name="heads_back",
    )(dq4, dkv)


def column_swap(blocks, send, recv, out, l_sem):
    y, z, x, c = coords()
    j = z * 2 + c

    def push(k, carry):
        t = (j + k) % 8
        remote(blocks.at[t], out.at[j], send, recv, dev(y, t // 2, x, t % 2)).start()
        return carry

    lax.fori_loop(1, 8, push, 0)
    here = pltpu.make_async_copy(blocks.at[j], out.at[j], l_sem)
    here.start()
    return here


def column_greet():
    y, z, x, c = coords()
    j = z * 2 + c

    def greet(k, carry):
        t = (j + k) % 8
        signal(dev(y, t // 2, x, t % 2))
        return carry

    lax.fori_loop(1, 8, greet, 0)
    pl.semaphore_wait(pltpu.get_barrier_semaphore(), 7)


def column_drain(send, recv, out):
    y, z, x, c = coords()
    drain = remote(out.at[pl.ds(0, 7)], out.at[pl.ds(0, 7)], send, recv, dev(y, z, x, 1 - c))
    drain.wait_send()
    drain.wait_recv()


def attn_return_kernel(blocks, out, l_sem, send, recv):
    column_greet()
    here = column_swap(blocks, send, recv, out, l_sem)
    here.wait()
    column_drain(send, recv, out)


def attn_return(blocks):
    return pl.pallas_call(
        attn_return_kernel,
        out_shape=jax.ShapeDtypeStruct((8, ROWS, HEAD_Q), BF),
        in_specs=[ANY],
        out_specs=ANY,
        scratch_shapes=[pltpu.SemaphoreType.DMA] * 3,
        compiler_params=params(4),
        name="attn_return",
    )(blocks)


def grad_attn_kernel(
    blocks, branch, attn, out, branch_sib, attn_sib, l_sem, send, recv, sib_send, sib_recv
):
    y, z, x, c = coords()
    sibling = dev(y, z, x, 1 - c)
    column_greet()
    here = column_swap(blocks, send, recv, out, l_sem)
    one = remote(branch, branch_sib, sib_send.at[0], sib_recv.at[0], sibling)
    one.start()
    two = remote(attn, attn_sib, sib_send.at[1], sib_recv.at[1], sibling)
    two.start()
    here.wait()
    column_drain(send, recv, out)
    one.wait()
    two.wait()


def grad_attn_out(blocks, branch, attn):
    return pl.pallas_call(
        grad_attn_kernel,
        out_shape=[
            jax.ShapeDtypeStruct((8, ROWS, HEAD_Q), BF),
            jax.ShapeDtypeStruct((ROWS, MODEL_WIDTH), BF),
            jax.ShapeDtypeStruct((ROWS, Q_HALF), BF),
        ],
        in_specs=[ANY] * 3,
        out_specs=[ANY] * 3,
        scratch_shapes=[pltpu.SemaphoreType.DMA] * 3
        + [pltpu.SemaphoreType.DMA((2,)), pltpu.SemaphoreType.DMA((2,))],
        compiler_params=params(5),
        name="grad_attn_out",
    )(blocks, branch, attn)


def dispatch_kernel(xs, gs, x_in, g_in, l_sem, send, recv, f_send, f_recv):
    y, z, x, c = coords()
    me = z * 4 + x
    sibling = dev(y, z, x, 1 - c)
    plane_greet(y, me, c, sibling)
    pairs = ((xs, x_in), (gs, g_in))

    for a, (src, dst) in enumerate(pairs):

        def push(k, carry):
            t = (me + k) % 16
            remote(
                src.at[t], dst.at[c, me], send.at[a, k], recv.at[a, k], dev(y, t // 4, t % 4, c)
            ).start()
            return carry

        lax.fori_loop(1, 16, push, 0)
    here = []
    for a, (src, dst) in enumerate(pairs):
        copy = pltpu.make_async_copy(src.at[me], dst.at[c, me], l_sem.at[a])
        copy.start()
        here.append(copy)
        remote(src.at[me], dst.at[c, me], f_send.at[a], f_recv.at[a], sibling).start()
    for a, (src, dst) in enumerate(pairs):

        def forward(k, carry):
            s = (me + 16 - k) % 16
            t = (me + k) % 16
            arrived = remote(
                src.at[t], dst.at[c, s], send.at[a, k], recv.at[a, k], dev(y, t // 4, t % 4, c)
            )
            arrived.wait_recv()
            remote(dst.at[c, s], dst.at[c, s], f_send.at[a], f_recv.at[a], sibling).start()
            arrived.wait_send()
            return carry

        lax.fori_loop(1, 16, forward, 0)
    for a, (src, dst) in enumerate(pairs):
        here[a].wait()
        drain = remote(dst.at[c], dst.at[1 - c], f_send.at[a], f_recv.at[a], sibling)
        drain.wait_send()
        drain.wait_recv()


def dispatch(xs, gs):
    shape = jax.ShapeDtypeStruct((2, 16, SLOTS, MODEL_WIDTH), BF)
    return pl.pallas_call(
        dispatch_kernel,
        out_shape=[shape, shape],
        in_specs=[ANY] * 2,
        out_specs=[ANY] * 2,
        scratch_shapes=[
            pltpu.SemaphoreType.DMA((2,)),
            pltpu.SemaphoreType.DMA((2, 16)),
            pltpu.SemaphoreType.DMA((2, 16)),
            pltpu.SemaphoreType.DMA((2,)),
            pltpu.SemaphoreType.DMA((2,)),
        ],
        compiler_params=params(6),
        name="dispatch",
    )(xs, gs)


def give_back_kernel(
    po, pg, o_ret, g_ret, own_o, own_g, sib_o, sib_g, l_sem, h_sem, s_send, s_recv, send, recv
):
    y, z, x, c = coords()
    me = z * 4 + x
    sibling = dev(y, z, x, 1 - c)
    plane_greet(y, me, c, sibling)
    arrays = ((po, own_o, sib_o, o_ret), (pg, own_g, sib_g, g_ret))
    loads = []
    for a, (part, own, sib, ret) in enumerate(arrays):
        load = pltpu.make_async_copy(part.at[c], own, l_sem.at[a])
        load.start()
        loads.append(load)

    def swap(k, carry):
        t = (me + k) % 16
        for a, (part, own, sib, ret) in enumerate(arrays):
            remote(part.at[1 - c, t], sib.at[t], s_send.at[a], s_recv.at[a, k % 16], sibling).start()
        return carry

    lax.fori_loop(1, 17, swap, 0)
    for load in loads:
        load.wait()

    def add(k, carry):
        t = (me + k) % 16
        for a, (part, own, sib, ret) in enumerate(arrays):
            remote(
                part.at[1 - c, t], sib.at[t], s_send.at[a], s_recv.at[a, k % 16], sibling
            ).wait_recv()
            own[t] = (own[t].astype(F32) + sib[t].astype(F32)).astype(BF)
        return carry

    def push(k, carry):
        add(k, carry)
        t = (me + k) % 16
        for a, (part, own, sib, ret) in enumerate(arrays):
            remote(own.at[t], ret.at[me], send.at[a], recv.at[a], dev(y, t // 4, t % 4, c)).start()
        return carry

    lax.fori_loop(1, 16, push, 0)
    add(16, 0)
    here = []
    for a, (part, own, sib, ret) in enumerate(arrays):
        copy = pltpu.make_async_copy(own.at[me], ret.at[me], h_sem.at[a])
        copy.start()
        here.append(copy)
    for a, (part, own, sib, ret) in enumerate(arrays):
        here[a].wait()
        remote(part.at[1 - c], sib, s_send.at[a], s_recv.at[a, 0], sibling).wait_send()
        drain = remote(
            own.at[pl.ds(0, 15)], ret.at[pl.ds(0, 15)], send.at[a], recv.at[a], sibling
        )
        drain.wait_send()
        drain.wait_recv()


def give_back(po, pg):
    shape = jax.ShapeDtypeStruct((16, SLOTS, MODEL_WIDTH), BF)
    buffer = pltpu.VMEM((16, SLOTS, MODEL_WIDTH), BF)
    return pl.pallas_call(
        give_back_kernel,
        out_shape=[shape, shape],
        in_specs=[ANY] * 2,
        out_specs=[ANY] * 2,
        scratch_shapes=[buffer] * 4
        + [
            pltpu.SemaphoreType.DMA((2,)),
            pltpu.SemaphoreType.DMA((2,)),
            pltpu.SemaphoreType.DMA((2,)),
            pltpu.SemaphoreType.DMA((2, 16)),
            pltpu.SemaphoreType.DMA((2,)),
            pltpu.SemaphoreType.DMA((2,)),
        ],
        compiler_params=params(7, 32 << 20),
        name="give_back",
    )(po, pg)


def reduce_kernel(
    g0, g1, g2, g3, partial, out, sib_partial,
    a0, a1, a2, a3, b0, b1, b2, b3, c0, c1, c2, c3, s0, s1, s2, s3, t0, t1, t2, t3,
    total, give, send, recv, sib_send, sib_recv,
):
    y, z, x, c = coords()
    place = {"y": y, "z": z, "x": x}
    sibling = dev(y, z, x, 1 - c)
    for axis in ("x", "y", "z"):
        for step in STEPS:
            signal(axis_peer(axis, step))
    signal(sibling)
    pl.semaphore_wait(pltpu.get_barrier_semaphore(), 10)
    other = remote(partial, sib_partial, sib_send.at[0], sib_recv.at[0], sibling)
    other.start()
    held = ((g0, g1, g2, g3), (s0, s1, s2, s3), (t0, t1, t2, t3))
    arrive = ((a0, a1, a2, a3), (b0, b1, b2, b3), (c0, c1, c2, c3))

    def at(phase, part, index):
        order = ORDERS[part][::-1]
        spot = [
            index if axis == order[phase] else slice(None)
            for axis in ("y", "z", "x")
            if axis not in order[:phase]
        ]
        return held[phase][part].at[tuple(spot)]

    for phase in range(3):
        copies = []
        for part in range(PARTS):
            axis = ORDERS[part][::-1][phase]
            for n, step in enumerate(STEPS):
                copy = remote(
                    at(phase, part, (place[axis] + step) % 4),
                    arrive[phase][part].at[n],
                    send.at[phase, part, n],
                    recv.at[phase, part, n],
                    axis_peer(axis, step),
                )
                copy.start()
                copies.append(copy)
        for copy in copies:
            copy.wait()
        for part in range(PARTS):
            axis = ORDERS[part][::-1][phase]
            mine = at(phase, part, place[axis])
            got = arrive[phase][part]
            if phase == 0:

                def add(i, carry):
                    p, q = i // 4, i % 4
                    value = mine[p, q].astype(F32)
                    for n in range(3):
                        value = value + got[n, p, q].astype(F32)
                    held[1][part][p, q] = value.astype(BF)
                    return carry

                lax.fori_loop(0, 16, add, 0)
            elif phase == 1:

                def add(p, carry):
                    value = mine[p].astype(F32)
                    for n in range(3):
                        value = value + got[n, p].astype(F32)
                    held[2][part][p] = value.astype(BF)
                    return carry

                lax.fori_loop(0, 4, add, 0)
            else:
                value = mine[...].astype(F32)
                for n in range(3):
                    value = value + got[n].astype(F32)
                total[:, pl.ds(STARTS[part], WIDTHS[part])] = value
    low, high = total[0:12], total[12:24]
    out[c, 0:12] = jnp.where(c == 0, low, high)
    out[c, 12:16] = jnp.zeros((4, PACK), F32)
    give[0:12] = jnp.where(c == 0, high, low)
    give[12:16] = jnp.zeros((4, PACK), F32)
    last = remote(give, out.at[c], sib_send.at[1], sib_recv.at[1], sibling)
    last.start()
    last.wait()
    other.wait()


def place_blocks(full):
    return full.reshape(4, 4, 4, 24, full.shape[-1])


def reduce_weights(grads, partial):
    scratch = (
        [pltpu.VMEM((3, 4, 4, 24, w), BF) for w in WIDTHS]
        + [pltpu.VMEM((3, 4, 24, w), BF) for w in WIDTHS]
        + [pltpu.VMEM((3, 24, w), BF) for w in WIDTHS]
        + [pltpu.VMEM((4, 4, 24, w), BF) for w in WIDTHS]
        + [pltpu.VMEM((4, 24, w), BF) for w in WIDTHS]
        + [pltpu.VMEM((24, PACK), F32), pltpu.VMEM((16, PACK), F32)]
    )
    return pl.pallas_call(
        reduce_kernel,
        out_shape=[
            jax.ShapeDtypeStruct((2, 16, PACK), F32),
            jax.ShapeDtypeStruct((ROWS, MODEL_WIDTH), F32),
        ],
        in_specs=[IN_VMEM] * PARTS + [ANY],
        out_specs=[IN_VMEM, ANY],
        scratch_shapes=scratch
        + [
            pltpu.SemaphoreType.DMA((3, PARTS, 3)),
            pltpu.SemaphoreType.DMA((3, PARTS, 3)),
            pltpu.SemaphoreType.DMA((2,)),
            pltpu.SemaphoreType.DMA((2,)),
        ],
        compiler_params=params(8, 48 << 20),
        name="reduce_weights",
    )(*[place_blocks(grad) for grad in grads], partial)


def dot(a, b, dims):
    return lax.dot_general(a, b, (dims, ((), ())), preferred_element_type=F32)


def wide(block, head, first):
    part = block[:, 64 * head : 64 * head + 64]
    zero = jnp.zeros_like(part)
    return jnp.concatenate([part, zero] if first else [zero, part], axis=1)


def allowed_keys(kb, first_ref, zq, hi):
    q_pos = hi * 256 + lax.broadcasted_iota(jnp.int32, (256, 256), 1)
    k_pos = kb * 256 + lax.broadcasted_iota(jnp.int32, (256, 256), 0)
    return (k_pos >= first_ref[zq]) & (k_pos <= q_pos)


def attn_forward_kernel(span, q_ref, kv_ref, first_ref, o_ref, ot_ref, lse_ref, qs, top, tot, acc):
    zq = pl.program_id(0)
    lo, hi = span[0, zq], span[1, zq]
    q = q_ref[0] * SCALE_QK
    for h in range(3):
        qs[h] = wide(q, h, True)
    top[...] = jnp.full_like(top, NEGATIVE)
    tot[...] = jnp.zeros_like(tot)
    acc[...] = jnp.zeros_like(acc)

    def step(kb, carry):
        kv = kv_ref[kb]
        ok = allowed_keys(kb, first_ref, zq, hi)
        for h in range(3):
            scores = jnp.where(ok, dot(kv, qs[h], ((1,), (1,))), NEGATIVE)
            old = top[h]
            new = jnp.maximum(old, jnp.max(scores, axis=0, keepdims=True))
            shrink = jnp.exp(old - new)
            probs = jnp.exp(scores - new)
            top[h] = new
            tot[h] = tot[h] * shrink + jnp.sum(probs, axis=0, keepdims=True)
            acc[h] = acc[h] * shrink + dot(kv, probs.astype(BF), ((0,), (0,)))
        return carry

    lax.fori_loop(lo, hi + 1, step, 0)
    heads = []
    for h in range(3):
        mixed = acc[h][64:] / tot[h]
        ot_ref[0, h] = mixed
        lse_ref[0, h] = top[h] + jnp.log(tot[h])
        heads.append(mixed)
    o_ref[0] = jnp.transpose(jnp.concatenate(heads, axis=0)).astype(BF)


def attn_forward(span, q, kv, first):
    return pl.pallas_call(
        attn_forward_kernel,
        out_shape=[
            jax.ShapeDtypeStruct((4, PAIR, HEAD_Q), BF),
            jax.ShapeDtypeStruct((4, 3, HD, PAIR), F32),
            jax.ShapeDtypeStruct((4, 3, 1, PAIR), F32),
        ],
        grid_spec=pltpu.PrefetchScalarGridSpec(
            num_scalar_prefetch=1,
            grid=(4,),
            in_specs=[
                pl.BlockSpec((1, PAIR, HEAD_Q), lambda i, s: (i, 0, 0)),
                pl.BlockSpec((16, PAIR, 128), lambda i, s: (0, 0, 0)),
                pl.BlockSpec((4, 1, PAIR), lambda i, s: (0, 0, 0)),
            ],
            out_specs=[
                pl.BlockSpec((1, PAIR, HEAD_Q), lambda i, s: (i, 0, 0)),
                pl.BlockSpec((1, 3, HD, PAIR), lambda i, s: (i, 0, 0, 0)),
                pl.BlockSpec((1, 3, 1, PAIR), lambda i, s: (i, 0, 0, 0)),
            ],
            scratch_shapes=[
                pltpu.VMEM((3, PAIR, 128), BF),
                pltpu.VMEM((3, 1, PAIR), F32),
                pltpu.VMEM((3, 1, PAIR), F32),
                pltpu.VMEM((3, 128, PAIR), F32),
            ],
        ),
        compiler_params=pltpu.CompilerParams(vmem_limit_bytes=32 << 20),
        name="attn_forward",
    )(span, q, kv, first)


def attn_backward_kernel(
    span, q_ref, kv_ref, first_ref, go_ref, ot_ref, lse_ref, dq_ref, dkv_ref, qs, gs, delta, dq, dkv
):
    zq = pl.program_id(0)
    lo, hi = span[0, zq], span[1, zq]
    q = q_ref[0] * SCALE_QK
    grad = go_ref[0]
    grad_t = jnp.transpose(grad.astype(F32))
    for h in range(3):
        qs[h] = wide(q, h, True)
        gs[h] = wide(grad, h, False)
        delta[h] = jnp.sum(grad_t[64 * h : 64 * h + 64] * ot_ref[0, h], axis=0, keepdims=True)
    dq[...] = jnp.zeros_like(dq)

    @pl.when(zq == 0)
    def _():
        dkv[...] = jnp.zeros_like(dkv)

    def step(kb, carry):
        kv = kv_ref[kb]
        ok = allowed_keys(kb, first_ref, zq, hi)
        total = dkv[kb]
        for h in range(3):
            probs = jnp.where(ok, jnp.exp(dot(kv, qs[h], ((1,), (1,))) - lse_ref[0, h]), 0.0)
            grad_probs = dot(kv, gs[h], ((1,), (1,)))
            grad_scores = (probs * (grad_probs - delta[h])).astype(BF)
            dq[h] = dq[h] + dot(kv, grad_scores, ((0,), (0,)))
            total = total + dot(grad_scores, qs[h], ((1,), (0,)))
            total = total + dot(probs.astype(BF), gs[h], ((1,), (0,)))
        dkv[kb] = total
        return carry

    lax.fori_loop(lo, hi + 1, step, 0)
    heads = jnp.concatenate([dq[h][:64] for h in range(3)], axis=0) * SCALE_QK
    dq_ref[0] = jnp.transpose(heads).astype(BF)

    @pl.when(zq == 3)
    def _():
        dkv_ref[...] = dkv[...].astype(BF)


def attn_backward(span, q, kv, first, grad, ot, lse):
    return pl.pallas_call(
        attn_backward_kernel,
        out_shape=[
            jax.ShapeDtypeStruct((4, PAIR, HEAD_Q), BF),
            jax.ShapeDtypeStruct((16, PAIR, 128), BF),
        ],
        grid_spec=pltpu.PrefetchScalarGridSpec(
            num_scalar_prefetch=1,
            grid=(4,),
            in_specs=[
                pl.BlockSpec((1, PAIR, HEAD_Q), lambda i, s: (i, 0, 0)),
                pl.BlockSpec((16, PAIR, 128), lambda i, s: (0, 0, 0)),
                pl.BlockSpec((4, 1, PAIR), lambda i, s: (0, 0, 0)),
                pl.BlockSpec((1, PAIR, HEAD_Q), lambda i, s: (i, 0, 0)),
                pl.BlockSpec((1, 3, HD, PAIR), lambda i, s: (i, 0, 0, 0)),
                pl.BlockSpec((1, 3, 1, PAIR), lambda i, s: (i, 0, 0, 0)),
            ],
            out_specs=[
                pl.BlockSpec((1, PAIR, HEAD_Q), lambda i, s: (i, 0, 0)),
                pl.BlockSpec((16, PAIR, 128), lambda i, s: (0, 0, 0)),
            ],
            scratch_shapes=[
                pltpu.VMEM((3, PAIR, 128), BF),
                pltpu.VMEM((3, PAIR, 128), BF),
                pltpu.VMEM((3, 1, PAIR), F32),
                pltpu.VMEM((3, 128, PAIR), F32),
                pltpu.VMEM((16, PAIR, 128), F32),
            ],
        ),
        compiler_params=pltpu.CompilerParams(vmem_limit_bytes=32 << 20),
        name="attn_backward",
    )(span, q, kv, first, grad, ot, lse)


def inverse_rms(values):
    return lax.rsqrt(jnp.mean(values * values, axis=-1, keepdims=True) + EPS)


def norm_backward(values, inverse, gain, grad_out):
    scaled = grad_out * gain
    return inverse * scaled - values * inverse**3 * jnp.mean(values * scaled, axis=-1, keepdims=True)


def column_sums(left, right):
    return lax.dot_general(left, right, (((0,), (0,)), ((), ())), precision=HIGH_PRECISION)


def only_column(rows, column):
    return jnp.broadcast_to((jnp.arange(EXTRA) == column).astype(F32), (rows, EXTRA))


def halves(matrix):
    return matrix.reshape(12, 2, Q_HALF).transpose(1, 0, 2)


def local(
    tokens,
    segment_ids,
    expert_ids,
    w_query,
    w_key,
    w_value,
    w_out,
    w_router,
    gain_attn,
    gain_moe,
    w_gate,
    w_up,
    w_down,
    cotangent,
):
    y, z, x, c = coords()
    key_value = jnp.concatenate(
        [w_key.reshape(12, 2, 4, HD), w_value.reshape(12, 2, 4, HD)], axis=3
    ).reshape(12, 2, KV_HALF)
    extra = jnp.concatenate(
        [w_router, gain_attn[:, None], gain_moe[:, None], jnp.zeros((12, EXTRA - 18), BF)], axis=1
    )
    pack = jnp.concatenate(
        [
            halves(w_query),
            key_value.transpose(1, 0, 2),
            halves(w_out.T),
            jnp.broadcast_to(extra[None], (2, 12, EXTRA)),
        ],
        axis=2,
    )
    pack = jnp.pad(pack, ((0, 0), (0, 4), (0, 0)))
    part_q, part_kv, part_out, part_extra, pair, seg_all = gather_weights(
        pack, tokens, segment_ids
    )
    pair, w_gate, w_up, w_down = lax.optimization_barrier((pair, w_gate, w_up, w_down))
    gate_w = lax.all_gather(w_gate, "dp", axis=0, tiled=True)
    up_w = lax.all_gather(w_up, "dp", axis=0, tiled=True)
    down_w = lax.all_gather(w_down, "dp", axis=1, tiled=True)
    full_q = part_q.reshape(MODEL_WIDTH, Q_HALF)
    full_kv = part_kv.reshape(MODEL_WIDTH, KV_HALF)
    half_out = part_out.reshape(MODEL_WIDTH, Q_HALF)
    full_extra = part_extra.reshape(MODEL_WIDTH, EXTRA)
    picks = (jnp.arange(EXTRA)[None, :] == jnp.arange(8)[:, None] + EXPERT_COUNT).astype(BF)
    gains = dot(picks, full_extra, ((1,), (1,)))
    gain_a, gain_m = gains[0:1], gains[1:2]
    router = full_extra[:, :EXPERT_COUNT]

    inputs2 = pair.reshape(PAIR, MODEL_WIDTH).astype(F32)
    inverse_a = inverse_rms(inputs2)
    normed = (inputs2 * inverse_a * gain_a).astype(BF)
    queries = dot(normed, full_q, ((1,), (0,))).astype(BF)
    keys_values = dot(normed, full_kv, ((1,), (0,))).astype(BF)
    q4 = queries.reshape(PAIR, 4, HEAD_Q).transpose(1, 0, 2)
    kv4 = keys_values.reshape(PAIR, 4, 128).transpose(1, 0, 2)
    q_in, kv_in, sib_out = heads_out(q4, kv4, half_out)

    segs = seg_all.reshape(1, 4096)
    counts = jnp.sum((segs < jnp.arange(16)[:, None]).astype(jnp.int32), axis=1)
    row_segs = lax.dynamic_index_in_dim(seg_all.reshape(4, 4, PAIR), x, 1, keepdims=False)
    first = jnp.sum(
        jnp.where(row_segs[:, :, None] == jnp.arange(16), counts, 0), axis=2
    )
    span = jnp.stack([first[:, 0] // PAIR, jnp.arange(4, dtype=jnp.int32) * 4 + x])
    first = first.reshape(4, 1, PAIR)
    attn_low, attn_t, lse = attn_forward(span, q_in, kv_in, first)
    attn = attn_return(attn_low.reshape(8, ROWS, HEAD_Q))
    attn = attn.reshape(4, 2, ROWS, HEAD_Q).transpose(1, 2, 0, 3).reshape(2, ROWS, Q_HALF)

    own_attn = jnp.where(c == 0, attn[0], attn[1])
    other_attn = jnp.where(c == 0, attn[1], attn[0])
    inputs = tokens.astype(F32)
    middle = (
        inputs
        + dot(own_attn, half_out, ((1,), (1,)))
        + dot(other_attn, sib_out, ((1,), (1,)))
    )
    inverse_m = inverse_rms(middle)
    moe_in = (middle * inverse_m * gain_m).astype(BF)
    logits = dot(moe_in, router, ((1,), (0,)))
    chosen = (expert_ids[:, :, None] == jnp.arange(EXPERT_COUNT, dtype=jnp.int32)).astype(F32)
    picked = jnp.sum(chosen * logits[:, None, :], axis=-1)
    gates = jax.nn.softmax(picked, axis=-1)
    used = jnp.sum(chosen, axis=1)
    earlier = (jnp.arange(ROWS)[:, None] > jnp.arange(ROWS)[None, :]).astype(BF)
    before = dot(earlier, used.astype(BF), ((1,), (0,)))
    place = jnp.sum(chosen * before[:, None, :], axis=-1)
    slot = jnp.where(
        place < EXPERT_CAPACITY, expert_ids * SLOTS + place.astype(jnp.int32), -1
    )
    hit = (slot.T[:, :, None] == jnp.arange(EXPERT_COUNT * SLOTS, dtype=jnp.int32)).astype(F32)
    both = (hit[0] + hit[1]).astype(BF)
    slot_gate = jnp.sum(hit * gates.T[:, :, None], axis=(0, 1))
    slots_in = dot(both, moe_in, ((0,), (0,))).astype(BF)
    grad_slots = (dot(both, cotangent, ((0,), (0,))) * slot_gate[:, None]).astype(BF)
    blocks = (EXPERT_COUNT, SLOTS, MODEL_WIDTH)
    x_in, g_in = dispatch(slots_in.reshape(blocks), grad_slots.reshape(blocks))

    expert_in = x_in.reshape(-1, MODEL_WIDTH)
    grad_expert = g_in.reshape(-1, MODEL_WIDTH)
    gate_val = dot(expert_in, gate_w, ((1,), (0,)))
    up_val = dot(expert_in, up_w, ((1,), (0,)))
    sig = jax.nn.sigmoid(gate_val)
    hidden = (gate_val * sig * up_val).astype(BF)
    part_out = dot(hidden, down_w, ((1,), (0,))).astype(BF)
    grad_hidden = dot(grad_expert, down_w, ((1,), (1,)))
    grad_gate = (grad_hidden * up_val * sig * (1.0 + gate_val * (1.0 - sig))).astype(BF)
    grad_up = (grad_hidden * gate_val * sig).astype(BF)
    part_grad = dot(grad_gate, gate_w, ((1,), (1,))) + dot(grad_up, up_w, ((1,), (1,)))
    shape = (2, 16, SLOTS, MODEL_WIDTH)
    out_ret, grad_ret = give_back(part_out.reshape(shape), part_grad.astype(BF).reshape(shape))
    grad_w_gate = dot(expert_in, grad_gate, ((0,), (0,))).astype(BF)
    grad_w_up = dot(expert_in, grad_up, ((0,), (0,))).astype(BF)
    grad_w_down = dot(hidden, grad_expert, ((0,), (0,))).astype(BF)
    expert_grads = (
        lax.psum_scatter(grad_w_gate, "dp", scatter_dimension=0, tiled=True).astype(F32),
        lax.psum_scatter(grad_w_up, "dp", scatter_dimension=0, tiled=True).astype(F32),
        lax.psum_scatter(grad_w_down, "dp", scatter_dimension=1, tiled=True).astype(F32),
    )

    grad_output = cotangent.astype(F32)
    out_ret = out_ret.reshape(EXPERT_COUNT * SLOTS, MODEL_WIDTH)
    grad_ret = grad_ret.reshape(EXPERT_COUNT * SLOTS, MODEL_WIDTH)
    rows_out = [dot(hit[k].astype(BF), out_ret, ((1,), (0,))) for k in range(2)]
    block_out = (middle + gates[:, 0:1] * rows_out[0] + gates[:, 1:2] * rows_out[1]).astype(BF)
    grad_pair = jnp.stack([jnp.sum(grad_output * rows, axis=-1) for rows in rows_out], axis=-1)
    grad_pick = gates * (grad_pair - jnp.sum(gates * grad_pair, axis=-1, keepdims=True))
    grad_logits = jnp.sum(chosen * grad_pick[:, :, None], axis=1)
    grad_moe_in = dot(both, grad_ret, ((1,), (0,))) + lax.dot_general(
        grad_logits, router.astype(F32), (((1,), (1,)), ((), ())), precision=HIGH_PRECISION
    )
    g_router = column_sums(moe_in.astype(F32), jnp.pad(grad_logits, ((0, 0), (0, EXTRA - EXPERT_COUNT))))
    g_gain_m = column_sums(grad_moe_in * middle * inverse_m, only_column(ROWS, EXPERT_COUNT + 1))
    grad_middle = grad_output + norm_backward(middle, inverse_m, gain_m, grad_moe_in)
    branch = grad_middle.astype(BF)
    own_heads = dot(branch, half_out, ((1,), (0,))).astype(BF)
    other_heads = dot(branch, sib_out, ((1,), (0,))).astype(BF)
    grad_heads = jnp.stack(
        [jnp.where(c == 0, own_heads, other_heads), jnp.where(c == 0, other_heads, own_heads)]
    )
    grad_heads = grad_heads.reshape(2, ROWS, 4, HEAD_Q).transpose(2, 0, 1, 3)
    go_in, branch_sib, attn_sib = grad_attn_out(
        grad_heads.reshape(8, ROWS, HEAD_Q), branch, other_attn
    )
    dq_low, dkv_low = attn_backward(
        span, q_in, kv_in, first, go_in.reshape(4, PAIR, HEAD_Q), attn_t, lse
    )
    dq_in, dkv_in = heads_back(dq_low, dkv_low)
    grad_q = dq_in.transpose(1, 0, 2).reshape(PAIR, Q_HALF)
    grad_kv = jnp.sum(dkv_in.reshape(4, 4, PAIR, 128).astype(F32), axis=1).astype(BF)
    grad_kv = grad_kv.transpose(1, 0, 2).reshape(PAIR, KV_HALF)

    part_normed = dot(grad_q, full_q, ((1,), (1,))) + dot(
        grad_kv, full_kv, ((1,), (1,))
    )
    g_gain_a = column_sums(part_normed * inputs2 * inverse_a, only_column(PAIR, EXPERT_COUNT))
    g_query = dot(normed, grad_q, ((0,), (0,))).astype(BF)
    g_kv = dot(normed, grad_kv, ((0,), (0,))).astype(BF)
    g_extra = (g_router + g_gain_m + g_gain_a).astype(BF)
    g_out = (dot(branch, own_attn, ((0,), (0,))) + dot(branch_sib, attn_sib, ((0,), (0,)))).astype(BF)
    by_core = part_normed.reshape(2, ROWS, MODEL_WIDTH)
    own_part = lax.dynamic_index_in_dim(by_core, c, 0, keepdims=False)
    other_part = lax.dynamic_index_in_dim(by_core, 1 - c, 0, keepdims=False)
    reduced, sib_part = reduce_weights((g_query, g_kv, g_out, g_extra), other_part)
    grad_normed = own_part + sib_part
    grad_tokens = grad_middle + norm_backward(
        inputs, inverse_rms(inputs), gain_a, grad_normed
    )
    reduced = reduced[:, :12]
    r_query = reduced[:, :, :Q_HALF].transpose(1, 0, 2).reshape(12, HEADS * HD)
    r_kv = reduced[:, :, Q_HALF : Q_HALF + KV_HALF].transpose(1, 0, 2).reshape(12, KV, 2, HD)
    r_out = reduced[:, :, STARTS[2] : STARTS[3]].transpose(1, 0, 2).reshape(12, HEADS * HD)
    r_extra = jnp.sum(reduced[:, :, STARTS[3] :], axis=0)
    return (
        block_out,
        grad_tokens,
        r_query,
        r_kv[:, :, 0].reshape(12, KV * HD),
        r_kv[:, :, 1].reshape(12, KV * HD),
        r_out.T,
        r_extra[:, :EXPERT_COUNT],
        r_extra[:, EXPERT_COUNT],
        r_extra[:, EXPERT_COUNT + 1],
        expert_grads[0],
        expert_grads[1],
        expert_grads[2],
    )


def solution(mesh):
    rows, flat, dense = P(("dp", "ctx"), None), P(("dp", "ctx")), P("dp", "ctx")
    placed = (
        rows, dense, rows, rows, rows, rows, P(None, ("dp", "ctx")), rows, flat, flat,
        dense, dense, P("ctx", "dp"), rows,
    )
    return jax.shard_map(
        local,
        mesh=mesh,
        in_specs=placed,
        out_specs=(
            rows, rows, rows, rows, rows, P(None, ("dp", "ctx")), rows, flat, flat,
            dense, dense, P("ctx", "dp"),
        ),
        check_vma=False,
    )
```

time: 2220 us -> 447 us (0.20)
  blocking collectives: 668 us -> 0 us
  starting transfers between devices: 623 us -> 0.42 us
  waiting for transfers between devices: 448 us -> 1.47 us
  Pallas kernels: 0 us -> 314 us
  local copies, waits for them, and re-layouts: 259 us -> 36.1 us
  loops' own time: 80 us -> 0 us
  matrix products: 86.3 us -> 59.2 us
    unnamed x163 -> x1, starting transfers between devices: 558 us -> 0.04 us
    unnamed x3 -> x0, blocking collectives: 549 us -> none
    pallas_call x0 -> x10, Pallas kernels: none -> 314 us  [the longest x1 55.1 us: reduce_weights(): pl.pallas_call(reduce_kernel, out_shape=[jax.ShapeDtypeStruct((2, 16, PAC...]
    all_gather x9 -> x3, waiting for transfers between devices: 193 us -> 0.02 us  [the longest x1 0.02 us: local(): gate_w = lax.all_gather(w_gate, 'dp', axis=0, tiled=True)]
    reduce_scatter x2, waiting for transfers between devices: 183 us -> 0.01 us  [the longest x1 0.01 us: local(): lax.psum_scatter(grad_w_up, 'dp', scatter_dimension=0, tiled=True)]
    unnamed x366 -> x117, local copies, waits for them, and re-layouts: 186 us -> 17.7 us
    all_gather x2 -> x0, blocking collectives: 83.4 us -> none  [the longest x1 57.5 us: local(): lax.all_gather(w_router, ('dp', 'ctx'), axis=0, tiled=True)]
    another operation x27 -> x0, loops' own time: 80 us -> none  [the longest x1 26.6 us: local(): lax.scan(grad_step, jnp.zeros((rows_loc, KV, per_group, HD), jnp.float32)...]
  transfers between devices with their start and end apart: 177 -> 6, of which waited for: 25 -> 0; matrix products, arithmetic and copies ran while one was open for 30% -> 18% of each run, Pallas kernels for 0% -> 59%
where the time goes in v1:
time: 447 us; the launch traced here: 444 us
  Pallas kernels  314 us (70%)
  matrix products  59.2 us (13%)
  local copies, waits for them, and re-layouts  36.1 us (8%)
  other arithmetic  17.5 us (4%)
  between operations  15.1 us (3%)
    pallas_call x1, Pallas kernels, reduce_weights(): pl.pallas_call(reduce_kernel, out_shape=[jax.ShapeDtypeStruct((2, 16, PAC...  55.1 us
    pallas_call x1, Pallas kernels, gather_weights(): pl.pallas_call(gather_kernel, out_shape=[jax.ShapeDtypeStruct((4, 4, 4, 2...  51.6 us
    dot_general x29, matrix products, dot(): return lax.dot_general(a, b, (dims, ((), ())), preferred_element_type=F32)  51.5 us
    pallas_call x1, Pallas kernels, give_back(): pl.pallas_call(give_back_kernel, out_shape=[shape, shape], in_specs=[ANY]...  45 us
    pallas_call x1, Pallas kernels, dispatch(): pl.pallas_call(dispatch_kernel, out_shape=[shape, shape], in_specs=[ANY]...  41.5 us
    pallas_call x1, Pallas kernels, attn_backward(): pl.pallas_call(attn_backward_kernel, out_shape=[jax.ShapeDtypeStruct((4,...  28.7 us
    pallas_call x1, Pallas kernels, attn_forward(): pl.pallas_call(attn_forward_kernel, out_shape=[jax.ShapeDtypeStruct((4, P...  26.7 us
    pallas_call x1, Pallas kernels, heads_back(): pl.pallas_call(heads_back_kernel, out_shape=[jax.ShapeDtypeStruct((4, PAI...  22.3 us
  transfers between devices with their start and end apart: 6, of which 0 were waited for; matrix products, arithmetic and copies ran while one was open for 18% of the time, Pallas kernels for 59%

profile of v1, /device:TPU:1, one launch (start us, length us, event | category | flops | bytes accessed | tf_op | source)
XLA Modules:
  0.0 444.1 jit_solution(1197643787511709679)
XLA Ops:
  13.7 51.6 %gather_weights.1 = (bf16[4,4,4,24,768]{4,3,2,1,0:T(8,128)(2,1)}, bf16[4,4,4,24,512]{4,3,2,1,0:T(8,128)(2,1)}, bf16[4,4,4,24,768]{4,3,2,1,0:T(8,128)(2,1)}, bf16...) custom-call(bf16[2,16,2176]{2,1,0:T(8,128)(2,1)} %fusion.24.pack, ...), custom_call_target="tpu_custom_call" | custom-call | tf_op jit(solution)/shard_map/gather_weights/pallas_call | solution.py:161
  71.6 2.3 convolution_convert_fusion.8
  74.9 2.4 convolution_convert_fusion.7
  78.5 21.6 %heads_out.1 = (bf16[4,256,192]{2,1,0:T(8,128)(2,1)}, bf16[16,256,128]{2,1,0:T(8,128)(2,1)}, bf16[1536,768]{1,0:T(8,128)(2,1)}) custom-call(bf16[4,256,192]{2,1,0:T(8,128)(2,1)} %bitcast.207, bf16[4,256,128]{2,1,0:T(8,128)(2,1)} %bitcast.216, bf16[1536,768]{1,0:T(8,128)(2,1)} %bitcast.180), custom_call_target="tpu_custom_call" | custom-call | tf_op jit(solution)/shard_map/heads_out/pallas_call | solution.py:237
  102.4 26.7 %attn_forward.1 = (bf16[4,256,192]{2,1,0:T(8,128)(2,1)S(1)}, f32[4,3,64,256]{3,2,1,0:T(8,128)S(1)}, f32[4,3,1,256]{3,2,1,0:T(1,128)S(1)}) custom-call(s32[2,4]{1,0:T(2,128)S(1)} %pad_add_fusion.span, bf16[4,256,192]{2,1,0:T(8,128)(2,1)S(1)} %copy-done.2, bf16[16,256,128]{2,1,0:T(8,128)(2,1)S(1)} %copy-done, s32[4,1,256]{2,1,0:T(1,128)S(1)} %reshape.426.first_ref), custom_call_target="tpu_custom_call" | custom-call | tf_op jit(solution)/shard_map/attn_forward/pallas_call | solution.py:712
  129.9 11.5 %attn_return.1 = bf16[8,128,192]{2,1,0:T(8,128)(2,1)} custom-call(bf16[8,128,192]{2,1,0:T(8,128)(2,1)} %bitcast.178), custom_call_target="tpu_custom_call" | custom-call | tf_op jit(solution)/shard_map/attn_return/pallas_call | solution.py:357
  143.6 2.7 convolution_add_fusion.5
  152.0 41.5 %dispatch.1 = (bf16[2,16,24,1536]{3,2,1,0:T(8,128)(2,1)}, bf16[2,16,24,1536]{3,2,1,0:T(8,128)(2,1)}) custom-call(bf16[16,24,1536]{2,1,0:T(8,128)(2,1)} %bitcast.192, bf16[16,24,1536]{2,1,0:T(8,128)(2,1)} %bitcast.193), custom_call_target="tpu_custom_call" | custom-call | tf_op jit(solution)/shard_map/dispatch/pallas_call | solution.py:448
  194.5 3.5 fusion.47
  198.1 4.6 %fusion.46 = f32[768,512]{1,0:T(8,128)} fusion(bf16[768,1536]{1,0:T(8,128)(2,1)} %bitcast.239, bf16[1536,512]{1,0:T(8,128)(2,1)} %all-gather.4.cloned.1.call-done), kind=kOutput, calls=%fused_computation.148 | convolution fusion | flops 1207959552 | bytes 5505024 | tf_op jit(solution)/shard_map/dot_general | solution.py:662
  202.7 5.9 %multiply_convert_fusion = (bf16[768,512]{1,0:T(8,128)(2,1)}, bf16[768,512]{1,0:T(8,128)(2,1)}, bf16[768,512]{1,0:T(8,128)(2,1)S(1)}) fusion(f32[768,512]{1,0:T(8,128)} %fusion.46, f32[768,512]{1,0:T(8,128)S(1)} %fusion.47, bf16[768,1536]{1,0:T(8,128)(2,1)} %bitcast.199, bf16[512,1536]{1,0:T(8,128)(2,1)} %all-gather.8.cloned.1.call-done), kind=kOutput, calls=%fused_computation.20 | convolution fusion | flops 1214251008 | bytes 9437184 | tf_op jit(solution)/shard_map/dot_general | solution.py:662
  213.7 2.9 convolution_convert_fusion.1
  219.7 45.0 %give_back.1 = (bf16[16,24,1536]{2,1,0:T(8,128)(2,1)S(1)}, bf16[16,24,1536]{2,1,0:T(8,128)(2,1)S(1)}) custom-call(bf16[2,16,24,1536]{3,2,1,0:T(8,128)(2,1)S(1)} %bitcast.175, bf16[2,16,24,1536]{3,2,1,0:T(8,128)(2,1)S(1)} %bitcast.171), custom_call_target="tpu_custom_call" | custom-call | tf_op jit(solution)/shard_map/give_back/pallas_call | solution.py:525
  267.5 2.6 convolution_convert_fusion.3
  278.9 2.0 copy.94
  280.9 10.5 %grad_attn_out.1 = (bf16[8,128,192]{2,1,0:T(8,128)(2,1)}, bf16[128,1536]{1,0:T(8,128)(2,1)}, bf16[128,768]{1,0:T(8,128)(2,1)}) custom-call(bf16[8,128,192]{2,1,0:T(8,128)(2,1)} %bitcast.205, bf16[128,1536]{1,0:T(8,128)(2,1)} %copy-done.11, bf16[128,768]{1,0:T(8,128)(2,1)} %copy.95.attn), custom_call_target="tpu_custom_call" | custom-call | tf_op jit(solution)/shard_map/grad_attn_out/pallas_call | solution.py:386
  292.5 28.7 %attn_backward.1 = (bf16[4,256,192]{2,1,0:T(8,128)(2,1)S(1)}, bf16[16,256,128]{2,1,0:T(8,128)(2,1)S(1)}) custom-call(s32[2,4]{1,0:T(2,128)S(1)} %pad_add_fusion.span, bf16[4,256,192]{2,1,0:T(8,128)(2,1)S(1)} %copy-done.3, bf16[16,256,128]{2,1,0:T(8,128)(2,1)S(1)} %copy-done.1, s32[4,1,256]{2,1,0:T(1,128)S(1)} %reshape.426.first_ref, ...), custom_call_target="tpu_custom_call" | custom-call | tf_op jit(solution)/shard_map/attn_backward/pallas_call | solution.py:786
  322.9 22.3 %heads_back.1 = (bf16[4,256,192]{2,1,0:T(8,128)(2,1)}, bf16[16,256,128]{2,1,0:T(8,128)(2,1)}) custom-call(bf16[4,256,192]{2,1,0:T(8,128)(2,1)} %copy-done.5, bf16[16,256,128]{2,1,0:T(8,128)(2,1)} %copy-done.4), custom_call_target="tpu_custom_call" | custom-call | tf_op jit(solution)/shard_map/heads_back/pallas_call | solution.py:294
  354.4 2.6 convolution_convert_fusion.4
  357.7 3.0 convolution_add_fusion.2
  360.7 2.6 fusion.2
  363.4 2.6 fusion.1
  368.2 2.2 add_convert_fusion
  370.4 55.1 %reduce_weights.1 = (f32[2,16,2176]{2,1,0:T(8,128)S(1)}, f32[128,1536]{1,0:T(8,128)S(1)}) custom-call(bf16[4,4,4,24,768]{4,3,2,1,0:T(8,128)(2,1)S(1)} %bitcast.170, bf16[4,4,4,24,512]{4,3,2,1,0:T(8,128)(2,1)S(1)} %bitcast.172, bf16[4,4,4,24,768]{4,3,2,1,0:T(8,128)(2,1)} %bitcast.186, bf16[4,4,4,24,128]{4,3,2,1,0:T(8,128)(2,1)S(1)} %bitcast.176, ...), custom_call_target="tpu_custom_call" | custom-call | tf_op jit(solution)/shard_map/reduce_weights/pallas_call | solution.py:641
  (238 shorter events, 72.7 us)
Async XLA Ops:
  7.2 62.8 %copy-start.46 = (s32[128,2]{0,1:T(2,128)S(1)}, s32[128,2]{0,1:T(2,128)}, u32[]{:S(2)}) copy-start(s32[128,2]{0,1:T(2,128)} %param.16) | copy-start | bytes 3076
  7.2 187.3 %all-gather.6.cloned.1.call-start = ((), (), s32[]{:S(2)}) async-start(), calls=%async_computation.4 | async-start | bytes 1966080 | tf_op jit(solution)/shard_map/all_gather | solution.py:879
  65.3 4.9 %copy-start.15 = (bf16[2,128,1536]{2,1,0:T(8,128)(2,1)S(1)}, bf16[2,128,1536]{2,1,0:T(8,128)(2,1)}, u32[]{:S(2)}) copy-start(bf16[2,128,1536]{2,1,0:T(8,128)(2,1)} %get-tuple-element.43) | copy-start | bytes 2359300
  65.3 5.7 %copy-start.29 = (bf16[4,4,4,24,128]{4,3,2,1,0:T(8,128)(2,1)S(1)}, bf16[4,4,4,24,128]{4,3,2,1,0:T(8,128)(2,1)}, u32[]{:S(2)}) copy-start(bf16[4,4,4,24,128]{4,3,2,1,0:T(8,128)(2,1)} %get-tuple-element.44) | copy-start | bytes 1179652
  65.3 132.7 %all-gather.4.cloned.1.call-start = ((), (), s32[]{:S(2)}) async-start(), calls=%async_computation.3 | async-start | bytes 1966080 | tf_op jit(solution)/shard_map/all_gather | solution.py:878
  66.1 136.6 %all-gather.8.cloned.1.call-start = ((), (), s32[]{:S(2)}) async-start(), calls=%async_computation.5 | async-start | bytes 1966080 | tf_op jit(solution)/shard_map/all_gather | solution.py:880
  66.8 364.4 %reduce-scatter.10.cloned.1.call-start = ((), (), s32[]{:S(2)}) async-start(), calls=%async_computation.8 | async-start | bytes 1966080
  71.5 3.3 copy-start.17
  129.9 13.7 %copy-start.21 = (bf16[128,1536]{1,0:T(8,128)(2,1)S(1)}, bf16[128,1536]{1,0:T(8,128)(2,1)}, u32[]{:S(2)}) copy-start(bf16[128,1536]{1,0:T(8,128)(2,1)} %tokens.1) | copy-start | bytes 1179652
  142.8 3.6 copy-start.34
  202.7 6.8 %copy-start.32 = (bf16[2,16,24,1536]{3,2,1,0:T(8,128)(2,1)S(1)}, bf16[2,16,24,1536]{3,2,1,0:T(8,128)(2,1)}, u32[]{:S(2)}) copy-start(bf16[2,16,24,1536]{3,2,1,0:T(8,128)(2,1)} %get-tuple-element.56) | copy-start | bytes 7077892
  212.5 220.8 %reduce-scatter.8.cloned.1.call-start = ((), (), s32[]{:S(2)}) async-start(), calls=%async_computation.7 | async-start | bytes 1966080 | tf_op jit(solution)/shard_map/reduce_scatter | solution.py:958
  219.7 45.0 %copy-start.26 = (f32[2,128,384]{2,1,0:T(8,128)S(1)}, f32[2,128,384]{2,1,0:T(8,128)}, u32[]{:S(2)}) copy-start(f32[2,128,384]{2,1,0:T(8,128)} %copy-done.25) | copy-start | bytes 1179652
  267.0 3.1 copy-start.43
  270.1 165.2 %reduce-scatter.6.cloned.1.call-start = ((), (), s32[]{:S(2)}) async-start(), calls=%async_computation.6 | async-start | bytes 1966080 | tf_op jit(solution)/shard_map/reduce_scatter | solution.py:957
  276.3 15.1 %copy-start.1 = (bf16[16,256,128]{2,1,0:T(8,128)(2,1)S(1)}, bf16[16,256,128]{2,1,0:T(8,128)(2,1)}, u32[]{:S(2)}) copy-start(bf16[16,256,128]{2,1,0:T(8,128)(2,1)} %get-tuple-element.49.kv_ref) | copy-start | bytes 3145732
  276.3 15.1 %copy-start.3 = (bf16[4,256,192]{2,1,0:T(8,128)(2,1)S(1)}, bf16[4,256,192]{2,1,0:T(8,128)(2,1)}, u32[]{:S(2)}) copy-start(bf16[4,256,192]{2,1,0:T(8,128)(2,1)} %get-tuple-element.48.q_ref) | copy-start | bytes 1179652
  345.2 3.6 copy-start.24
  345.2 3.6 copy-start.44
  346.5 3.8 copy-start.18
  357.7 3.0 copy-start.20
  357.7 3.0 copy-start.47
  425.5 4.1 copy-start.10
  425.5 4.1 copy-start.22
  (37 other events, 62.9 us)
Sparse Core Ops, SparseCore 0:
  65.5 25.0 all-gather.5
  92.2 26.4 all-gather.3
  120.4 26.5 all-gather.7
  212.7 21.9 reduce-scatter.9
  270.2 21.8 reduce-scatter.7
  357.2 25.9 reduce-scatter.5

commit v2 on v1

--- a/solution.py
+++ b/solution.py
@@ -32,6 +32,10 @@
 IN_VMEM = pl.BlockSpec(memory_space=pltpu.VMEM)
 BF = jnp.bfloat16
 F32 = jnp.float32
+
+
+def dot(a, b, dims):
+    return lax.dot_general(a, b, (dims, ((), ())), preferred_element_type=F32)
 
 
 def coords():
@@ -399,146 +403,214 @@
     )(blocks, branch, attn)
 
 
-def dispatch_kernel(xs, gs, x_in, g_in, l_sem, send, recv, f_send, f_recv):
-    y, z, x, c = coords()
-    me = z * 4 + x
-    sibling = dev(y, z, x, 1 - c)
-    plane_greet(y, me, c, sibling)
-    pairs = ((xs, x_in), (gs, g_in))
-
-    for a, (src, dst) in enumerate(pairs):
-
-        def push(k, carry):
-            t = (me + k) % 16
-            remote(
-                src.at[t], dst.at[c, me], send.at[a, k], recv.at[a, k], dev(y, t // 4, t % 4, c)
-            ).start()
-            return carry
-
-        lax.fori_loop(1, 16, push, 0)
-    here = []
-    for a, (src, dst) in enumerate(pairs):
-        copy = pltpu.make_async_copy(src.at[me], dst.at[c, me], l_sem.at[a])
-        copy.start()
-        here.append(copy)
-        remote(src.at[me], dst.at[c, me], f_send.at[a], f_recv.at[a], sibling).start()
-    for a, (src, dst) in enumerate(pairs):
-
-        def forward(k, carry):
-            s = (me + 16 - k) % 16
-            t = (me + k) % 16
-            arrived = remote(
-                src.at[t], dst.at[c, s], send.at[a, k], recv.at[a, k], dev(y, t // 4, t % 4, c)
-            )
-            arrived.wait_recv()
-            remote(dst.at[c, s], dst.at[c, s], f_send.at[a], f_recv.at[a], sibling).start()
-            arrived.wait_send()
-            return carry
-
-        lax.fori_loop(1, 16, forward, 0)
-    for a, (src, dst) in enumerate(pairs):
-        here[a].wait()
-        drain = remote(dst.at[c], dst.at[1 - c], f_send.at[a], f_recv.at[a], sibling)
-        drain.wait_send()
-        drain.wait_recv()
-
-
-def dispatch(xs, gs):
-    shape = jax.ShapeDtypeStruct((2, 16, SLOTS, MODEL_WIDTH), BF)
-    return pl.pallas_call(
-        dispatch_kernel,
-        out_shape=[shape, shape],
-        in_specs=[ANY] * 2,
-        out_specs=[ANY] * 2,
-        scratch_shapes=[
-            pltpu.SemaphoreType.DMA((2,)),
-            pltpu.SemaphoreType.DMA((2, 16)),
-            pltpu.SemaphoreType.DMA((2, 16)),
-            pltpu.SemaphoreType.DMA((2,)),
-            pltpu.SemaphoreType.DMA((2,)),
-        ],
-        compiler_params=params(6),
-        name="dispatch",
-    )(xs, gs)
-
-
-def give_back_kernel(
-    po, pg, o_ret, g_ret, own_o, own_g, sib_o, sib_g, l_sem, h_sem, s_send, s_recv, send, recv
+def flat_rows(blocks):
+    return blocks.reshape(blocks.shape[0] * SLOTS, blocks.shape[2])
+
+
+def experts_kernel(
+    xs, gs, gate_w, up_w, down_w, out_ret, grad_ret, d_gate, d_up, d_down,
+    x_all, g_all, wg, wu, wd, gate_v, up_v, hidden, g_gate, g_up, part_o, part_g, sib_o, sib_g,
+    v_gate, v_up, v_down,
+    w_sem, l_sem, send, recv, f_send, f_recv, s_send, s_recv, r_send, r_recv, o_sem,
 ):
     y, z, x, c = coords()
     me = z * 4 + x
     sibling = dev(y, z, x, 1 - c)
     plane_greet(y, me, c, sibling)
-    arrays = ((po, own_o, sib_o, o_ret), (pg, own_g, sib_g, g_ret))
-    loads = []
-    for a, (part, own, sib, ret) in enumerate(arrays):
-        load = pltpu.make_async_copy(part.at[c], own, l_sem.at[a])
+    loads = [
+        pltpu.make_async_copy(src, dst, w_sem.at[n])
+        for n, (src, dst) in enumerate(((gate_w, wg), (up_w, wu), (down_w, wd)))
+    ]
+    for load in loads:
         load.start()
-        loads.append(load)
-
-    def swap(k, carry):
-        t = (me + k) % 16
-        for a, (part, own, sib, ret) in enumerate(arrays):
-            remote(part.at[1 - c, t], sib.at[t], s_send.at[a], s_recv.at[a, k % 16], sibling).start()
-        return carry
-
-    lax.fori_loop(1, 17, swap, 0)
+    arrays = ((xs, x_all), (gs, g_all))
+
+    def scatter(a):
+        src, dst = arrays[a]
+
+        def push(k, carry):
+            t = (me + k) % 16
+            remote(
+                src.at[t], dst.at[c * 16 + me], send.at[a, k], recv.at[a, k], dev(y, t // 4, t % 4, c)
+            ).start()
+            return carry
+
+        lax.fori_loop(1, 16, push, 0)
+        pltpu.make_async_copy(src.at[me], dst.at[c * 16 + me], l_sem.at[a]).start()
+        remote(src.at[me], dst.at[c * 16 + me], f_send.at[a], f_recv.at[a], sibling).start()
+
+    def hand_over(a):
+        src, dst = arrays[a]
+
+        def forward(k, carry):
+            s = (me + 16 - k) % 16
+            t = (me + k) % 16
+            arrived = remote(
+                src.at[t], dst.at[c * 16 + s], send.at[a, k], recv.at[a, k], dev(y, t // 4, t % 4, c)
+            )
+            arrived.wait_recv()
+            remote(
+                dst.at[c * 16 + s], dst.at[c * 16 + s], f_send.at[a], f_recv.at[a], sibling
+            ).start()
+            arrived.wait_send()
+            return carry
+
+        lax.fori_loop(1, 16, forward, 0)
+
+    def settle(a):
+        src, dst = arrays[a]
+        pltpu.make_async_copy(src.at[me], dst.at[c * 16 + me], l_sem.at[a]).wait()
+        half = pl.ds(0, 16)
+        drain = remote(dst.at[half], dst.at[half], f_send.at[a], f_recv.at[a], sibling)
+        drain.wait_send()
+        drain.wait_recv()
+
+    def swap(part, sib, a):
+        rows = pl.ds((1 - c) * 16, 16)
+        return remote(part.at[rows], sib, s_send.at[a], s_recv.at[a], sibling)
+
+    def give(part, sib, ret, a):
+        def add(t):
+            rows = c * 16 + t
+            part[rows] = (
+                part[rows].astype(F32) + sib[t].astype(F32)
+            ).astype(BF)
+            return part.at[rows]
+
+        def push(k, carry):
+            t = (me + k) % 16
+            remote(add(t), ret.at[me], r_send.at[a], r_recv.at[a], dev(y, t // 4, t % 4, c)).start()
+            return carry
+
+        lax.fori_loop(1, 16, push, 0)
+        pltpu.make_async_copy(add(me), ret.at[me], l_sem.at[2 + a]).start()
+
+    def given(part, ret, a):
+        pltpu.make_async_copy(part.at[c * 16 + me], ret.at[me], l_sem.at[2 + a]).wait()
+        drain = remote(ret.at[pl.ds(0, 15)], ret.at[pl.ds(0, 15)], r_send.at[a], r_recv.at[a], sibling)
+        drain.wait_send()
+        drain.wait_recv()
+
+    def tile(n):
+        h = 1 - c if n == 0 else c
+        rows = 16 * SLOTS
+        return pl.ds(h * 16, 16), pl.ds(pl.multiple_of(h * rows, rows), rows)
+
+    scatter(0)
+    hand_over(0)
+    scatter(1)
+    settle(0)
     for load in loads:
         load.wait()
-
-    def add(k, carry):
-        t = (me + k) % 16
-        for a, (part, own, sib, ret) in enumerate(arrays):
-            remote(
-                part.at[1 - c, t], sib.at[t], s_send.at[a], s_recv.at[a, k % 16], sibling
-            ).wait_recv()
-            own[t] = (own[t].astype(F32) + sib[t].astype(F32)).astype(BF)
+    for n in range(2):
+        blocks, rows = tile(n)
+        rows_in = flat_rows(x_all[blocks])
+        gate_val = dot(rows_in, wg[...], ((1,), (0,)))
+        up_val = dot(rows_in, wu[...], ((1,), (0,)))
+        gate_v[rows] = gate_val
+        up_v[rows] = up_val
+        low = (gate_val * jax.nn.sigmoid(gate_val) * up_val).astype(BF)
+        hidden[rows] = low
+        part_o[blocks] = dot(low, wd[...], ((1,), (0,))).astype(BF).reshape(16, SLOTS, MODEL_WIDTH)
+        if n == 0:
+            swap(part_o, sib_o, 0).start()
+    hand_over(1)
+    swap(part_o, sib_o, 0).wait()
+    give(part_o, sib_o, out_ret, 0)
+    settle(1)
+    for n in range(2):
+        blocks, rows = tile(n)
+        grad_hidden = dot(flat_rows(g_all[blocks]), wd[...], ((1,), (1,)))
+        gate_val = gate_v[rows]
+        up_val = up_v[rows]
+        sig = jax.nn.sigmoid(gate_val)
+        grad_gate = (grad_hidden * up_val * sig * (1.0 + gate_val * (1.0 - sig))).astype(BF)
+        grad_up = (grad_hidden * gate_val * sig).astype(BF)
+        g_gate[rows] = grad_gate
+        g_up[rows] = grad_up
+        grad_rows = dot(grad_gate, wg[...], ((1,), (1,))) + dot(grad_up, wu[...], ((1,), (1,)))
+        part_g[blocks] = grad_rows.astype(BF).reshape(16, SLOTS, MODEL_WIDTH)
+        if n == 0:
+            swap(part_g, sib_g, 1).start()
+    swap(part_g, sib_g, 1).wait()
+    give(part_g, sib_g, grad_ret, 1)
+
+    def weights_in(j, carry):
+        cols = pl.ds(pl.multiple_of(j * 256, 256), 256)
+        left = flat_rows(x_all[:, :, cols])
+        v_gate[cols] = dot(left, g_gate[...], ((0,), (0,))).astype(BF)
+        v_up[cols] = dot(left, g_up[...], ((0,), (0,))).astype(BF)
         return carry
 
-    def push(k, carry):
-        add(k, carry)
-        t = (me + k) % 16
-        for a, (part, own, sib, ret) in enumerate(arrays):
-            remote(own.at[t], ret.at[me], send.at[a], recv.at[a], dev(y, t // 4, t % 4, c)).start()
+    lax.fori_loop(0, MODEL_WIDTH // 256, weights_in, 0)
+    stores = [
+        pltpu.make_async_copy(src, dst, o_sem.at[n])
+        for n, (src, dst) in enumerate(((v_gate, d_gate), (v_up, d_up), (v_down, d_down)))
+    ]
+    stores[0].start()
+    stores[1].start()
+
+    def weights_down(j, carry):
+        cols = pl.ds(pl.multiple_of(j * 256, 256), 256)
+        v_down[cols] = dot(hidden[:, cols], flat_rows(g_all[...]), ((0,), (0,))).astype(BF)
         return carry
 
-    lax.fori_loop(1, 16, push, 0)
-    add(16, 0)
-    here = []
-    for a, (part, own, sib, ret) in enumerate(arrays):
-        copy = pltpu.make_async_copy(own.at[me], ret.at[me], h_sem.at[a])
-        copy.start()
-        here.append(copy)
-    for a, (part, own, sib, ret) in enumerate(arrays):
-        here[a].wait()
-        remote(part.at[1 - c], sib, s_send.at[a], s_recv.at[a, 0], sibling).wait_send()
-        drain = remote(
-            own.at[pl.ds(0, 15)], ret.at[pl.ds(0, 15)], send.at[a], recv.at[a], sibling
-        )
-        drain.wait_send()
-        drain.wait_recv()
-
-
-def give_back(po, pg):
-    shape = jax.ShapeDtypeStruct((16, SLOTS, MODEL_WIDTH), BF)
-    buffer = pltpu.VMEM((16, SLOTS, MODEL_WIDTH), BF)
+    lax.fori_loop(0, 2, weights_down, 0)
+    stores[2].start()
+    for store in stores:
+        store.wait()
+    given(part_o, out_ret, 0)
+    given(part_g, grad_ret, 1)
+
+
+def experts(xs, gs, gate_w, up_w, down_w):
+    rows = 32 * SLOTS
+    width = gate_w.shape[1]
+    back = jax.ShapeDtypeStruct((16, SLOTS, MODEL_WIDTH), BF)
     return pl.pallas_call(
-        give_back_kernel,
-        out_shape=[shape, shape],
-        in_specs=[ANY] * 2,
-        out_specs=[ANY] * 2,
-        scratch_shapes=[buffer] * 4
-        + [
+        experts_kernel,
+        out_shape=[
+            back,
+            back,
+            jax.ShapeDtypeStruct(gate_w.shape, BF),
+            jax.ShapeDtypeStruct(up_w.shape, BF),
+            jax.ShapeDtypeStruct(down_w.shape, BF),
+        ],
+        in_specs=[ANY] * 5,
+        out_specs=[ANY] * 5,
+        scratch_shapes=[
+            pltpu.VMEM((32, SLOTS, MODEL_WIDTH), BF),
+            pltpu.VMEM((32, SLOTS, MODEL_WIDTH), BF),
+            pltpu.VMEM(gate_w.shape, BF),
+            pltpu.VMEM(up_w.shape, BF),
+            pltpu.VMEM(down_w.shape, BF),
+            pltpu.VMEM((rows, width), F32),
+            pltpu.VMEM((rows, width), F32),
+            pltpu.VMEM((rows, width), BF),
+            pltpu.VMEM((rows, width), BF),
+            pltpu.VMEM((rows, width), BF),
+            pltpu.VMEM((32, SLOTS, MODEL_WIDTH), BF),
+            pltpu.VMEM((32, SLOTS, MODEL_WIDTH), BF),
+            pltpu.VMEM((16, SLOTS, MODEL_WIDTH), BF),
+            pltpu.VMEM((16, SLOTS, MODEL_WIDTH), BF),
+            pltpu.VMEM(gate_w.shape, BF),
+            pltpu.VMEM(up_w.shape, BF),
+            pltpu.VMEM(down_w.shape, BF),
+            pltpu.SemaphoreType.DMA((3,)),
+            pltpu.SemaphoreType.DMA((4,)),
+            pltpu.SemaphoreType.DMA((2, 16)),
+            pltpu.SemaphoreType.DMA((2, 16)),
             pltpu.SemaphoreType.DMA((2,)),
             pltpu.SemaphoreType.DMA((2,)),
             pltpu.SemaphoreType.DMA((2,)),
-            pltpu.SemaphoreType.DMA((2, 16)),
             pltpu.SemaphoreType.DMA((2,)),
             pltpu.SemaphoreType.DMA((2,)),
-        ],
-        compiler_params=params(7, 32 << 20),
-        name="give_back",
-    )(po, pg)
+            pltpu.SemaphoreType.DMA((2,)),
+            pltpu.SemaphoreType.DMA((3,)),
+        ],
+        compiler_params=params(6, 56 << 20),
+        name="experts",
+    )(xs, gs, gate_w, up_w, down_w)
 
 
 def reduce_kernel(
@@ -656,10 +728,6 @@
         compiler_params=params(8, 48 << 20),
         name="reduce_weights",
     )(*[place_blocks(grad) for grad in grads], partial)
-
-
-def dot(a, b, dims):
-    return lax.dot_general(a, b, (dims, ((), ())), preferred_element_type=F32)
 
 
 def wide(block, head, first):
@@ -935,24 +1003,9 @@
     slots_in = dot(both, moe_in, ((0,), (0,))).astype(BF)
     grad_slots = (dot(both, cotangent, ((0,), (0,))) * slot_gate[:, None]).astype(BF)
     blocks = (EXPERT_COUNT, SLOTS, MODEL_WIDTH)
-    x_in, g_in = dispatch(slots_in.reshape(blocks), grad_slots.reshape(blocks))
-
-    expert_in = x_in.reshape(-1, MODEL_WIDTH)
-    grad_expert = g_in.reshape(-1, MODEL_WIDTH)
-    gate_val = dot(expert_in, gate_w, ((1,), (0,)))
-    up_val = dot(expert_in, up_w, ((1,), (0,)))
-    sig = jax.nn.sigmoid(gate_val)
-    hidden = (gate_val * sig * up_val).astype(BF)
-    part_out = dot(hidden, down_w, ((1,), (0,))).astype(BF)
-    grad_hidden = dot(grad_expert, down_w, ((1,), (1,)))
-    grad_gate = (grad_hidden * up_val * sig * (1.0 + gate_val * (1.0 - sig))).astype(BF)
-    grad_up = (grad_hidden * gate_val * sig).astype(BF)
-    part_grad = dot(grad_gate, gate_w, ((1,), (1,))) + dot(grad_up, up_w, ((1,), (1,)))
-    shape = (2, 16, SLOTS, MODEL_WIDTH)
-    out_ret, grad_ret = give_back(part_out.reshape(shape), part_grad.astype(BF).reshape(shape))
-    grad_w_gate = dot(expert_in, grad_gate, ((0,), (0,))).astype(BF)
-    grad_w_up = dot(expert_in, grad_up, ((0,), (0,))).astype(BF)
-    grad_w_down = dot(hidden, grad_expert, ((0,), (0,))).astype(BF)
+    out_ret, grad_ret, grad_w_gate, grad_w_up, grad_w_down = experts(
+        slots_in.reshape(blocks), grad_slots.reshape(blocks), gate_w, up_w, down_w
+    )
     expert_grads = (
         lax.psum_scatter(grad_w_gate, "dp", scatter_dimension=0, tiled=True).astype(F32),
         lax.psum_scatter(grad_w_up, "dp", scatter_dimension=0, tiled=True).astype(F32),

time: 447 us -> 406 us (0.908)
  matrix products: 59.2 us -> 31.4 us
  Pallas kernels: 314 us -> 306 us
    dot_general x29 -> x20, matrix products: 51.5 us -> 25.2 us  [dot(): return lax.dot_general(a, b, (dims, ((), ())), preferred_element_type=F32)]
    pallas_call x2 -> x1, Pallas kernels: 86.5 us -> 66.1 us  [experts(): pl.pallas_call(experts_kernel, out_shape=[back, back, jax.ShapeDtypeStruc...]
    pallas_call x1, Pallas kernels: 55.1 us -> 60 us  [reduce_weights(): pl.pallas_call(reduce_kernel, out_shape=[jax.ShapeDtypeStruct((2, 16, PAC...]
    unnamed x117 -> x109, local copies, waits for them, and re-layouts: 17.7 us -> 15.3 us
  transfers between devices with their start and end apart: 6 -> 6, of which waited for: 0 -> 0; matrix products, arithmetic and copies ran while one was open for 18% -> 15% of each run, Pallas kernels for 59% -> 46%
where the time goes in v2:
time: 406 us
  Pallas kernels  306 us (75%)
  local copies, waits for them, and re-layouts  33.7 us (8%)
  matrix products  31.4 us (8%)
  other arithmetic  17.5 us (4%)
  between operations  15.1 us (4%)
    pallas_call x1, Pallas kernels, experts(): pl.pallas_call(experts_kernel, out_shape=[back, back, jax.ShapeDtypeStruc...  66.1 us
    pallas_call x1, Pallas kernels, reduce_weights(): pl.pallas_call(reduce_kernel, out_shape=[jax.ShapeDtypeStruct((2, 16, PAC...  60 us
    pallas_call x1, Pallas kernels, gather_weights(): pl.pallas_call(gather_kernel, out_shape=[jax.ShapeDtypeStruct((4, 4, 4, 2...  51.6 us
    pallas_call x1, Pallas kernels, attn_backward(): pl.pallas_call(attn_backward_kernel, out_shape=[jax.ShapeDtypeStruct((4,...  31.9 us
    pallas_call x1, Pallas kernels, attn_forward(): pl.pallas_call(attn_forward_kernel, out_shape=[jax.ShapeDtypeStruct((4, P...  29.7 us
    dot_general x20, matrix products, dot(): return lax.dot_general(a, b, (dims, ((), ())), preferred_element_type=F32)  25.2 us
    pallas_call x1, Pallas kernels, heads_back(): pl.pallas_call(heads_back_kernel, out_shape=[jax.ShapeDtypeStruct((4, PAI...  21.7 us
    pallas_call x1, Pallas kernels, heads_out(): pl.pallas_call(heads_out_kernel, out_shape=[jax.ShapeDtypeStruct((4, PAIR...  21.6 us
  transfers between devices with their start and end apart: 6, of which 0 were waited for; matrix products, arithmetic and copies ran while one was open for 15% of the time, Pallas kernels for 46%

profile of v2, /device:TPU:1, one launch (start us, length us, event | category | flops | bytes accessed | tf_op | source)
XLA Modules:
  0.0 405.6 jit_solution(11470304637365254960)
XLA Ops:
  13.7 51.6 %gather_weights.1 = (bf16[4,4,4,24,768]{4,3,2,1,0:T(8,128)(2,1)}, bf16[4,4,4,24,512]{4,3,2,1,0:T(8,128)(2,1)}, bf16[4,4,4,24,768]{4,3,2,1,0:T(8,128)(2,1)}, bf16...) custom-call(bf16[2,16,2176]{2,1,0:T(8,128)(2,1)} %fusion.24.pack, ...), custom_call_target="tpu_custom_call" | custom-call | tf_op jit(solution)/shard_map/gather_weights/pallas_call | solution.py:165
  72.4 2.9 convolution_convert_fusion.3
  78.4 21.6 %heads_out.1 = (bf16[4,256,192]{2,1,0:T(8,128)(2,1)}, bf16[16,256,128]{2,1,0:T(8,128)(2,1)}, bf16[1536,768]{1,0:T(8,128)(2,1)}) custom-call(bf16[4,256,192]{2,1,0:T(8,128)(2,1)} %bitcast.180, bf16[4,256,128]{2,1,0:T(8,128)(2,1)} %bitcast.190, bf16[1536,768]{1,0:T(8,128)(2,1)} %bitcast.153), custom_call_target="tpu_custom_call" | custom-call | tf_op jit(solution)/shard_map/heads_out/pallas_call | solution.py:241
  102.3 29.7 %attn_forward.1 = (bf16[4,256,192]{2,1,0:T(8,128)(2,1)S(1)}, f32[4,3,64,256]{3,2,1,0:T(8,128)S(1)}, f32[4,3,1,256]{3,2,1,0:T(1,128)S(1)}) custom-call(s32[2,4]{1,0:T(2,128)S(1)} %pad_add_fusion.span, bf16[4,256,192]{2,1,0:T(8,128)(2,1)S(1)} %copy-done.2, bf16[16,256,128]{2,1,0:T(8,128)(2,1)S(1)} %copy-done, s32[4,1,256]{2,1,0:T(1,128)S(1)} %reshape.414.first_ref), custom_call_target="tpu_custom_call" | custom-call | tf_op jit(solution)/shard_map/attn_forward/pallas_call | solution.py:780
  132.8 11.5 %attn_return.1 = bf16[8,128,192]{2,1,0:T(8,128)(2,1)} custom-call(bf16[8,128,192]{2,1,0:T(8,128)(2,1)} %bitcast.151), custom_call_target="tpu_custom_call" | custom-call | tf_op jit(solution)/shard_map/attn_return/pallas_call | solution.py:361
  145.7 2.7 convolution_add_fusion.5
  150.4 1.5 convolution_convert_fusion.2
  152.0 1.6 fusion
  153.5 66.1 %experts.1 = (bf16[16,24,1536]{2,1,0:T(8,128)(2,1)}, bf16[16,24,1536]{2,1,0:T(8,128)(2,1)}, bf16[1536,512]{1,0:T(8,128)(2,1)}, bf16[1536,512]{1,0:T(8,128)(2,1)}, bf16[512,1536]{1,0:T(8,128)(2,1)}) custom-call(bf16[16,24,1536]{2,1,0:T(8,128)(2,1)} %bitcast.167, bf16[16,24,1536]{2,1,0:T(8,128)(2,1)} %bitcast.168, ...), custom_call_target="tpu_custom_call" | custom-call | tf_op jit(solution)/shard_map/experts/pallas_call | solution.py:570
  219.6 2.7 copy.101
  233.2 1.8 maximum_bitcast_fusion
  235.1 2.0 copy.94
  237.1 12.1 %grad_attn_out.1 = (bf16[8,128,192]{2,1,0:T(8,128)(2,1)}, bf16[128,1536]{1,0:T(8,128)(2,1)}, bf16[128,768]{1,0:T(8,128)(2,1)}) custom-call(bf16[8,128,192]{2,1,0:T(8,128)(2,1)} %bitcast.178, bf16[128,1536]{1,0:T(8,128)(2,1)} %copy-done.11, bf16[128,768]{1,0:T(8,128)(2,1)} %copy.95.attn), custom_call_target="tpu_custom_call" | custom-call | tf_op jit(solution)/shard_map/grad_attn_out/pallas_call | solution.py:390
  250.2 31.9 %attn_backward.1 = (bf16[4,256,192]{2,1,0:T(8,128)(2,1)S(1)}, bf16[16,256,128]{2,1,0:T(8,128)(2,1)S(1)}) custom-call(s32[2,4]{1,0:T(2,128)S(1)} %pad_add_fusion.span, bf16[4,256,192]{2,1,0:T(8,128)(2,1)S(1)} %copy-done.3, bf16[16,256,128]{2,1,0:T(8,128)(2,1)S(1)} %copy-done.1, s32[4,1,256]{2,1,0:T(1,128)S(1)} %reshape.414.first_ref, ...), custom_call_target="tpu_custom_call" | custom-call | tf_op jit(solution)/shard_map/attn_backward/pallas_call | solution.py:854
  283.9 21.7 %heads_back.1 = (bf16[4,256,192]{2,1,0:T(8,128)(2,1)}, bf16[16,256,128]{2,1,0:T(8,128)(2,1)}) custom-call(bf16[4,256,192]{2,1,0:T(8,128)(2,1)} %copy-done.5, bf16[16,256,128]{2,1,0:T(8,128)(2,1)} %copy-done.4), custom_call_target="tpu_custom_call" | custom-call | tf_op jit(solution)/shard_map/heads_back/pallas_call | solution.py:298
  309.8 1.6 convolution_convert_fusion.1
  311.5 2.4 convolution_add_fusion.2
  313.8 1.8 fusion.47
  316.7 3.1 fusion.2
  319.9 2.6 fusion.1
  324.7 2.2 add_convert_fusion
  327.0 60.0 %reduce_weights.1 = (f32[2,16,2176]{2,1,0:T(8,128)S(1)}, f32[128,1536]{1,0:T(8,128)S(1)}) custom-call(bf16[4,4,4,24,768]{4,3,2,1,0:T(8,128)(2,1)S(1)} %bitcast.148, bf16[4,4,4,24,512]{4,3,2,1,0:T(8,128)(2,1)S(1)} %bitcast.149, bf16[4,4,4,24,768]{4,3,2,1,0:T(8,128)(2,1)} %bitcast.159, bf16[4,4,4,24,128]{4,3,2,1,0:T(8,128)(2,1)S(1)} %bitcast.150, ...), custom_call_target="tpu_custom_call" | custom-call | tf_op jit(solution)/shard_map/reduce_weights/pallas_call | solution.py:713
  394.8 2.0 convert_element_type.159
  396.8 2.0 convert_element_type.160
  (220 shorter events, 51.7 us)
Async XLA Ops:
  7.2 146.3 %all-gather.4.cloned.1.call-start = ((), (), s32[]{:S(2)}) async-start(), calls=%async_computation.3 | async-start | bytes 1966080 | tf_op jit(solution)/shard_map/all_gather | solution.py:946
  65.3 6.0 %copy-start.15 = (bf16[2,128,1536]{2,1,0:T(8,128)(2,1)S(1)}, bf16[2,128,1536]{2,1,0:T(8,128)(2,1)}, u32[]{:S(2)}) copy-start(bf16[2,128,1536]{2,1,0:T(8,128)(2,1)} %get-tuple-element.44) | copy-start | bytes 2359300
  65.3 88.2 %all-gather.6.cloned.1.call-start = ((), (), s32[]{:S(2)}) async-start(), calls=%async_computation.4 | async-start | bytes 1966080 | tf_op jit(solution)/shard_map/all_gather | solution.py:947
  66.1 87.5 %all-gather.8.cloned.1.call-start = ((), (), s32[]{:S(2)}) async-start(), calls=%async_computation.5 | async-start | bytes 1966080 | tf_op jit(solution)/shard_map/all_gather | solution.py:948
  66.8 325.9 %reduce-scatter.10.cloned.1.call-start = ((), (), s32[]{:S(2)}) async-start(), calls=%async_computation.8 | async-start | bytes 1966080
  72.3 4.1 %copy-start.17 = (bf16[2,128,1536]{2,1,0:T(8,128)(2,1)}, bf16[2,128,1536]{2,1,0:T(8,128)(2,1)S(1)}, u32[]{:S(2)}) copy-start(bf16[2,128,1536]{2,1,0:T(8,128)(2,1)S(1)} %multiply_convert_fusion) | copy-start | bytes 2359300
  132.8 12.9 %copy-start.22 = (bf16[128,1536]{1,0:T(8,128)(2,1)S(1)}, bf16[128,1536]{1,0:T(8,128)(2,1)}, u32[]{:S(2)}) copy-start(bf16[128,1536]{1,0:T(8,128)(2,1)} %tokens.1) | copy-start | bytes 1179652
  145.6 2.8 copy-start.35
  145.7 2.8 copy-start.13
  149.5 78.4 %copy-start.46 = (f32[128]{0:T(128)}, f32[128]{0:T(128)S(1)}, u32[]{:S(2)}) copy-start(f32[128]{0:T(128)S(1)} %get-tuple-element.100) | copy-start | bytes 1540
  222.3 172.5 %reduce-scatter.6.cloned.1.call-start = ((), (), s32[]{:S(2)}) async-start(), calls=%async_computation.6 | async-start | bytes 1966080 | tf_op jit(solution)/shard_map/reduce_scatter | solution.py:1010
  226.6 170.2 %reduce-scatter.8.cloned.1.call-start = ((), (), s32[]{:S(2)}) async-start(), calls=%async_computation.7 | async-start | bytes 1966080 | tf_op jit(solution)/shard_map/reduce_scatter | solution.py:1011
  229.1 2.5 copy-start.11
  232.4 16.7 %copy-start.1 = (bf16[16,256,128]{2,1,0:T(8,128)(2,1)S(1)}, bf16[16,256,128]{2,1,0:T(8,128)(2,1)}, u32[]{:S(2)}) copy-start(bf16[16,256,128]{2,1,0:T(8,128)(2,1)} %get-tuple-element.50.kv_ref) | copy-start | bytes 3145732
  232.4 16.7 %copy-start.3 = (bf16[4,256,192]{2,1,0:T(8,128)(2,1)S(1)}, bf16[4,256,192]{2,1,0:T(8,128)(2,1)}, u32[]{:S(2)}) copy-start(bf16[4,256,192]{2,1,0:T(8,128)(2,1)} %get-tuple-element.49.q_ref) | copy-start | bytes 1179652
  305.5 3.6 copy-start.25
  305.6 3.6 copy-start.43
  306.9 2.9 copy-start.18
  316.7 3.2 copy-start.33
  316.7 3.2 copy-start.49
  319.9 2.7 copy-start.9
  319.9 2.7 copy-start.19
  387.0 4.1 %copy-start.10 = (f32[256,1536]{1,0:T(8,128)S(1)}, f32[256,1536]{1,0:T(8,128)}, u32[]{:S(2)}) copy-start(f32[256,1536]{1,0:T(8,128)} %copy-done.9) | copy-start | bytes 4718596
  387.0 4.1 %copy-start.23 = (bf16[128,1536]{1,0:T(8,128)(2,1)S(1)}, bf16[128,1536]{1,0:T(8,128)(2,1)}, u32[]{:S(2)}) copy-start(bf16[128,1536]{1,0:T(8,128)(2,1)} %tokens.1) | copy-start | bytes 1179652
  (33 other events, 49.5 us)
Sparse Core Ops, SparseCore 0:
  65.4 24.9 all-gather.3
  92.1 26.5 all-gather.5
  120.4 26.6 all-gather.7
  222.4 26.4 reduce-scatter.9
  251.2 25.5 reduce-scatter.5
  315.8 28.7 reduce-scatter.7

commit v3 on v2

v3 whole, which is shorter than its diff:
```python
import functools

import jax
import jax.numpy as jnp
from jax import lax
from jax.experimental import pallas as pl
from jax.experimental.pallas import tpu as pltpu
from jax.sharding import PartitionSpec as P

MODEL_WIDTH = 1536
HEADS = 24
KV = 8
HD = 64
EXPERT_COUNT = 16
FF = 1024
EXPERT_CAPACITY = 20
SLOTS = 24
ROWS = 128
PAIR = 256
HEAD_Q = 192
Q_HALF = 768
KV_HALF = 512
EXTRA = 128
PACK = Q_HALF + KV_HALF + EXTRA + Q_HALF

EPS = 1e-05
SCALE_QK = 0.125
NEGATIVE = -1e30
HIGH_PRECISION = lax.Precision.HIGHEST
MESH = pl.DeviceIdType.MESH
ANY = pl.BlockSpec(memory_space=pl.ANY)
IN_VMEM = pl.BlockSpec(memory_space=pltpu.VMEM)
BF = jnp.bfloat16
F32 = jnp.float32


def dot(a, b, dims):
    return lax.dot_general(a, b, (dims, ((), ())), preferred_element_type=F32)


def coords():
    i = lax.axis_index("ctx")
    return lax.axis_index("dp"), i // 8, (i // 2) % 4, i % 2


def dev(y, z, x, c):
    return (y, z * 8 + x * 2 + c)


def signal(target):
    pl.semaphore_signal(
        pltpu.get_barrier_semaphore(), inc=1, device_id=target, device_id_type=MESH
    )


def remote(src, dst, send, recv, target):
    return pltpu.make_async_remote_copy(
        src_ref=src, dst_ref=dst, send_sem=send, recv_sem=recv, device_id=target, device_id_type=MESH
    )


def params(cid, vmem=None):
    return pltpu.CompilerParams(collective_id=cid, has_side_effects=True, vmem_limit_bytes=vmem)


def axis_peer(axis, step):
    y, z, x, c = coords()
    if axis == "y":
        return dev((y + step) % 4, z, x, c)
    if axis == "z":
        return dev(y, (z + step) % 4, x, c)
    return dev(y, z, (x + step) % 4, c)


WIDTHS = (Q_HALF, KV_HALF, Q_HALF, EXTRA)
STARTS = (0, Q_HALF, Q_HALF + KV_HALF, 2 * Q_HALF + KV_HALF)
STEPS = (1, 3, 2)
FIRST_PARTS = (
    (0, 0, 512, ("x", "z", "y")),
    (1, 0, 512, ("y", "x", "z")),
    (0, 512, 256, ("z", "y", "x")),
    (3, 0, 128, ("z", "y", "x")),
)
OUT_PARTS = (
    (2, 0, 256, ("x", "z", "y")),
    (2, 256, 256, ("y", "x", "z")),
    (2, 512, 256, ("z", "y", "x")),
)
GATHER_PARTS = FIRST_PARTS + OUT_PARTS


def slab(ref, done, y, z, x, cols):
    return ref.at[
        slice(None) if "y" in done else y,
        slice(None) if "z" in done else z,
        slice(None) if "x" in done else x,
        slice(None),
        cols,
    ]


def gather_kernel(
    pack, tokens, segs, out0, out1, out2, out3, pair, seg_all,
    sib, block, p_send, p_recv, l_sem, s_send, s_recv, sib_send, sib_recv,
):
    y, z, x, c = coords()
    outs = (out0, out1, out2, out3)
    me = z * 8 + x * 2 + c
    sibling = dev(y, z, x, 1 - c)

    def greet(k, carry):
        signal((y, (me + k) % 32))
        return carry

    lax.fori_loop(1, 32, greet, 0)
    for step in STEPS:
        signal(axis_peer("y", step))
    pl.semaphore_wait(pltpu.get_barrier_semaphore(), 34)

    first = remote(pack.at[1 - c], sib, sib_send.at[0], sib_recv.at[0], sibling)
    first.start()
    second = remote(tokens, pair.at[c], sib_send.at[1], sib_recv.at[1], sibling)
    second.start()
    own_rows = pltpu.make_async_copy(tokens, pair.at[c], l_sem.at[4])
    own_rows.start()
    own_segs = pltpu.make_async_copy(segs, seg_all.at[me], l_sem.at[5])
    own_segs.start()

    def spread(k, carry):
        remote(segs, seg_all.at[me], s_send, s_recv, (y, (me + k) % 32)).start()
        return carry

    lax.fori_loop(1, 32, spread, 0)

    first.wait()
    own = pack[c, :12].astype(F32)
    other = sib[:12].astype(F32)
    low = jnp.where(c == 0, own, other)
    high = jnp.where(c == 0, other, own)
    block[...] = jnp.concatenate([low, high], axis=0).astype(BF)

    locals_ = []
    for n in range(4):
        cols = pl.ds(STARTS[n], WIDTHS[n])
        here = pltpu.make_async_copy(block.at[:, cols], outs[n].at[y, z, x], l_sem.at[n])
        here.start()
        locals_.append(here)
    for phase in range(3):
        copies = []
        for part, (n, start, width, order) in enumerate(GATHER_PARTS if phase < 2 else FIRST_PARTS):
            for k, step in enumerate(STEPS):
                dst = slab(outs[n], order[:phase], y, z, x, pl.ds(start, width))
                src = block.at[:, pl.ds(STARTS[n] + start, width)] if phase == 0 else dst
                copy = remote(
                    src, dst, p_send.at[phase, part, k], p_recv.at[phase, part, k],
                    axis_peer(order[phase], step),
                )
                copy.start()
                copies.append(copy)
        if phase == 0:
            for here in locals_:
                here.wait()
        for copy in copies:
            copy.wait()
    second.wait()
    own_rows.wait()
    own_segs.wait()
    drain = remote(
        seg_all.at[pl.ds(0, 31)], seg_all.at[pl.ds(0, 31)], s_send, s_recv, sibling
    )
    drain.wait_send()
    drain.wait_recv()


def gather_weights(pack, tokens, segs):
    return pl.pallas_call(
        gather_kernel,
        out_shape=[jax.ShapeDtypeStruct((4, 4, 4, 24, width), BF) for width in WIDTHS]
        + [
            jax.ShapeDtypeStruct((2, ROWS, MODEL_WIDTH), BF),
            jax.ShapeDtypeStruct((32, 1, 128), jnp.int32),
        ],
        in_specs=[IN_VMEM, ANY, ANY],
        out_specs=[ANY] * 6,
        scratch_shapes=[
            pltpu.VMEM((16, PACK), BF),
            pltpu.VMEM((24, PACK), BF),
            pltpu.SemaphoreType.DMA((3, 7, 3)),
            pltpu.SemaphoreType.DMA((3, 7, 3)),
            pltpu.SemaphoreType.DMA((6,)),
            pltpu.SemaphoreType.DMA,
            pltpu.SemaphoreType.DMA,
            pltpu.SemaphoreType.DMA((2,)),
            pltpu.SemaphoreType.DMA((2,)),
        ],
        compiler_params=params(1),
        name="gather_weights",
    )(pack, tokens, segs)


def plane_greet(y, me, c, sibling):
    def greet(k, carry):
        t = (me + k) % 16
        signal(dev(y, t // 4, t % 4, c))
        return carry

    lax.fori_loop(1, 16, greet, 0)
    if sibling is not None:
        signal(sibling)
        pl.semaphore_wait(pltpu.get_barrier_semaphore(), 16)
    else:
        pl.semaphore_wait(pltpu.get_barrier_semaphore(), 15)


def wide(block, head, first):
    part = block[:, 64 * head : 64 * head + 64]
    zero = jnp.zeros_like(part)
    return jnp.concatenate([part, zero] if first else [zero, part], axis=1)


KEYS = 1024


def attend_kernel(
    q4, kv4, half_in, cots, first_ref, q_in, kv_in, attn, ot_ref, lse_ref, half, half_sib, c_all,
    qs, acc, o_buf,
    l_sem, q_send, q_recv, k_send, k_recv, w_send, w_recv, sib_send, sib_recv,
    c_send, c_recv, f_send, f_recv, o_send, o_recv,
):
    y, z, x, c = coords()
    me = z * 4 + x
    sibling = dev(y, z, x, 1 - c)

    wide_greet()

    q_copies = []
    for n, step in enumerate(STEPS):
        to = (z + step) % 4
        copy = remote(q4.at[to], q_in.at[z], q_send.at[n], q_recv.at[n], dev(y, to, x, c))
        copy.start()
        q_copies.append(copy)

    def send_kv(k, carry):
        t = (me + k) % 16
        remote(kv4.at[t // 4], kv_in.at[me], k_send, k_recv, dev(y, t // 4, t % 4, c)).start()
        return carry

    lax.fori_loop(1, 16, send_kv, 0)
    here = [
        pltpu.make_async_copy(q4.at[z], q_in.at[z], l_sem.at[0]),
        pltpu.make_async_copy(kv4.at[z], kv_in.at[me], l_sem.at[1]),
    ]
    for copy in here:
        copy.start()
    for copy in here:
        copy.wait()
    for copy in q_copies:
        copy.wait()
    drain = remote(kv_in.at[pl.ds(0, 15)], kv_in.at[pl.ds(0, 15)], k_send, k_recv, sibling)
    drain.wait_send()
    drain.wait_recv()

    w_copies = []
    for part, (n, start, width, order) in enumerate(OUT_PARTS):
        spot = slab(half, order[:2], y, z, x, pl.ds(start, width))
        for k, step in enumerate(STEPS):
            copy = remote(
                spot, spot, w_send.at[part, k], w_recv.at[part, k], axis_peer(order[2], step)
            )
            copy.start()
            w_copies.append(copy)

    def send_cots(k, carry):
        t = (me + k) % 16
        remote(
            cots.at[t], c_all.at[c * 16 + me], c_send.at[k], c_recv.at[k], dev(y, t // 4, t % 4, c)
        ).start()
        return carry

    lax.fori_loop(1, 16, send_cots, 0)
    own_cots = pltpu.make_async_copy(cots.at[me], c_all.at[c * 16 + me], l_sem.at[2])
    own_cots.start()
    remote(cots.at[me], c_all.at[c * 16 + me], f_send, f_recv, sibling).start()

    def forward_cots(k, carry):
        s = c * 16 + (me + 16 - k) % 16
        t = (me + k) % 16
        arrived = remote(cots.at[t], c_all.at[s], c_send.at[k], c_recv.at[k], dev(y, t // 4, t % 4, c))
        arrived.wait_recv()
        remote(c_all.at[s], c_all.at[s], f_send, f_recv, sibling).start()
        arrived.wait_send()
        return carry

    swap = remote(half, half_sib, sib_send, sib_recv, sibling)
    j = z * 2 + c
    returns = []
    for n in range(4):
        zq = (z + n + 1) % 4
        q = q_in[zq] * SCALE_QK
        for h in range(3):
            qs[256 * h : 256 * h + 256] = wide(q, h, True)
        acc[...] = jnp.zeros_like(acc)
        first = first_ref[zq]
        q_pos = (zq * 4 + x) * PAIR + lax.broadcasted_iota(jnp.int32, (1, PAIR), 1)

        def step(kb, stats):
            kv = kv_in[pl.ds(kb * (KEYS // PAIR), KEYS // PAIR)].reshape(KEYS, 128)
            k_pos = kb * KEYS + lax.broadcasted_iota(jnp.int32, (KEYS, PAIR), 0)
            ok = (k_pos >= first) & (k_pos <= q_pos)
            scores = [dot(kv, qs[256 * h : 256 * h + 256], ((1,), (1,))) for h in range(3)]
            later, probs, shrinks = [], [], []
            for h in range(3):
                top, tot = stats[h]
                masked = jnp.where(ok, scores[h], NEGATIVE)
                new = jnp.maximum(top, jnp.max(masked, axis=0, keepdims=True))
                prob = jnp.exp(masked - new)
                shrink = jnp.exp(top - new)
                later.append((new, tot * shrink + jnp.sum(prob, axis=0, keepdims=True)))
                probs.append(prob.astype(BF))
                shrinks.append(shrink)
            for h in range(3):
                cols = slice(256 * h, 256 * h + 256)
                acc[:, cols] = acc[:, cols] * shrinks[h] + dot(kv, probs[h], ((0,), (0,)))
            return tuple(later)

        none = (jnp.full((1, PAIR), NEGATIVE, F32), jnp.zeros((1, PAIR), F32))
        stats = lax.fori_loop(0, zq + 1, step, (none, none, none))
        heads = []
        for h in range(3):
            cols = slice(256 * h, 256 * h + 256)
            mixed = acc[64:, cols] / stats[h][1]
            ot_ref[zq, :, cols] = mixed
            lse_ref[zq, :, cols] = stats[h][0] + jnp.log(stats[h][1])
            heads.append(mixed)
        heads = jnp.concatenate(heads, axis=0)
        rows = jnp.transpose(heads).astype(BF)
        o_buf[n, 0] = rows[:ROWS]
        o_buf[n, 1] = rows[ROWS:]
        for d in range(2):
            core = c if d == 0 else 1 - c
            if n == 3 and d == 0:
                back = pltpu.make_async_copy(o_buf.at[n, core], attn.at[j], l_sem.at[3])
            else:
                back = remote(
                    o_buf.at[n, core], attn.at[j], o_send.at[n, d], o_recv.at[n, d], dev(y, zq, x, core)
                )
            back.start()
            returns.append(back)
        if n == 1:
            for copy in w_copies:
                copy.wait()
            swap.start()
        if n == 2:
            lax.fori_loop(1, 16, forward_cots, 0)
    own_cots.wait()
    mine = c_all.at[pl.ds(c * 16, 16)]
    drain = remote(mine, mine, f_send, f_recv, sibling)
    drain.wait_send()
    drain.wait_recv()
    swap.wait()
    for back in returns:
        back.wait()


def attend(q4, kv4, half, cots, first):
    blocks = jax.ShapeDtypeStruct((4, 4, 4, 24, Q_HALF), BF)
    return pl.pallas_call(
        attend_kernel,
        out_shape=[
            jax.ShapeDtypeStruct((4, PAIR, HEAD_Q), BF),
            jax.ShapeDtypeStruct((16, PAIR, 128), BF),
            jax.ShapeDtypeStruct((8, ROWS, HEAD_Q), BF),
            jax.ShapeDtypeStruct((4, HD, 3 * PAIR), F32),
            jax.ShapeDtypeStruct((4, 1, 3 * PAIR), F32),
            blocks,
            blocks,
            jax.ShapeDtypeStruct((32, SLOTS, MODEL_WIDTH), BF),
        ],
        in_specs=[ANY, ANY, ANY, ANY, IN_VMEM],
        out_specs=[IN_VMEM, IN_VMEM, ANY, IN_VMEM, IN_VMEM, ANY, ANY, ANY],
        input_output_aliases={2: 5},
        scratch_shapes=[
            pltpu.VMEM((3 * PAIR, 128), BF),
            pltpu.VMEM((128, 3 * PAIR), F32),
            pltpu.VMEM((4, 2, ROWS, HEAD_Q), BF),
            pltpu.SemaphoreType.DMA((4,)),
            pltpu.SemaphoreType.DMA((3,)),
            pltpu.SemaphoreType.DMA((3,)),
            pltpu.SemaphoreType.DMA,
            pltpu.SemaphoreType.DMA,
            pltpu.SemaphoreType.DMA((3, 3)),
            pltpu.SemaphoreType.DMA((3, 3)),
            pltpu.SemaphoreType.DMA,
            pltpu.SemaphoreType.DMA,
            pltpu.SemaphoreType.DMA((16,)),
            pltpu.SemaphoreType.DMA((16,)),
            pltpu.SemaphoreType.DMA,
            pltpu.SemaphoreType.DMA,
            pltpu.SemaphoreType.DMA((4, 2)),
            pltpu.SemaphoreType.DMA((4, 2)),
        ],
        compiler_params=params(2, 56 << 20),
        name="attend",
    )(q4, kv4, half, cots, first)


def flat_rows(blocks):
    return blocks.reshape(blocks.shape[0] * SLOTS, blocks.shape[2])


def experts_kernel(
    xs, gates, cots, weights, out_ret, grad_ret, d_all,
    x_all, t_all, g_all, w_all, gate_v, up_v, hidden, g_both, part_o, part_g, sib_o, sib_g,
    v_all,
    w_sem, l_sem, send, recv, f_send, f_recv, s_send, s_recv, r_send, r_recv, o_sem,
):
    y, z, x, c = coords()
    me = z * 4 + x
    width = hidden.shape[1]
    sibling = dev(y, z, x, 1 - c)
    plane_greet(y, me, c, sibling)
    loads = [
        pltpu.make_async_copy(src, dst, w_sem.at[n])
        for n, (src, dst) in enumerate(((weights, w_all), (cots, g_all)))
    ]
    for load in loads:
        load.start()
    arrays = ((xs, x_all), (gates, t_all))

    def scatter(a):
        src, dst = arrays[a]

        def push(k, carry):
            t = (me + k) % 16
            remote(
                src.at[t], dst.at[c * 16 + me], send.at[a, k], recv.at[a, k], dev(y, t // 4, t % 4, c)
            ).start()
            return carry

        lax.fori_loop(1, 16, push, 0)
        pltpu.make_async_copy(src.at[me], dst.at[c * 16 + me], l_sem.at[a]).start()
        remote(src.at[me], dst.at[c * 16 + me], f_send.at[a], f_recv.at[a], sibling).start()

    def hand_over(a):
        src, dst = arrays[a]

        def forward(k, carry):
            s = (me + 16 - k) % 16
            t = (me + k) % 16
            arrived = remote(
                src.at[t], dst.at[c * 16 + s], send.at[a, k], recv.at[a, k], dev(y, t // 4, t % 4, c)
            )
            arrived.wait_recv()
            remote(
                dst.at[c * 16 + s], dst.at[c * 16 + s], f_send.at[a], f_recv.at[a], sibling
            ).start()
            arrived.wait_send()
            return carry

        lax.fori_loop(1, 16, forward, 0)

    def settle(a):
        src, dst = arrays[a]
        pltpu.make_async_copy(src.at[me], dst.at[c * 16 + me], l_sem.at[a]).wait()
        half = pl.ds(0, 16)
        drain = remote(dst.at[half], dst.at[half], f_send.at[a], f_recv.at[a], sibling)
        drain.wait_send()
        drain.wait_recv()

    def swap(part, sib, a):
        rows = pl.ds((1 - c) * 16, 16)
        return remote(part.at[rows], sib, s_send.at[a], s_recv.at[a], sibling)

    def give(part, sib, ret, a):
        def add(t):
            rows = c * 16 + t
            part[rows] = (
                part[rows].astype(F32) + sib[t].astype(F32)
            ).astype(BF)
            return part.at[rows]

        def push(k, carry):
            t = (me + k) % 16
            remote(add(t), ret.at[me], r_send.at[a], r_recv.at[a], dev(y, t // 4, t % 4, c)).start()
            return carry

        lax.fori_loop(1, 16, push, 0)
        pltpu.make_async_copy(add(me), ret.at[me], l_sem.at[2 + a]).start()

    def given(part, ret, a):
        pltpu.make_async_copy(part.at[c * 16 + me], ret.at[me], l_sem.at[2 + a]).wait()
        drain = remote(ret.at[pl.ds(0, 15)], ret.at[pl.ds(0, 15)], r_send.at[a], r_recv.at[a], sibling)
        drain.wait_send()
        drain.wait_recv()

    def tile(n):
        h = 1 - c if n == 0 else c
        rows = 16 * SLOTS
        return pl.ds(h * 16, 16), pl.ds(pl.multiple_of(h * rows, rows), rows)

    scatter(0)
    scatter(1)
    hand_over(0)
    hand_over(1)
    settle(0)
    settle(1)
    for load in loads:
        load.wait()
    for n in range(2):
        blocks, rows = tile(n)
        rows_in = flat_rows(x_all[blocks])
        both = dot(rows_in, w_all[:, : 2 * width], ((1,), (0,)))
        gate_val, up_val = both[:, :width], both[:, width:]
        gate_v[rows] = gate_val
        up_v[rows] = up_val
        low = (gate_val * jax.nn.sigmoid(gate_val) * up_val).astype(BF)
        hidden[rows] = low
        part_o[blocks] = dot(low, w_all[:, 2 * width :], ((1,), (1,))).astype(BF).reshape(16, SLOTS, MODEL_WIDTH)
        if n == 0:
            swap(part_o, sib_o, 0).start()
    swap(part_o, sib_o, 0).wait()
    give(part_o, sib_o, out_ret, 0)
    for n in range(2):
        blocks, rows = tile(n)
        scale = jnp.concatenate([flat_rows(t_all[blocks])] * (MODEL_WIDTH // 128), axis=1)
        grad_expert = (flat_rows(g_all[blocks]).astype(F32) * scale).astype(BF)
        g_all[blocks] = grad_expert.reshape(16, SLOTS, MODEL_WIDTH)
        grad_hidden = dot(grad_expert, w_all[:, 2 * width :], ((1,), (0,)))
        gate_val = gate_v[rows]
        up_val = up_v[rows]
        sig = jax.nn.sigmoid(gate_val)
        grad_gate = (grad_hidden * up_val * sig * (1.0 + gate_val * (1.0 - sig))).astype(BF)
        grad_up = (grad_hidden * gate_val * sig).astype(BF)
        grads = jnp.concatenate([grad_gate, grad_up], axis=1)
        g_both[rows] = grads
        grad_rows = dot(grads, w_all[:, : 2 * width], ((1,), (1,)))
        part_g[blocks] = grad_rows.astype(BF).reshape(16, SLOTS, MODEL_WIDTH)
        if n == 0:
            swap(part_g, sib_g, 1).start()
    swap(part_g, sib_g, 1).wait()
    give(part_g, sib_g, grad_ret, 1)

    def weight_grads(j, carry):
        cols = pl.ds(pl.multiple_of(j * 256, 256), 256)
        v_all[cols, : 2 * width] = dot(flat_rows(x_all[:, :, cols]), g_both[...], ((0,), (0,))).astype(BF)
        v_all[cols, 2 * width :] = dot(flat_rows(g_all[:, :, cols]), hidden[...], ((0,), (0,))).astype(BF)
        return carry

    lax.fori_loop(0, MODEL_WIDTH // 256, weight_grads, 0)
    store = pltpu.make_async_copy(v_all, d_all, o_sem)
    store.start()
    store.wait()
    given(part_o, out_ret, 0)
    given(part_g, grad_ret, 1)


def experts(xs, gates, cots, weights):
    rows = 32 * SLOTS
    width = weights.shape[1] // 3
    back = jax.ShapeDtypeStruct((16, SLOTS, MODEL_WIDTH), BF)
    return pl.pallas_call(
        experts_kernel,
        out_shape=[back, back, jax.ShapeDtypeStruct(weights.shape, BF)],
        in_specs=[ANY] * 4,
        out_specs=[ANY] * 3,
        scratch_shapes=[
            pltpu.VMEM((32, SLOTS, MODEL_WIDTH), BF),
            pltpu.VMEM((32, SLOTS, 128), F32),
            pltpu.VMEM((32, SLOTS, MODEL_WIDTH), BF),
            pltpu.VMEM(weights.shape, BF),
            pltpu.VMEM((rows, width), F32),
            pltpu.VMEM((rows, width), F32),
            pltpu.VMEM((rows, width), BF),
            pltpu.VMEM((rows, 2 * width), BF),
            pltpu.VMEM((32, SLOTS, MODEL_WIDTH), BF),
            pltpu.VMEM((32, SLOTS, MODEL_WIDTH), BF),
            pltpu.VMEM((16, SLOTS, MODEL_WIDTH), BF),
            pltpu.VMEM((16, SLOTS, MODEL_WIDTH), BF),
            pltpu.VMEM(weights.shape, BF),
            pltpu.SemaphoreType.DMA((2,)),
            pltpu.SemaphoreType.DMA((4,)),
            pltpu.SemaphoreType.DMA((2, 16)),
            pltpu.SemaphoreType.DMA((2, 16)),
            pltpu.SemaphoreType.DMA((2,)),
            pltpu.SemaphoreType.DMA((2,)),
            pltpu.SemaphoreType.DMA((2,)),
            pltpu.SemaphoreType.DMA((2,)),
            pltpu.SemaphoreType.DMA((2,)),
            pltpu.SemaphoreType.DMA((2,)),
            pltpu.SemaphoreType.DMA,
        ],
        compiler_params=params(6, 56 << 20),
        name="experts",
    )(xs, gates, cots, weights)


def reduce_kernel(g_q, g_kv, g_extra, ready, partial, out, sib_partial, *rest):
    parts = len(FIRST_PARTS)
    arrive = [rest[parts * k : parts * k + parts] for k in range(3)]
    held = [None, rest[3 * parts : 4 * parts], rest[4 * parts : 5 * parts]]
    total, give, send, recv, sib_send, sib_recv = rest[5 * parts :]
    grads = (g_q, g_kv, None, g_extra)
    y, z, x, c = coords()
    place = {"y": y, "z": z, "x": x}
    sibling = dev(y, z, x, 1 - c)
    for axis in ("x", "y", "z"):
        for step in STEPS:
            signal(axis_peer(axis, step))
    signal(sibling)
    pl.semaphore_wait(pltpu.get_barrier_semaphore(), 10)
    other = remote(partial, sib_partial, sib_send.at[0], sib_recv.at[0], sibling)
    other.start()

    def at(phase, part, index):
        n, start, width, order = FIRST_PARTS[part]
        order = order[::-1]
        spot = [
            index if axis == order[phase] else slice(None)
            for axis in ("y", "z", "x")
            if axis not in order[:phase]
        ]
        if phase == 0:
            return grads[n].at[tuple(spot) + (slice(None), pl.ds(start, width))]
        return held[phase][part].at[tuple(spot)]

    for phase in range(3):
        copies = []
        for part in range(parts):
            axis = FIRST_PARTS[part][3][::-1][phase]
            for n, step in enumerate(STEPS):
                copy = remote(
                    at(phase, part, (place[axis] + step) % 4),
                    arrive[phase][part].at[n],
                    send.at[phase, part, n],
                    recv.at[phase, part, n],
                    axis_peer(axis, step),
                )
                copy.start()
                copies.append(copy)
        for copy in copies:
            copy.wait()
        for part in range(parts):
            array, start, width, order = FIRST_PARTS[part]
            mine = at(phase, part, place[order[::-1][phase]])
            got = arrive[phase][part]
            if phase < 2:

                def add(p, carry):
                    value = mine[p].astype(F32)
                    for n in range(3):
                        value = value + got[n, p].astype(F32)
                    held[phase + 1][part][p] = value.astype(BF)
                    return carry

                lax.fori_loop(0, 4, add, 0)
            else:
                value = mine[...].astype(F32)
                for n in range(3):
                    value = value + got[n].astype(F32)
                total[:, STARTS[array] + start : STARTS[array] + start + width] = value
    total[:, STARTS[2] : STARTS[3]] = ready[...]
    low, high = total[0:12], total[12:24]
    out[c, 0:12] = jnp.where(c == 0, low, high)
    out[c, 12:16] = jnp.zeros((4, PACK), F32)
    give[0:12] = jnp.where(c == 0, high, low)
    give[12:16] = jnp.zeros((4, PACK), F32)
    last = remote(give, out.at[c], sib_send.at[1], sib_recv.at[1], sibling)
    last.start()
    last.wait()
    other.wait()


def place_blocks(full):
    return full.reshape(4, 4, 4, 24, full.shape[-1])


def reduce_weights(g_q, g_kv, g_extra, ready, partial):
    widths = [part[2] for part in FIRST_PARTS]
    scratch = (
        [pltpu.VMEM((3, 4, 4, 24, w), BF) for w in widths]
        + [pltpu.VMEM((3, 4, 24, w), BF) for w in widths]
        + [pltpu.VMEM((3, 24, w), BF) for w in widths]
        + [pltpu.VMEM((4, 4, 24, w), BF) for w in widths]
        + [pltpu.VMEM((4, 24, w), BF) for w in widths]
        + [pltpu.VMEM((24, PACK), F32), pltpu.VMEM((16, PACK), F32)]
    )
    sems = (3, len(FIRST_PARTS), 3)
    return pl.pallas_call(
        reduce_kernel,
        out_shape=[
            jax.ShapeDtypeStruct((2, 16, PACK), F32),
            jax.ShapeDtypeStruct((ROWS, MODEL_WIDTH), F32),
        ],
        in_specs=[IN_VMEM] * 4 + [ANY],
        out_specs=[IN_VMEM, ANY],
        scratch_shapes=scratch
        + [
            pltpu.SemaphoreType.DMA(sems),
            pltpu.SemaphoreType.DMA(sems),
            pltpu.SemaphoreType.DMA((2,)),
            pltpu.SemaphoreType.DMA((2,)),
        ],
        compiler_params=params(8, 48 << 20),
        name="reduce_weights",
    )(place_blocks(g_q), place_blocks(g_kv), place_blocks(g_extra), ready, partial)


def wide_greet():
    y, z, x, c = coords()
    me = z * 4 + x

    def greet(k, carry):
        t = (me + k) % 16
        signal(dev(y, t // 4, t % 4, c))
        return carry

    lax.fori_loop(1, 16, greet, 0)
    for step in STEPS:
        signal(axis_peer("y", step))
        signal(dev(y, (z + step) % 4, x, 1 - c))
    signal(dev(y, z, x, 1 - c))
    pl.semaphore_wait(pltpu.get_barrier_semaphore(), 22)


def attend_back_kernel(
    heads, branch, own_attn, other_attn, q_in, kv_in, first_ref, ot_ref, lse_ref,
    dq_out, dkv_out, total,
    go, branch_sib, attn_sib, qs, gs, dq, dkv, dkv_low, dq_low,
    g_out, s_out, t_out, a_out, b_out, c_out,
    l_sem, h_send, h_recv, sib_send, sib_recv, q_send, q_recv, k_send, k_recv,
    w_send, w_recv,
):
    y, z, x, c = coords()
    me = z * 4 + x
    j = z * 2 + c
    sibling = dev(y, z, x, 1 - c)
    place = {"y": y, "z": z, "x": x}
    wide_greet()

    def push(k, carry):
        t = (j + k) % 8
        remote(heads.at[t], go.at[j], h_send, h_recv, dev(y, t // 2, x, t % 2)).start()
        return carry

    lax.fori_loop(1, 8, push, 0)
    one = remote(branch, branch_sib, sib_send.at[0], sib_recv.at[0], sibling)
    one.start()
    two = remote(other_attn, attn_sib, sib_send.at[1], sib_recv.at[1], sibling)
    two.start()
    here = pltpu.make_async_copy(heads.at[j], go.at[j], l_sem.at[0])
    here.start()
    here.wait()
    drain = remote(go.at[pl.ds(0, 7)], go.at[pl.ds(0, 7)], h_send, h_recv, sibling)
    drain.wait_send()
    drain.wait_recv()
    one.wait()
    two.wait()

    rows_b = jnp.concatenate([branch[...], branch_sib[...]], axis=0)
    rows_a = jnp.concatenate([own_attn[...], attn_sib[...]], axis=0)
    for n in range(4):
        part = dot(rows_b[:, 384 * n : 384 * n + 384], rows_a, ((0,), (0,)))
        g_out[n] = part.astype(BF).reshape(4, 4, 24, Q_HALF)

    held = (g_out, s_out, t_out)
    arrive = (a_out, b_out, c_out)

    def spot(phase, part, index):
        n, start, width, order = OUT_PARTS[part]
        order = order[::-1]
        cut = [
            index if axis == order[phase] else slice(None)
            for axis in ("y", "z", "x")
            if axis not in order[:phase]
        ]
        if phase == 0:
            return held[0].at[tuple(cut) + (slice(None), pl.ds(start, width))]
        return held[phase].at[(part,) + tuple(cut)]

    def w_copies(phase):
        copies = []
        for part in range(3):
            axis = OUT_PARTS[part][3][::-1][phase]
            for n, step in enumerate(STEPS):
                copies.append(
                    remote(
                        spot(phase, part, (place[axis] + step) % 4), arrive[phase].at[part, n],
                        w_send.at[phase, part, n], w_recv.at[phase, part, n], axis_peer(axis, step),
                    )
                )
        return copies

    def w_sum(phase):
        for copy in w_copies(phase):
            copy.wait()
        for part in range(3):
            n, start, width, order = OUT_PARTS[part]
            mine = spot(phase, part, place[order[::-1][phase]])
            if phase == 2:
                value = mine[...].astype(F32)
                for k in range(3):
                    value = value + arrive[2][part, k].astype(F32)
                total[:, start : start + width] = value
            else:

                def add(p, carry):
                    value = mine[p].astype(F32)
                    for k in range(3):
                        value = value + arrive[phase][part, k, p].astype(F32)
                    held[phase + 1][part, p] = value.astype(BF)
                    return carry

                lax.fori_loop(0, 4, add, 0)

    for copy in w_copies(0):
        copy.start()

    dkv[...] = jnp.zeros_like(dkv)
    for n in range(4):
        zq = 3 - n
        q = q_in[zq] * SCALE_QK
        grad = jnp.concatenate([go[2 * zq], go[2 * zq + 1]], axis=0)
        grad_t = jnp.transpose(grad.astype(F32))
        deltas, sums_log = [], []
        for h in range(3):
            cols = slice(256 * h, 256 * h + 256)
            qs[cols] = wide(q, h, True)
            gs[cols] = wide(grad, h, False)
            deltas.append(
                jnp.sum(grad_t[64 * h : 64 * h + 64] * ot_ref[zq, :, cols], axis=0, keepdims=True)
            )
            sums_log.append(lse_ref[zq, :, cols])
        dq[...] = jnp.zeros_like(dq)
        first = first_ref[zq]
        hi = zq * 4 + x
        q_pos = hi * PAIR + lax.broadcasted_iota(jnp.int32, (1, PAIR), 1)

        def step(kb, carry):
            kv = kv_in[kb]
            k_pos = kb * PAIR + lax.broadcasted_iota(jnp.int32, (PAIR, PAIR), 0)
            ok = (k_pos >= first) & (k_pos <= q_pos)
            scores = [dot(kv, qs[256 * h : 256 * h + 256], ((1,), (1,))) for h in range(3)]
            grad_probs = [dot(kv, gs[256 * h : 256 * h + 256], ((1,), (1,))) for h in range(3)]
            grad_scores, probs = [], []
            for h in range(3):
                prob = jnp.where(ok, jnp.exp(scores[h] - sums_log[h]), 0.0)
                grad_scores.append((prob * (grad_probs[h] - deltas[h])).astype(BF))
                probs.append(prob.astype(BF))
            for h in range(3):
                cols = slice(256 * h, 256 * h + 256)
                dq[:, cols] = dq[:, cols] + dot(kv, grad_scores[h], ((0,), (0,)))
            dkv[kb] = (
                dkv[kb]
                + dot(jnp.concatenate(grad_scores, axis=1), qs[...], ((1,), (0,)))
                + dot(jnp.concatenate(probs, axis=1), gs[...], ((1,), (0,)))
            )
            return carry

        lax.fori_loop(0, hi + 1, step, 0)
        by_head = jnp.concatenate([dq[:64, 256 * h : 256 * h + 256] for h in range(3)], axis=0)
        dq_low[zq] = jnp.transpose(by_head * SCALE_QK).astype(BF)
        away = (zq - z + 4) % 4

        @pl.when(away != 0)
        def _():
            remote(dq_low.at[zq], dq_out.at[z], q_send.at[away], q_recv.at[away], dev(y, zq, x, c)).start()

        @pl.when(away == 0)
        def _():
            pltpu.make_async_copy(dq_low.at[zq], dq_out.at[z], l_sem.at[1]).start()

        for xt in range(4):
            t = zq * 4 + xt
            dkv_low[t] = dkv[t].astype(BF)

            @pl.when(t != me)
            def _():
                remote(dkv_low.at[t], dkv_out.at[me], k_send, k_recv, dev(y, zq, xt, c)).start()

            @pl.when(t == me)
            def _():
                pltpu.make_async_copy(dkv_low.at[t], dkv_out.at[me], l_sem.at[2]).start()

        if n in (1, 2):
            w_sum(n - 1)
            for copy in w_copies(n):
                copy.start()

    w_sum(2)
    pltpu.make_async_copy(dq_low.at[z], dq_out.at[z], l_sem.at[1]).wait()
    pltpu.make_async_copy(dkv_low.at[me], dkv_out.at[me], l_sem.at[2]).wait()
    for k in range(1, 4):
        done = remote(dq_low.at[0], dq_out.at[0], q_send.at[k], q_recv.at[k], sibling)
        done.wait_send()
        done.wait_recv()
    drain = remote(dkv_out.at[pl.ds(0, 15)], dkv_out.at[pl.ds(0, 15)], k_send, k_recv, sibling)
    drain.wait_send()
    drain.wait_recv()


def attend_back(heads, branch, own_attn, other_attn, q_in, kv_in, first, ot, lse):
    return pl.pallas_call(
        attend_back_kernel,
        out_shape=[
            jax.ShapeDtypeStruct((4, PAIR, HEAD_Q), BF),
            jax.ShapeDtypeStruct((16, PAIR, 128), BF),
            jax.ShapeDtypeStruct((24, Q_HALF), F32),
        ],
        in_specs=[ANY] + [IN_VMEM] * 8,
        out_specs=[ANY, ANY, IN_VMEM],
        scratch_shapes=[
            pltpu.VMEM((8, ROWS, HEAD_Q), BF),
            pltpu.VMEM((ROWS, MODEL_WIDTH), BF),
            pltpu.VMEM((ROWS, Q_HALF), BF),
            pltpu.VMEM((3 * PAIR, 128), BF),
            pltpu.VMEM((3 * PAIR, 128), BF),
            pltpu.VMEM((128, 3 * PAIR), F32),
            pltpu.VMEM((16, PAIR, 128), F32),
            pltpu.VMEM((16, PAIR, 128), BF),
            pltpu.VMEM((4, PAIR, HEAD_Q), BF),
            pltpu.VMEM((4, 4, 4, 24, Q_HALF), BF),
            pltpu.VMEM((3, 4, 4, 24, 256), BF),
            pltpu.VMEM((3, 4, 24, 256), BF),
            pltpu.VMEM((3, 3, 4, 4, 24, 256), BF),
            pltpu.VMEM((3, 3, 4, 24, 256), BF),
            pltpu.VMEM((3, 3, 24, 256), BF),
            pltpu.SemaphoreType.DMA((3,)),
            pltpu.SemaphoreType.DMA,
            pltpu.SemaphoreType.DMA,
            pltpu.SemaphoreType.DMA((2,)),
            pltpu.SemaphoreType.DMA((2,)),
            pltpu.SemaphoreType.DMA((4,)),
            pltpu.SemaphoreType.DMA((4,)),
            pltpu.SemaphoreType.DMA,
            pltpu.SemaphoreType.DMA,
            pltpu.SemaphoreType.DMA((3, 3, 3)),
            pltpu.SemaphoreType.DMA((3, 3, 3)),
        ],
        compiler_params=params(4, 58 << 20),
        name="attend_back",
    )(heads, branch, own_attn, other_attn, q_in, kv_in, first, ot, lse)


def inverse_rms(values):
    return lax.rsqrt(jnp.mean(values * values, axis=-1, keepdims=True) + EPS)


def norm_backward(values, inverse, gain, grad_out):
    scaled = grad_out * gain
    return inverse * scaled - values * inverse**3 * jnp.mean(values * scaled, axis=-1, keepdims=True)


def column_sums(left, right):
    return lax.dot_general(left, right, (((0,), (0,)), ((), ())), precision=HIGH_PRECISION)


def only_column(rows, column):
    return jnp.broadcast_to((jnp.arange(EXTRA) == column).astype(F32), (rows, EXTRA))


def halves(matrix):
    return matrix.reshape(12, 2, Q_HALF).transpose(1, 0, 2)


def local(
    tokens,
    segment_ids,
    expert_ids,
    w_query,
    w_key,
    w_value,
    w_out,
    w_router,
    gain_attn,
    gain_moe,
    w_gate,
    w_up,
    w_down,
    cotangent,
):
    y, z, x, c = coords()
    width = w_gate.shape[1]
    key_value = jnp.concatenate(
        [w_key.reshape(12, 2, 4, HD), w_value.reshape(12, 2, 4, HD)], axis=3
    ).reshape(12, 2, KV_HALF)
    extra = jnp.concatenate(
        [w_router, gain_attn[:, None], gain_moe[:, None], jnp.zeros((12, EXTRA - 18), BF)], axis=1
    )
    pack = jnp.concatenate(
        [
            halves(w_query),
            key_value.transpose(1, 0, 2),
            halves(w_out.T),
            jnp.broadcast_to(extra[None], (2, 12, EXTRA)),
        ],
        axis=2,
    )
    pack = jnp.pad(pack, ((0, 0), (0, 4), (0, 0)))
    w_experts = jnp.concatenate([w_gate, w_up, w_down.T], axis=1)
    part_q, part_kv, part_out, part_extra, pair, seg_all = gather_weights(
        pack, tokens, segment_ids
    )
    pair, w_experts = lax.optimization_barrier((pair, w_experts))
    full_experts = lax.all_gather(w_experts, "dp", axis=0, tiled=True)
    full_q = part_q.reshape(MODEL_WIDTH, Q_HALF)
    full_kv = part_kv.reshape(MODEL_WIDTH, KV_HALF)
    full_extra = part_extra.reshape(MODEL_WIDTH, EXTRA)
    picks = (jnp.arange(EXTRA)[None, :] == jnp.arange(8)[:, None] + EXPERT_COUNT).astype(BF)
    gains = dot(picks, full_extra, ((1,), (1,)))
    gain_a, gain_m = gains[0:1], gains[1:2]
    router = full_extra[:, :EXPERT_COUNT]

    inputs2 = pair.reshape(PAIR, MODEL_WIDTH).astype(F32)
    inverse_a = inverse_rms(inputs2)
    normed = (inputs2 * inverse_a * gain_a).astype(BF)
    queries = dot(normed, full_q, ((1,), (0,))).astype(BF)
    keys_values = dot(normed, full_kv, ((1,), (0,))).astype(BF)
    q4 = queries.reshape(PAIR, 4, HEAD_Q).transpose(1, 0, 2)
    kv4 = keys_values.reshape(PAIR, 4, 128).transpose(1, 0, 2)
    segs = seg_all.reshape(1, 4096)
    counts = jnp.sum((segs < jnp.arange(16)[:, None]).astype(jnp.int32), axis=1)
    row_segs = lax.dynamic_index_in_dim(seg_all.reshape(4, 4, PAIR), x, 1, keepdims=False)
    first = jnp.sum(
        jnp.where(row_segs[:, :, None] == jnp.arange(16), counts, 0), axis=2
    )
    first = first.reshape(4, 1, PAIR)
    chosen = (expert_ids[:, :, None] == jnp.arange(EXPERT_COUNT, dtype=jnp.int32)).astype(F32)
    used = jnp.sum(chosen, axis=1)
    earlier = (jnp.arange(ROWS)[:, None] > jnp.arange(ROWS)[None, :]).astype(BF)
    before = dot(earlier, used.astype(BF), ((1,), (0,)))
    place = jnp.sum(chosen * before[:, None, :], axis=-1)
    slot = jnp.where(
        place < EXPERT_CAPACITY, expert_ids * SLOTS + place.astype(jnp.int32), -1
    )
    hit = (slot.T[:, :, None] == jnp.arange(EXPERT_COUNT * SLOTS, dtype=jnp.int32)).astype(F32)
    both = (hit[0] + hit[1]).astype(BF)
    blocks = (EXPERT_COUNT, SLOTS, MODEL_WIDTH)
    cot_slots = dot(both, cotangent, ((0,), (0,))).astype(BF)
    q_in, kv_in, attn, attn_t, lse, half_out, sib_out, cot_all = attend(
        q4, kv4, part_out, cot_slots.reshape(blocks), first
    )
    half_out = half_out.reshape(MODEL_WIDTH, Q_HALF)
    sib_out = sib_out.reshape(MODEL_WIDTH, Q_HALF)
    attn = attn.reshape(4, 2, ROWS, HEAD_Q).transpose(1, 2, 0, 3).reshape(2, ROWS, Q_HALF)

    own_attn = jnp.where(c == 0, attn[0], attn[1])
    other_attn = jnp.where(c == 0, attn[1], attn[0])
    inputs = tokens.astype(F32)
    middle = (
        inputs
        + dot(own_attn, half_out, ((1,), (1,)))
        + dot(other_attn, sib_out, ((1,), (1,)))
    )
    inverse_m = inverse_rms(middle)
    moe_in = (middle * inverse_m * gain_m).astype(BF)
    logits = dot(moe_in, router, ((1,), (0,)))
    picked = jnp.sum(chosen * logits[:, None, :], axis=-1)
    gates = jax.nn.softmax(picked, axis=-1)
    slot_gate = jnp.sum(hit * gates.T[:, :, None], axis=(0, 1))
    slots_in = dot(both, moe_in, ((0,), (0,))).astype(BF)
    slot_gate = jnp.broadcast_to(slot_gate.reshape(EXPERT_COUNT, SLOTS, 1), (EXPERT_COUNT, SLOTS, 128))
    out_ret, grad_ret, grad_experts = experts(
        slots_in.reshape(blocks), slot_gate, cot_all, full_experts
    )
    sum_experts = lax.psum_scatter(grad_experts, "dp", scatter_dimension=0, tiled=True)

    grad_output = cotangent.astype(F32)
    out_ret = out_ret.reshape(EXPERT_COUNT * SLOTS, MODEL_WIDTH)
    grad_ret = grad_ret.reshape(EXPERT_COUNT * SLOTS, MODEL_WIDTH)
    rows_out = [dot(hit[k].astype(BF), out_ret, ((1,), (0,))) for k in range(2)]
    block_out = (middle + gates[:, 0:1] * rows_out[0] + gates[:, 1:2] * rows_out[1]).astype(BF)
    grad_pair = jnp.stack([jnp.sum(grad_output * rows, axis=-1) for rows in rows_out], axis=-1)
    grad_pick = gates * (grad_pair - jnp.sum(gates * grad_pair, axis=-1, keepdims=True))
    grad_logits = jnp.sum(chosen * grad_pick[:, :, None], axis=1)
    grad_moe_in = dot(both, grad_ret, ((1,), (0,))) + lax.dot_general(
        grad_logits, router.astype(F32), (((1,), (1,)), ((), ())), precision=HIGH_PRECISION
    )
    g_router = column_sums(moe_in.astype(F32), jnp.pad(grad_logits, ((0, 0), (0, EXTRA - EXPERT_COUNT))))
    g_gain_m = column_sums(grad_moe_in * middle * inverse_m, only_column(ROWS, EXPERT_COUNT + 1))
    grad_middle = grad_output + norm_backward(middle, inverse_m, gain_m, grad_moe_in)
    branch = grad_middle.astype(BF)
    own_heads = dot(branch, half_out, ((1,), (0,))).astype(BF)
    other_heads = dot(branch, sib_out, ((1,), (0,))).astype(BF)
    grad_heads = jnp.stack(
        [jnp.where(c == 0, own_heads, other_heads), jnp.where(c == 0, other_heads, own_heads)]
    )
    grad_heads = grad_heads.reshape(2, ROWS, 4, HEAD_Q).transpose(2, 0, 1, 3)
    dq_in, dkv_in, sum_out = attend_back(
        grad_heads.reshape(8, ROWS, HEAD_Q), branch, own_attn, other_attn, q_in, kv_in, first,
        attn_t, lse,
    )
    grad_q = dq_in.transpose(1, 0, 2).reshape(PAIR, Q_HALF)
    grad_kv = jnp.sum(dkv_in.reshape(4, 4, PAIR, 128).astype(F32), axis=1).astype(BF)
    grad_kv = grad_kv.transpose(1, 0, 2).reshape(PAIR, KV_HALF)

    part_normed = dot(grad_q, full_q, ((1,), (1,))) + dot(
        grad_kv, full_kv, ((1,), (1,))
    )
    g_gain_a = column_sums(part_normed * inputs2 * inverse_a, only_column(PAIR, EXPERT_COUNT))
    g_query = dot(normed, grad_q, ((0,), (0,))).astype(BF)
    g_kv = dot(normed, grad_kv, ((0,), (0,))).astype(BF)
    g_extra = (g_router + g_gain_m + g_gain_a).astype(BF)
    by_core = part_normed.reshape(2, ROWS, MODEL_WIDTH)
    own_part = lax.dynamic_index_in_dim(by_core, c, 0, keepdims=False)
    other_part = lax.dynamic_index_in_dim(by_core, 1 - c, 0, keepdims=False)
    reduced, sib_part = reduce_weights(g_query, g_kv, g_extra, sum_out, other_part)
    grad_normed = own_part + sib_part
    grad_tokens = grad_middle + norm_backward(
        inputs, inverse_rms(inputs), gain_a, grad_normed
    )
    reduced = reduced[:, :12]
    r_query = reduced[:, :, :Q_HALF].transpose(1, 0, 2).reshape(12, HEADS * HD)
    r_kv = reduced[:, :, Q_HALF : Q_HALF + KV_HALF].transpose(1, 0, 2).reshape(12, KV, 2, HD)
    r_out = reduced[:, :, STARTS[2] : STARTS[3]].transpose(1, 0, 2).reshape(12, HEADS * HD)
    r_extra = jnp.sum(reduced[:, :, STARTS[3] :], axis=0)
    return (
        block_out,
        grad_tokens,
        r_query,
        r_kv[:, :, 0].reshape(12, KV * HD),
        r_kv[:, :, 1].reshape(12, KV * HD),
        r_out.T,
        r_extra[:, :EXPERT_COUNT],
        r_extra[:, EXPERT_COUNT],
        r_extra[:, EXPERT_COUNT + 1],
        sum_experts[:, :width].astype(F32),
        sum_experts[:, width : 2 * width].astype(F32),
        sum_experts[:, 2 * width :].astype(F32).T,
    )


def solution(mesh):
    rows, flat, dense = P(("dp", "ctx"), None), P(("dp", "ctx")), P("dp", "ctx")
    placed = (
        rows, dense, rows, rows, rows, rows, P(None, ("dp", "ctx")), rows, flat, flat,
        dense, dense, P("ctx", "dp"), rows,
    )
    return jax.shard_map(
        local,
        mesh=mesh,
        in_specs=placed,
        out_specs=(
            rows, rows, rows, rows, rows, P(None, ("dp", "ctx")), rows, flat, flat,
            dense, dense, P("ctx", "dp"),
        ),
        check_vma=False,
    )
```

time: 406 us -> 382 us (0.941)
  Pallas kernels: 306 us -> 285 us
  matrix products: 31.4 us -> 25.8 us
    pallas_call x1, Pallas kernels: 60 us -> 38.5 us  [reduce_weights(): pl.pallas_call(reduce_kernel, out_shape=[jax.ShapeDtypeStruct((2, 16, PAC...]
    pallas_call x6 -> x2, Pallas kernels: 128 us -> 139 us  [the longest x1 81.7 us: attend_back(): pl.pallas_call(attend_back_kernel, out_shape=[jax.ShapeDtypeStruct((4, PA...]
    pallas_call x1, Pallas kernels: 51.6 us -> 43.5 us  [gather_weights(): pl.pallas_call(gather_kernel, out_shape=[jax.ShapeDtypeStruct((4, 4, 4, 2...]
    convert_element_type x3 -> x0, other arithmetic: 4.87 us -> none  [the longest x1 1.97 us: local(): lax.psum_scatter(grad_w_gate, 'dp', scatter_dimension=0, tiled=True)]
    dot_general x20 -> x18, matrix products: 25.2 us -> 20.5 us  [dot(): return lax.dot_general(a, b, (dims, ((), ())), preferred_element_type=F32)]
    unnamed x109, local copies, waits for them, and re-layouts: 15.3 us -> 11.1 us
  transfers between devices with their start and end apart: 6 -> 2, of which waited for: 0 -> 0; matrix products, arithmetic and copies ran while one was open for 15% -> 15% of each run, Pallas kernels for 46% -> 47%
where the time goes in v3:
time: 382 us; the launch traced here: 379 us
  Pallas kernels  285 us (75%)
  local copies, waits for them, and re-layouts  33.6 us (9%)
  matrix products  25.8 us (7%)
  other arithmetic  19.4 us (5%)
  between operations  15.2 us (4%)
    pallas_call x1, Pallas kernels, attend_back(): pl.pallas_call(attend_back_kernel, out_shape=[jax.ShapeDtypeStruct((4, PA...  81.7 us
    pallas_call x1, Pallas kernels, experts(): pl.pallas_call(experts_kernel, out_shape=[back, back, jax.ShapeDtypeStruc...  63.6 us
    pallas_call x1, Pallas kernels, attend(): pl.pallas_call(attend_kernel, out_shape=[jax.ShapeDtypeStruct((4, PAIR, H...  57.3 us
    pallas_call x1, Pallas kernels, gather_weights(): pl.pallas_call(gather_kernel, out_shape=[jax.ShapeDtypeStruct((4, 4, 4, 2...  43.5 us
    pallas_call x1, Pallas kernels, reduce_weights(): pl.pallas_call(reduce_kernel, out_shape=[jax.ShapeDtypeStruct((2, 16, PAC...  38.5 us
    dot_general x18, matrix products, dot(): return lax.dot_general(a, b, (dims, ((), ())), preferred_element_type=F32)  20.5 us
    unnamed x109, local copies, waits for them, and re-layouts  11.1 us
  transfers between devices with their start and end apart: 2, of which 0 were waited for; matrix products, arithmetic and copies ran while one was open for 15% of the time, Pallas kernels for 47%

profile of v3, /device:TPU:1, one launch (start us, length us, event | category | flops | bytes accessed | tf_op | source)
XLA Modules:
  0.0 378.5 jit_solution(2807806127438537837)
XLA Ops:
  15.0 43.5 %gather_weights.1 = (bf16[4,4,4,24,768]{4,3,2,1,0:T(8,128)(2,1)}, bf16[4,4,4,24,512]{4,3,2,1,0:T(8,128)(2,1)}, bf16[4,4,4,24,768]{4,3,2,1,0:T(8,128)(2,1)}, bf16...) custom-call(bf16[2,16,2176]{2,1,0:T(8,128)(2,1)} %fusion.23.pack, ...), custom_call_target="tpu_custom_call" | custom-call | tf_op jit(solution)/shard_map/gather_weights/pallas_call | solution.py:176
  61.3 2.7 convolution_convert_fusion.4
  70.3 1.5 convolution_convert_fusion.3
  71.8 57.3 %attend.1 = (bf16[4,256,192]{2,1,0:T(8,128)(2,1)}, bf16[16,256,128]{2,1,0:T(8,128)(2,1)}, bf16[8,128,192]{2,1,0:T(8,128)(2,1)}, f32[4,64,768]{2,1,0:T(8,128)}, f...) custom-call(bf16[4,256,192]{2,1,0:T(8,128)(2,1)} %bitcast.162, ...), custom_call_target="tpu_custom_call", output_to_operand_aliasing={{5}: (2, {})} | custom-call | tf_op jit(solution)/shard_map/attend/pallas_call | solution.py:367
  129.1 1.3 copy.101
  130.6 2.7 convolution_add_fusion.5
  139.7 1.4 select_reduce_fusion
  141.1 1.4 broadcast_in_dim.35
  142.5 2.6 convolution_convert_fusion.2
  145.1 1.5 broadcast_in_dim.36.gates
  146.6 63.6 %experts.1 = (bf16[16,24,1536]{2,1,0:T(8,128)(2,1)}, bf16[16,24,1536]{2,1,0:T(8,128)(2,1)}, bf16[1536,1536]{1,0:T(8,128)(2,1)}) custom-call(bf16[16,24,1536]{2,1,0:T(8,128)(2,1)} %bitcast.152, f32[16,24,128]{2,1,0:T(8,128)} %broadcast_in_dim.36.gates, bf16[32,24,1536]{2,1,0:T(8,128)(2,1)} %get-tuple-element.46.cots, ...), custom_call_target="tpu_custom_call" | custom-call | tf_op jit(solution)/shard_map/experts/pallas_call | solution.py:561
  210.2 1.7 copy.105.own_attn
  211.9 1.7 copy.106.other_attn
  215.4 1.8 fusion.28
  222.0 1.3 copy-done.1
  225.2 81.7 %attend_back.1 = (bf16[4,256,192]{2,1,0:T(8,128)(2,1)}, bf16[16,256,128]{2,1,0:T(8,128)(2,1)}, f32[24,768]{1,0:T(8,128)}) custom-call(bf16[8,128,192]{2,1,0:T(8,128)(2,1)} %bitcast.163, bf16[128,1536]{1,0:T(8,128)(2,1)} %copy-done.12, bf16[128,768]{1,0:T(8,128)(2,1)} %copy.105.own_attn, bf16[128,768]{1,0:T(8,128)(2,1)} %copy.106.other_attn, ...), custom_call_target="tpu_custom_call" | custom-call | tf_op jit(solution)/shard_map/attend_back/pallas_call | solution.py:902
  306.9 1.4 copy.107
  308.3 2.2 bitcast_reduce_fusion
  317.1 1.5 convolution_add_fusion.2
  318.6 2.6 fusion
  321.3 2.3 convolution_convert_fusion
  323.5 38.5 %reduce_weights.1 = (f32[2,16,2176]{2,1,0:T(8,128)S(1)}, f32[128,1536]{1,0:T(8,128)S(1)}) custom-call(bf16[4,4,4,24,768]{4,3,2,1,0:T(8,128)(2,1)} %bitcast.142, bf16[4,4,4,24,512]{4,3,2,1,0:T(8,128)(2,1)S(1)} %bitcast.135, bf16[4,4,4,24,128]{4,3,2,1,0:T(8,128)(2,1)S(1)} %bitcast.136, f32[24,768]{1,0:T(8,128)S(1)} %copy-done, ...), custom_call_target="tpu_custom_call" | custom-call | tf_op jit(solution)/shard_map/reduce_weights/pallas_call | solution.py:688
  366.4 1.3 fusion.7
  367.6 2.7 convert_bitcast_fusion
  (201 shorter events, 43.3 us)
Async XLA Ops:
  7.2 51.3 %copy-start.30 = (bf16[384,512]{1,0:T(8,128)(2,1)S(1)}, bf16[384,512]{1,0:T(8,128)(2,1)}, u32[]{:S(2)}) copy-start(bf16[384,512]{1,0:T(8,128)(2,1)} %param.25) | copy-start | bytes 1179652
  7.2 51.3 %copy-start.31 = (bf16[384,512]{1,0:T(8,128)(2,1)S(1)}, bf16[384,512]{1,0:T(8,128)(2,1)}, u32[]{:S(2)}) copy-start(bf16[384,512]{1,0:T(8,128)(2,1)} %param.24) | copy-start | bytes 1179652
  7.2 137.9 %all-gather.2.cloned.1.call-start = ((), (), s32[]{:S(2)}) async-start(), calls=%async_computation.1 | async-start | bytes 5898240 | tf_op jit(solution)/shard_map/all_gather | solution.py:1004
  59.6 308.0 %reduce-scatter.2.cloned.1.call-start = ((), (), s32[]{:S(2)}) async-start(), calls=%async_computation.2 | async-start | bytes 5898240 | tf_op jit(solution)/shard_map/reduce_scatter | solution.py:1065
  61.2 3.9 %copy-start.5 = (bf16[2,128,1536]{2,1,0:T(8,128)(2,1)}, bf16[2,128,1536]{2,1,0:T(8,128)(2,1)S(1)}, u32[]{:S(2)}) copy-start(bf16[2,128,1536]{2,1,0:T(8,128)(2,1)S(1)} %multiply_convert_fusion) | copy-start | bytes 2359300
  65.6 2.1 copy-start.35
  65.6 3.7 copy-start.37
  66.1 4.2 %copy-start.16 = (bf16[128,1536]{1,0:T(8,128)(2,1)S(1)}, bf16[128,1536]{1,0:T(8,128)(2,1)}, u32[]{:S(2)}) copy-start(bf16[128,1536]{1,0:T(8,128)(2,1)} %param.27) | copy-start | bytes 1179652
  69.4 59.7 %copy-start.43 = (s32[2,128]{1,0:T(2,128)}, s32[2,128]{1,0:T(2,128)S(1)}, u32[]{:S(2)}) copy-start(s32[2,128]{1,0:T(2,128)S(1)} %fusion.39) | copy-start | bytes 3076
  130.5 2.8 copy-start.24
  130.5 2.8 copy-start.23
  130.6 2.8 copy-start.2
  133.4 2.5 copy-start.19
  213.7 3.5 copy-start.13
  213.7 3.5 copy-start.15
  213.7 3.6 copy-start.17
  217.3 1.8 copy-start.29
  221.5 2.3 copy-start.12
  221.5 1.8 copy-start.1
  306.9 4.6 %copy-start.28 = (bf16[4,4,4,24,512]{4,3,2,1,0:T(8,128)(2,1)S(1)}, bf16[4,4,4,24,512]{4,3,2,1,0:T(8,128)(2,1)}, u32[]{:S(2)}) copy-start(bf16[4,4,4,24,512]{4,3,2,1,0:T(8,128)(2,1)} %get-tuple-element.40) | copy-start | bytes 4718596
  311.6 1.9 copy-start.22
  311.6 1.9 copy-start.47
  321.2 2.3 copy-start
  365.4 2.3 copy-start.34
  (29 other events, 35.8 us)
Sparse Core Ops, SparseCore 0:
  59.8 59.3 all-gather.1
  210.3 57.6 reduce-scatter.1

commit v4 on v3

--- a/solution.py
+++ b/solution.py
@@ -82,10 +82,11 @@
     (3, 0, 128, ("z", "y", "x")),
 )
 OUT_PARTS = (
-    (2, 0, 256, ("x", "z", "y")),
-    (2, 256, 256, ("y", "x", "z")),
-    (2, 512, 256, ("z", "y", "x")),
+    (2, 0, 128, ("z", "x", "y")),
+    (2, 128, 384, ("z", "y", "x")),
+    (2, 512, 256, ("y", "x", "z")),
 )
+OUT_SUMS = ((0, ("x", "y", "z")), (256, ("x", "z", "y")), (512, ("z", "x", "y")))
 GATHER_PARTS = FIRST_PARTS + OUT_PARTS
 
 
@@ -212,17 +213,11 @@
         pl.semaphore_wait(pltpu.get_barrier_semaphore(), 15)
 
 
-def wide(block, head, first):
-    part = block[:, 64 * head : 64 * head + 64]
-    zero = jnp.zeros_like(part)
-    return jnp.concatenate([part, zero] if first else [zero, part], axis=1)
-
-
 KEYS = 1024
 
 
 def attend_kernel(
-    q4, kv4, half_in, cots, first_ref, q_in, kv_in, attn, ot_ref, lse_ref, half, half_sib, c_all,
+    q4, kv2, half_in, cots, first_ref, q_in, kv_in, attn, ot_ref, lse_ref, half, half_sib, c_all,
     qs, acc, o_buf,
     l_sem, q_send, q_recv, k_send, k_recv, w_send, w_recv, sib_send, sib_recv,
     c_send, c_recv, f_send, f_recv, o_send, o_recv,
@@ -240,15 +235,18 @@
         copy.start()
         q_copies.append(copy)
 
+    def head(index):
+        return kv2.at[:, pl.ds(pl.multiple_of(index * 128, 128), 128)]
+
     def send_kv(k, carry):
         t = (me + k) % 16
-        remote(kv4.at[t // 4], kv_in.at[me], k_send, k_recv, dev(y, t // 4, t % 4, c)).start()
+        remote(head(t // 4), kv_in.at[me], k_send, k_recv, dev(y, t // 4, t % 4, c)).start()
         return carry
 
     lax.fori_loop(1, 16, send_kv, 0)
     here = [
         pltpu.make_async_copy(q4.at[z], q_in.at[z], l_sem.at[0]),
-        pltpu.make_async_copy(kv4.at[z], kv_in.at[me], l_sem.at[1]),
+        pltpu.make_async_copy(head(z), kv_in.at[me], l_sem.at[1]),
     ]
     for copy in here:
         copy.start()
@@ -260,7 +258,7 @@
     drain.wait_send()
     drain.wait_recv()
 
-    w_copies = []
+    w_copies = [[], [], []]
     for part, (n, start, width, order) in enumerate(OUT_PARTS):
         spot = slab(half, order[:2], y, z, x, pl.ds(start, width))
         for k, step in enumerate(STEPS):
@@ -268,7 +266,7 @@
                 spot, spot, w_send.at[part, k], w_recv.at[part, k], axis_peer(order[2], step)
             )
             copy.start()
-            w_copies.append(copy)
+            w_copies[part].append(copy)
 
     def send_cots(k, carry):
         t = (me + k) % 16
@@ -291,14 +289,20 @@
         arrived.wait_send()
         return carry
 
-    swap = remote(half, half_sib, sib_send, sib_recv, sibling)
-    j = z * 2 + c
+    def swap(part):
+        start, width = OUT_PARTS[part][1:3]
+        cols = half.at[:, :, :, :, pl.ds(start, width)]
+        there = half_sib.at[:, :, :, :, pl.ds(start, width)]
+        return remote(cols, there, sib_send.at[part], sib_recv.at[part], sibling)
+
+    j = c * 4 + z
+    qs[64:] = jnp.zeros((64, 3 * PAIR), BF)
     returns = []
     for n in range(4):
         zq = (z + n + 1) % 4
         q = q_in[zq] * SCALE_QK
         for h in range(3):
-            qs[256 * h : 256 * h + 256] = wide(q, h, True)
+            qs[:64, 256 * h : 256 * h + 256] = q[64 * h : 64 * h + 64]
         acc[...] = jnp.zeros_like(acc)
         first = first_ref[zq]
         q_pos = (zq * 4 + x) * PAIR + lax.broadcasted_iota(jnp.int32, (1, PAIR), 1)
@@ -307,7 +311,7 @@
             kv = kv_in[pl.ds(kb * (KEYS // PAIR), KEYS // PAIR)].reshape(KEYS, 128)
             k_pos = kb * KEYS + lax.broadcasted_iota(jnp.int32, (KEYS, PAIR), 0)
             ok = (k_pos >= first) & (k_pos <= q_pos)
-            scores = [dot(kv, qs[256 * h : 256 * h + 256], ((1,), (1,))) for h in range(3)]
+            scores = [dot(kv, qs[:, 256 * h : 256 * h + 256], ((1,), (0,))) for h in range(3)]
             later, probs, shrinks = [], [], []
             for h in range(3):
                 top, tot = stats[h]
@@ -332,10 +336,9 @@
             ot_ref[zq, :, cols] = mixed
             lse_ref[zq, :, cols] = stats[h][0] + jnp.log(stats[h][1])
             heads.append(mixed)
-        heads = jnp.concatenate(heads, axis=0)
-        rows = jnp.transpose(heads).astype(BF)
-        o_buf[n, 0] = rows[:ROWS]
-        o_buf[n, 1] = rows[ROWS:]
+        heads = jnp.concatenate(heads, axis=0).astype(BF)
+        o_buf[n, 0] = heads[:, :ROWS]
+        o_buf[n, 1] = heads[:, ROWS:]
         for d in range(2):
             core = c if d == 0 else 1 - c
             if n == 3 and d == 0:
@@ -346,30 +349,31 @@
                 )
             back.start()
             returns.append(back)
-        if n == 1:
-            for copy in w_copies:
-                copy.wait()
-            swap.start()
-        if n == 2:
+    for part in range(3):
+        for copy in w_copies[part]:
+            copy.wait()
+        swap(part).start()
+        if part == 0:
             lax.fori_loop(1, 16, forward_cots, 0)
     own_cots.wait()
     mine = c_all.at[pl.ds(c * 16, 16)]
     drain = remote(mine, mine, f_send, f_recv, sibling)
     drain.wait_send()
     drain.wait_recv()
-    swap.wait()
+    for part in range(3):
+        swap(part).wait()
     for back in returns:
         back.wait()
 
 
-def attend(q4, kv4, half, cots, first):
+def attend(q4, kv2, half, cots, first):
     blocks = jax.ShapeDtypeStruct((4, 4, 4, 24, Q_HALF), BF)
     return pl.pallas_call(
         attend_kernel,
         out_shape=[
-            jax.ShapeDtypeStruct((4, PAIR, HEAD_Q), BF),
+            jax.ShapeDtypeStruct((4, HEAD_Q, PAIR), BF),
             jax.ShapeDtypeStruct((16, PAIR, 128), BF),
-            jax.ShapeDtypeStruct((8, ROWS, HEAD_Q), BF),
+            jax.ShapeDtypeStruct((8, HEAD_Q, ROWS), BF),
             jax.ShapeDtypeStruct((4, HD, 3 * PAIR), F32),
             jax.ShapeDtypeStruct((4, 1, 3 * PAIR), F32),
             blocks,
@@ -380,9 +384,9 @@
         out_specs=[IN_VMEM, IN_VMEM, ANY, IN_VMEM, IN_VMEM, ANY, ANY, ANY],
         input_output_aliases={2: 5},
         scratch_shapes=[
-            pltpu.VMEM((3 * PAIR, 128), BF),
+            pltpu.VMEM((128, 3 * PAIR), BF),
             pltpu.VMEM((128, 3 * PAIR), F32),
-            pltpu.VMEM((4, 2, ROWS, HEAD_Q), BF),
+            pltpu.VMEM((4, 2, HEAD_Q, ROWS), BF),
             pltpu.SemaphoreType.DMA((4,)),
             pltpu.SemaphoreType.DMA((3,)),
             pltpu.SemaphoreType.DMA((3,)),
@@ -390,8 +394,8 @@
             pltpu.SemaphoreType.DMA,
             pltpu.SemaphoreType.DMA((3, 3)),
             pltpu.SemaphoreType.DMA((3, 3)),
-            pltpu.SemaphoreType.DMA,
-            pltpu.SemaphoreType.DMA,
+            pltpu.SemaphoreType.DMA((3,)),
+            pltpu.SemaphoreType.DMA((3,)),
             pltpu.SemaphoreType.DMA((16,)),
             pltpu.SemaphoreType.DMA((16,)),
             pltpu.SemaphoreType.DMA,
@@ -401,7 +405,7 @@
         ],
         compiler_params=params(2, 56 << 20),
         name="attend",
-    )(q4, kv4, half, cots, first)
+    )(q4, kv2, half, cots, first)
 
 
 def flat_rows(blocks):
@@ -594,26 +598,38 @@
     )(xs, gates, cots, weights)
 
 
-def reduce_kernel(g_q, g_kv, g_extra, ready, partial, out, sib_partial, *rest):
-    parts = len(FIRST_PARTS)
-    arrive = [rest[parts * k : parts * k + parts] for k in range(3)]
-    held = [None, rest[3 * parts : 4 * parts], rest[4 * parts : 5 * parts]]
-    total, give, send, recv, sib_send, sib_recv = rest[5 * parts :]
-    grads = (g_q, g_kv, None, g_extra)
+SUMS = tuple((n, start, width, order[::-1]) for n, start, width, order in FIRST_PARTS) + tuple(
+    (2, start, 256, order) for start, order in OUT_SUMS
+)
+LATE = len(FIRST_PARTS)
+
+
+def reduce_kernel(
+    gq_t, dkv, normed, g_moe, s_out, pair, gain, grad_middle, w_q, w_kv,
+    o_tokens, o_q, o_k, o_v, o_out, o_extra,
+    v_q, v_kv, v_extra, wq, wkv, gkv, mine_part, give_part, sib_part, both, total, give, *rest,
+):
+    parts = len(SUMS)
+    first_in, rest = rest[:LATE], rest[LATE:]
+    arrive = [list(first_in) + [None] * 3, rest[:parts], rest[parts : 2 * parts]]
+    rest = rest[2 * parts :]
+    held = [None, list(rest[:LATE]) + [s_out.at[k] for k in range(3)], rest[LATE : LATE + parts]]
+    l_sem, send, recv, sib_send, sib_recv = rest[LATE + parts :]
+    grads = (v_q, v_kv, None, v_extra)
     y, z, x, c = coords()
     place = {"y": y, "z": z, "x": x}
     sibling = dev(y, z, x, 1 - c)
+    loads = [pltpu.make_async_copy(w_q, wq, l_sem.at[0]), pltpu.make_async_copy(w_kv, wkv, l_sem.at[1])]
+    for load in loads:
+        load.start()
     for axis in ("x", "y", "z"):
         for step in STEPS:
             signal(axis_peer(axis, step))
     signal(sibling)
     pl.semaphore_wait(pltpu.get_barrier_semaphore(), 10)
-    other = remote(partial, sib_partial, sib_send.at[0], sib_recv.at[0], sibling)
-    other.start()
 
     def at(phase, part, index):
-        n, start, width, order = FIRST_PARTS[part]
-        order = order[::-1]
+        n, start, width, order = SUMS[part]
         spot = [
             index if axis == order[phase] else slice(None)
             for axis in ("y", "z", "x")
@@ -623,86 +639,145 @@
             return grads[n].at[tuple(spot) + (slice(None), pl.ds(start, width))]
         return held[phase][part].at[tuple(spot)]
 
+    def copies_of(phase, part):
+        axis = SUMS[part][3][phase]
+        return [
+            remote(
+                at(phase, part, (place[axis] + step) % 4), arrive[phase][part].at[n],
+                send.at[phase, part, n], recv.at[phase, part, n], axis_peer(axis, step),
+            )
+            for n, step in enumerate(STEPS)
+        ]
+
+    def begin(phase, part):
+        for copy in copies_of(phase, part):
+            copy.start()
+
+    def finish(phase, part):
+        for copy in copies_of(phase, part):
+            copy.wait()
+        array, start, width, order = SUMS[part]
+        mine = at(phase, part, place[order[phase]])
+        got = arrive[phase][part]
+        if phase < 2:
+
+            def add(p, carry):
+                value = mine[p].astype(F32)
+                for n in range(3):
+                    value = value + got[n, p].astype(F32)
+                held[phase + 1][part][p] = value.astype(BF)
+                return carry
+
+            lax.fori_loop(0, 4, add, 0)
+        else:
+            value = mine[...].astype(F32)
+            for n in range(3):
+                value = value + got[n].astype(F32)
+            total[:, STARTS[array] + start : STARTS[array] + start + width] = value
+
+    for part in range(LATE, parts):
+        begin(1, part)
+    for h in range(4):
+        value = dkv[4 * h].astype(F32)
+        for n in range(1, 4):
+            value = value + dkv[4 * h + n].astype(F32)
+        gkv[:, 128 * h : 128 * h + 128] = value.astype(BF)
+    for n in range(4):
+        left = normed[:, 384 * n : 384 * n + 384]
+        v_q[n] = dot(left, gq_t[...], ((0,), (1,))).astype(BF).reshape(4, 4, 24, Q_HALF)
+        v_kv[n] = dot(left, gkv[...], ((0,), (0,))).astype(BF).reshape(4, 4, 24, KV_HALF)
+    for part in range(3):
+        begin(0, part)
+
+    for load in loads:
+        load.wait()
+    gain_sum = jnp.zeros((1, MODEL_WIDTH), F32)
+    for n in range(2):
+        core = 1 - c if n == 0 else c
+        rows = pl.ds(pl.multiple_of(core * ROWS, ROWS), ROWS)
+        part = dot(gq_t[:, rows], wq[...], ((0,), (1,))) + dot(gkv[rows], wkv[...], ((1,), (1,)))
+        values = pair[rows].astype(F32)
+        gain_sum = gain_sum + jnp.sum(part * values * inverse_rms(values), axis=0, keepdims=True)
+        if n == 0:
+            give_part[...] = part
+            remote(give_part, sib_part, sib_send.at[0], sib_recv.at[0], sibling).start()
+        else:
+            mine_part[...] = part
+    column = jnp.transpose(jnp.broadcast_to(gain_sum, (EXTRA, MODEL_WIDTH)))
+    lane = lax.broadcasted_iota(jnp.int32, (MODEL_WIDTH, EXTRA), 1)
+    extra = g_moe[...] + jnp.where(lane == EXPERT_COUNT, column, 0.0)
+    v_extra[...] = extra.astype(BF).reshape(4, 4, 4, 24, EXTRA)
+    begin(0, 3)
+    remote(give_part, sib_part, sib_send.at[0], sib_recv.at[0], sibling).wait()
+    rows = pl.ds(pl.multiple_of(c * ROWS, ROWS), ROWS)
+    values = pair[rows].astype(F32)
+    o_tokens[...] = grad_middle[...] + norm_backward(
+        values, inverse_rms(values), gain[...], mine_part[...] + sib_part[...]
+    )
+
+    for part in range(LATE, parts):
+        finish(1, part)
+        begin(2, part)
     for phase in range(3):
-        copies = []
-        for part in range(parts):
-            axis = FIRST_PARTS[part][3][::-1][phase]
-            for n, step in enumerate(STEPS):
-                copy = remote(
-                    at(phase, part, (place[axis] + step) % 4),
-                    arrive[phase][part].at[n],
-                    send.at[phase, part, n],
-                    recv.at[phase, part, n],
-                    axis_peer(axis, step),
-                )
-                copy.start()
-                copies.append(copy)
-        for copy in copies:
-            copy.wait()
-        for part in range(parts):
-            array, start, width, order = FIRST_PARTS[part]
-            mine = at(phase, part, place[order[::-1][phase]])
-            got = arrive[phase][part]
+        for part in range(LATE):
+            finish(phase, part)
             if phase < 2:
-
-                def add(p, carry):
-                    value = mine[p].astype(F32)
-                    for n in range(3):
-                        value = value + got[n, p].astype(F32)
-                    held[phase + 1][part][p] = value.astype(BF)
-                    return carry
-
-                lax.fori_loop(0, 4, add, 0)
-            else:
-                value = mine[...].astype(F32)
-                for n in range(3):
-                    value = value + got[n].astype(F32)
-                total[:, STARTS[array] + start : STARTS[array] + start + width] = value
-    total[:, STARTS[2] : STARTS[3]] = ready[...]
+                begin(phase + 1, part)
+    for part in range(LATE, parts):
+        finish(2, part)
     low, high = total[0:12], total[12:24]
-    out[c, 0:12] = jnp.where(c == 0, low, high)
-    out[c, 12:16] = jnp.zeros((4, PACK), F32)
+    both[c, 0:12] = jnp.where(c == 0, low, high)
     give[0:12] = jnp.where(c == 0, high, low)
     give[12:16] = jnp.zeros((4, PACK), F32)
-    last = remote(give, out.at[c], sib_send.at[1], sib_recv.at[1], sibling)
+    last = remote(give, both.at[c], sib_send.at[1], sib_recv.at[1], sibling)
     last.start()
     last.wait()
-    other.wait()
-
-
-def place_blocks(full):
-    return full.reshape(4, 4, 4, 24, full.shape[-1])
-
-
-def reduce_weights(g_q, g_kv, g_extra, ready, partial):
-    widths = [part[2] for part in FIRST_PARTS]
+    keys, values = [], []
+    for k in range(2):
+        o_q[:, Q_HALF * k : Q_HALF * k + Q_HALF] = both[k, 0:12, :Q_HALF]
+        o_out[:, Q_HALF * k : Q_HALF * k + Q_HALF] = both[k, 0:12, STARTS[2] : STARTS[3]]
+        for h in range(4):
+            first = STARTS[1] + 128 * h
+            keys.append(both[k, 0:12, first : first + HD])
+            values.append(both[k, 0:12, first + HD : first + 2 * HD])
+    o_k[...] = jnp.concatenate(keys, axis=1)
+    o_v[...] = jnp.concatenate(values, axis=1)
+    o_extra[...] = both[0, 0:12, STARTS[3] :] + both[1, 0:12, STARTS[3] :]
+
+
+def reduce_weights(gq_t, dkv, normed, g_moe, s_out, pair, gain, grad_middle, w_q, w_kv):
+    widths = [part[2] for part in SUMS]
+    full = lambda width: pltpu.VMEM((4, 4, 4, 24, width), BF)
+    rows = pltpu.VMEM((ROWS, MODEL_WIDTH), F32)
     scratch = (
-        [pltpu.VMEM((3, 4, 4, 24, w), BF) for w in widths]
+        [full(Q_HALF), full(KV_HALF), full(EXTRA)]
+        + [pltpu.VMEM((MODEL_WIDTH, Q_HALF), BF), pltpu.VMEM((MODEL_WIDTH, KV_HALF), BF)]
+        + [pltpu.VMEM((PAIR, KV_HALF), BF), rows, rows, rows]
+        + [pltpu.VMEM((2, 16, PACK), F32), pltpu.VMEM((24, PACK), F32), pltpu.VMEM((16, PACK), F32)]
+        + [pltpu.VMEM((3, 4, 4, 24, w), BF) for w in widths[:LATE]]
         + [pltpu.VMEM((3, 4, 24, w), BF) for w in widths]
         + [pltpu.VMEM((3, 24, w), BF) for w in widths]
-        + [pltpu.VMEM((4, 4, 24, w), BF) for w in widths]
+        + [pltpu.VMEM((4, 4, 24, w), BF) for w in widths[:LATE]]
         + [pltpu.VMEM((4, 24, w), BF) for w in widths]
-        + [pltpu.VMEM((24, PACK), F32), pltpu.VMEM((16, PACK), F32)]
-    )
-    sems = (3, len(FIRST_PARTS), 3)
+    )
+    sems = (3, len(SUMS), 3)
+    shapes = ((ROWS, MODEL_WIDTH), (12, MODEL_WIDTH), (12, KV * HD), (12, KV * HD), (12, MODEL_WIDTH), (12, EXTRA))
     return pl.pallas_call(
         reduce_kernel,
-        out_shape=[
-            jax.ShapeDtypeStruct((2, 16, PACK), F32),
-            jax.ShapeDtypeStruct((ROWS, MODEL_WIDTH), F32),
-        ],
-        in_specs=[IN_VMEM] * 4 + [ANY],
-        out_specs=[IN_VMEM, ANY],
+        out_shape=[jax.ShapeDtypeStruct(shape, F32) for shape in shapes],
+        in_specs=[IN_VMEM] * 8 + [ANY] * 2,
+        out_specs=[IN_VMEM] * 6,
         scratch_shapes=scratch
         + [
+            pltpu.SemaphoreType.DMA((2,)),
             pltpu.SemaphoreType.DMA(sems),
             pltpu.SemaphoreType.DMA(sems),
             pltpu.SemaphoreType.DMA((2,)),
             pltpu.SemaphoreType.DMA((2,)),
         ],
-        compiler_params=params(8, 48 << 20),
+        compiler_params=params(8, 58 << 20),
         name="reduce_weights",
-    )(place_blocks(g_q), place_blocks(g_kv), place_blocks(g_extra), ready, partial)
+    )(gq_t, dkv, normed, g_moe, s_out, pair, gain, grad_middle, w_q, w_kv)
 
 
 def wide_greet():
@@ -724,22 +799,22 @@
 
 def attend_back_kernel(
     heads, branch, own_attn, other_attn, q_in, kv_in, first_ref, ot_ref, lse_ref,
-    dq_out, dkv_out, total,
+    dq_out, dkv_out, s_out,
     go, branch_sib, attn_sib, qs, gs, dq, dkv, dkv_low, dq_low,
-    g_out, s_out, t_out, a_out, b_out, c_out,
+    g_out, a_out,
     l_sem, h_send, h_recv, sib_send, sib_recv, q_send, q_recv, k_send, k_recv,
     w_send, w_recv,
 ):
     y, z, x, c = coords()
     me = z * 4 + x
-    j = z * 2 + c
+    j = c * 4 + z
     sibling = dev(y, z, x, 1 - c)
     place = {"y": y, "z": z, "x": x}
     wide_greet()
 
     def push(k, carry):
         t = (j + k) % 8
-        remote(heads.at[t], go.at[j], h_send, h_recv, dev(y, t // 2, x, t % 2)).start()
+        remote(heads.at[t], go.at[j], h_send, h_recv, dev(y, t % 4, x, t // 4)).start()
         return carry
 
     lax.fori_loop(1, 8, push, 0)
@@ -757,77 +832,42 @@
     two.wait()
 
     rows_b = jnp.concatenate([branch[...], branch_sib[...]], axis=0)
-    rows_a = jnp.concatenate([own_attn[...], attn_sib[...]], axis=0)
+    rows_a = jnp.concatenate([own_attn[...], attn_sib[...]], axis=1)
     for n in range(4):
-        part = dot(rows_b[:, 384 * n : 384 * n + 384], rows_a, ((0,), (0,)))
+        part = dot(rows_b[:, 384 * n : 384 * n + 384], rows_a, ((0,), (1,)))
         g_out[n] = part.astype(BF).reshape(4, 4, 24, Q_HALF)
 
-    held = (g_out, s_out, t_out)
-    arrive = (a_out, b_out, c_out)
-
-    def spot(phase, part, index):
-        n, start, width, order = OUT_PARTS[part]
-        order = order[::-1]
-        cut = [
-            index if axis == order[phase] else slice(None)
-            for axis in ("y", "z", "x")
-            if axis not in order[:phase]
-        ]
-        if phase == 0:
-            return held[0].at[tuple(cut) + (slice(None), pl.ds(start, width))]
-        return held[phase].at[(part,) + tuple(cut)]
-
-    def w_copies(phase):
-        copies = []
-        for part in range(3):
-            axis = OUT_PARTS[part][3][::-1][phase]
-            for n, step in enumerate(STEPS):
-                copies.append(
-                    remote(
-                        spot(phase, part, (place[axis] + step) % 4), arrive[phase].at[part, n],
-                        w_send.at[phase, part, n], w_recv.at[phase, part, n], axis_peer(axis, step),
-                    )
-                )
-        return copies
-
-    def w_sum(phase):
-        for copy in w_copies(phase):
-            copy.wait()
-        for part in range(3):
-            n, start, width, order = OUT_PARTS[part]
-            mine = spot(phase, part, place[order[::-1][phase]])
-            if phase == 2:
-                value = mine[...].astype(F32)
-                for k in range(3):
-                    value = value + arrive[2][part, k].astype(F32)
-                total[:, start : start + width] = value
-            else:
-
-                def add(p, carry):
-                    value = mine[p].astype(F32)
-                    for k in range(3):
-                        value = value + arrive[phase][part, k, p].astype(F32)
-                    held[phase + 1][part, p] = value.astype(BF)
-                    return carry
-
-                lax.fori_loop(0, 4, add, 0)
-
-    for copy in w_copies(0):
-        copy.start()
+    def spot(part, index):
+        start, order = OUT_SUMS[part]
+        cut = [index if axis == order[0] else slice(None) for axis in ("y", "z", "x")]
+        return g_out.at[tuple(cut) + (slice(None), pl.ds(start, 256))]
+
+    w_copies = []
+    for part in range(3):
+        axis = OUT_SUMS[part][1][0]
+        for n, step in enumerate(STEPS):
+            copy = remote(
+                spot(part, (place[axis] + step) % 4), a_out.at[part, n],
+                w_send.at[part, n], w_recv.at[part, n], axis_peer(axis, step),
+            )
+            copy.start()
+            w_copies.append(copy)
 
     dkv[...] = jnp.zeros_like(dkv)
+    qs[64:] = jnp.zeros((64, 3 * PAIR), BF)
+    gs[:64] = jnp.zeros((64, 3 * PAIR), BF)
     for n in range(4):
         zq = 3 - n
         q = q_in[zq] * SCALE_QK
-        grad = jnp.concatenate([go[2 * zq], go[2 * zq + 1]], axis=0)
-        grad_t = jnp.transpose(grad.astype(F32))
+        grad = jnp.concatenate([go[zq], go[4 + zq]], axis=1)
         deltas, sums_log = [], []
         for h in range(3):
             cols = slice(256 * h, 256 * h + 256)
-            qs[cols] = wide(q, h, True)
-            gs[cols] = wide(grad, h, False)
+            rows = slice(64 * h, 64 * h + 64)
+            qs[:64, cols] = q[rows]
+            gs[64:, cols] = grad[rows]
             deltas.append(
-                jnp.sum(grad_t[64 * h : 64 * h + 64] * ot_ref[zq, :, cols], axis=0, keepdims=True)
+                jnp.sum(grad[rows].astype(F32) * ot_ref[zq, :, cols], axis=0, keepdims=True)
             )
             sums_log.append(lse_ref[zq, :, cols])
         dq[...] = jnp.zeros_like(dq)
@@ -839,8 +879,8 @@
             kv = kv_in[kb]
             k_pos = kb * PAIR + lax.broadcasted_iota(jnp.int32, (PAIR, PAIR), 0)
             ok = (k_pos >= first) & (k_pos <= q_pos)
-            scores = [dot(kv, qs[256 * h : 256 * h + 256], ((1,), (1,))) for h in range(3)]
-            grad_probs = [dot(kv, gs[256 * h : 256 * h + 256], ((1,), (1,))) for h in range(3)]
+            scores = [dot(kv, qs[:, 256 * h : 256 * h + 256], ((1,), (0,))) for h in range(3)]
+            grad_probs = [dot(kv, gs[:, 256 * h : 256 * h + 256], ((1,), (0,))) for h in range(3)]
             grad_scores, probs = [], []
             for h in range(3):
                 prob = jnp.where(ok, jnp.exp(scores[h] - sums_log[h]), 0.0)
@@ -851,14 +891,14 @@
                 dq[:, cols] = dq[:, cols] + dot(kv, grad_scores[h], ((0,), (0,)))
             dkv[kb] = (
                 dkv[kb]
-                + dot(jnp.concatenate(grad_scores, axis=1), qs[...], ((1,), (0,)))
-                + dot(jnp.concatenate(probs, axis=1), gs[...], ((1,), (0,)))
+                + dot(jnp.concatenate(grad_scores, axis=1), qs[...], ((1,), (1,)))
+                + dot(jnp.concatenate(probs, axis=1), gs[...], ((1,), (1,)))
             )
             return carry
 
         lax.fori_loop(0, hi + 1, step, 0)
         by_head = jnp.concatenate([dq[:64, 256 * h : 256 * h + 256] for h in range(3)], axis=0)
-        dq_low[zq] = jnp.transpose(by_head * SCALE_QK).astype(BF)
+        dq_low[zq] = (by_head * SCALE_QK).astype(BF)
         away = (zq - z + 4) % 4
 
         @pl.when(away != 0)
@@ -881,12 +921,20 @@
             def _():
                 pltpu.make_async_copy(dkv_low.at[t], dkv_out.at[me], l_sem.at[2]).start()
 
-        if n in (1, 2):
-            w_sum(n - 1)
-            for copy in w_copies(n):
-                copy.start()
-
-    w_sum(2)
+
+    for copy in w_copies:
+        copy.wait()
+    for part in range(3):
+        mine = spot(part, place[OUT_SUMS[part][1][0]])
+
+        def add(p, carry):
+            value = mine[p].astype(F32)
+            for k in range(3):
+                value = value + a_out[part, k, p].astype(F32)
+            s_out[part, p] = value.astype(BF)
+            return carry
+
+        lax.fori_loop(0, 4, add, 0)
     pltpu.make_async_copy(dq_low.at[z], dq_out.at[z], l_sem.at[1]).wait()
     pltpu.make_async_copy(dkv_low.at[me], dkv_out.at[me], l_sem.at[2]).wait()
     for k in range(1, 4):
@@ -902,28 +950,24 @@
     return pl.pallas_call(
         attend_back_kernel,
         out_shape=[
-            jax.ShapeDtypeStruct((4, PAIR, HEAD_Q), BF),
+            jax.ShapeDtypeStruct((4, HEAD_Q, PAIR), BF),
             jax.ShapeDtypeStruct((16, PAIR, 128), BF),
-            jax.ShapeDtypeStruct((24, Q_HALF), F32),
+            jax.ShapeDtypeStruct((3, 4, 4, 24, 256), BF),
         ],
         in_specs=[ANY] + [IN_VMEM] * 8,
         out_specs=[ANY, ANY, IN_VMEM],
         scratch_shapes=[
-            pltpu.VMEM((8, ROWS, HEAD_Q), BF),
+            pltpu.VMEM((8, HEAD_Q, ROWS), BF),
             pltpu.VMEM((ROWS, MODEL_WIDTH), BF),
-            pltpu.VMEM((ROWS, Q_HALF), BF),
-            pltpu.VMEM((3 * PAIR, 128), BF),
-            pltpu.VMEM((3 * PAIR, 128), BF),
+            pltpu.VMEM((Q_HALF, ROWS), BF),
+            pltpu.VMEM((128, 3 * PAIR), BF),
+            pltpu.VMEM((128, 3 * PAIR), BF),
             pltpu.VMEM((128, 3 * PAIR), F32),
             pltpu.VMEM((16, PAIR, 128), F32),
             pltpu.VMEM((16, PAIR, 128), BF),
-            pltpu.VMEM((4, PAIR, HEAD_Q), BF),
+            pltpu.VMEM((4, HEAD_Q, PAIR), BF),
             pltpu.VMEM((4, 4, 4, 24, Q_HALF), BF),
-            pltpu.VMEM((3, 4, 4, 24, 256), BF),
-            pltpu.VMEM((3, 4, 24, 256), BF),
             pltpu.VMEM((3, 3, 4, 4, 24, 256), BF),
-            pltpu.VMEM((3, 3, 4, 24, 256), BF),
-            pltpu.VMEM((3, 3, 24, 256), BF),
             pltpu.SemaphoreType.DMA((3,)),
             pltpu.SemaphoreType.DMA,
             pltpu.SemaphoreType.DMA,
@@ -933,8 +977,8 @@
             pltpu.SemaphoreType.DMA((4,)),
             pltpu.SemaphoreType.DMA,
             pltpu.SemaphoreType.DMA,
-            pltpu.SemaphoreType.DMA((3, 3, 3)),
-            pltpu.SemaphoreType.DMA((3, 3, 3)),
+            pltpu.SemaphoreType.DMA((3, 3)),
+            pltpu.SemaphoreType.DMA((3, 3)),
         ],
         compiler_params=params(4, 58 << 20),
         name="attend_back",
@@ -1013,10 +1057,8 @@
     inputs2 = pair.reshape(PAIR, MODEL_WIDTH).astype(F32)
     inverse_a = inverse_rms(inputs2)
     normed = (inputs2 * inverse_a * gain_a).astype(BF)
-    queries = dot(normed, full_q, ((1,), (0,))).astype(BF)
+    q4 = dot(full_q, normed, ((0,), (1,))).astype(BF).reshape(4, HEAD_Q, PAIR)
     keys_values = dot(normed, full_kv, ((1,), (0,))).astype(BF)
-    q4 = queries.reshape(PAIR, 4, HEAD_Q).transpose(1, 0, 2)
-    kv4 = keys_values.reshape(PAIR, 4, 128).transpose(1, 0, 2)
     segs = seg_all.reshape(1, 4096)
     counts = jnp.sum((segs < jnp.arange(16)[:, None]).astype(jnp.int32), axis=1)
     row_segs = lax.dynamic_index_in_dim(seg_all.reshape(4, 4, PAIR), x, 1, keepdims=False)
@@ -1037,19 +1079,19 @@
     blocks = (EXPERT_COUNT, SLOTS, MODEL_WIDTH)
     cot_slots = dot(both, cotangent, ((0,), (0,))).astype(BF)
     q_in, kv_in, attn, attn_t, lse, half_out, sib_out, cot_all = attend(
-        q4, kv4, part_out, cot_slots.reshape(blocks), first
+        q4, keys_values, part_out, cot_slots.reshape(blocks), first
     )
     half_out = half_out.reshape(MODEL_WIDTH, Q_HALF)
     sib_out = sib_out.reshape(MODEL_WIDTH, Q_HALF)
-    attn = attn.reshape(4, 2, ROWS, HEAD_Q).transpose(1, 2, 0, 3).reshape(2, ROWS, Q_HALF)
+    attn = attn.reshape(2, Q_HALF, ROWS)
 
     own_attn = jnp.where(c == 0, attn[0], attn[1])
     other_attn = jnp.where(c == 0, attn[1], attn[0])
     inputs = tokens.astype(F32)
     middle = (
         inputs
-        + dot(own_attn, half_out, ((1,), (1,)))
-        + dot(other_attn, sib_out, ((1,), (1,)))
+        + dot(own_attn, half_out, ((0,), (1,)))
+        + dot(other_attn, sib_out, ((0,), (1,)))
     )
     inverse_m = inverse_rms(middle)
     moe_in = (middle * inverse_m * gain_m).astype(BF)
@@ -1079,46 +1121,25 @@
     g_gain_m = column_sums(grad_moe_in * middle * inverse_m, only_column(ROWS, EXPERT_COUNT + 1))
     grad_middle = grad_output + norm_backward(middle, inverse_m, gain_m, grad_moe_in)
     branch = grad_middle.astype(BF)
-    own_heads = dot(branch, half_out, ((1,), (0,))).astype(BF)
-    other_heads = dot(branch, sib_out, ((1,), (0,))).astype(BF)
+    own_heads = dot(half_out, branch, ((0,), (1,))).astype(BF)
+    other_heads = dot(sib_out, branch, ((0,), (1,))).astype(BF)
     grad_heads = jnp.stack(
         [jnp.where(c == 0, own_heads, other_heads), jnp.where(c == 0, other_heads, own_heads)]
     )
-    grad_heads = grad_heads.reshape(2, ROWS, 4, HEAD_Q).transpose(2, 0, 1, 3)
     dq_in, dkv_in, sum_out = attend_back(
-        grad_heads.reshape(8, ROWS, HEAD_Q), branch, own_attn, other_attn, q_in, kv_in, first,
+        grad_heads.reshape(8, HEAD_Q, ROWS), branch, own_attn, other_attn, q_in, kv_in, first,
         attn_t, lse,
     )
-    grad_q = dq_in.transpose(1, 0, 2).reshape(PAIR, Q_HALF)
-    grad_kv = jnp.sum(dkv_in.reshape(4, 4, PAIR, 128).astype(F32), axis=1).astype(BF)
-    grad_kv = grad_kv.transpose(1, 0, 2).reshape(PAIR, KV_HALF)
-
-    part_normed = dot(grad_q, full_q, ((1,), (1,))) + dot(
-        grad_kv, full_kv, ((1,), (1,))
-    )
-    g_gain_a = column_sums(part_normed * inputs2 * inverse_a, only_column(PAIR, EXPERT_COUNT))
-    g_query = dot(normed, grad_q, ((0,), (0,))).astype(BF)
-    g_kv = dot(normed, grad_kv, ((0,), (0,))).astype(BF)
-    g_extra = (g_router + g_gain_m + g_gain_a).astype(BF)
-    by_core = part_normed.reshape(2, ROWS, MODEL_WIDTH)
-    own_part = lax.dynamic_index_in_dim(by_core, c, 0, keepdims=False)
-    other_part = lax.dynamic_index_in_dim(by_core, 1 - c, 0, keepdims=False)
-    reduced, sib_part = reduce_weights(g_query, g_kv, g_extra, sum_out, other_part)
-    grad_normed = own_part + sib_part
-    grad_tokens = grad_middle + norm_backward(
-        inputs, inverse_rms(inputs), gain_a, grad_normed
-    )
-    reduced = reduced[:, :12]
-    r_query = reduced[:, :, :Q_HALF].transpose(1, 0, 2).reshape(12, HEADS * HD)
-    r_kv = reduced[:, :, Q_HALF : Q_HALF + KV_HALF].transpose(1, 0, 2).reshape(12, KV, 2, HD)
-    r_out = reduced[:, :, STARTS[2] : STARTS[3]].transpose(1, 0, 2).reshape(12, HEADS * HD)
-    r_extra = jnp.sum(reduced[:, :, STARTS[3] :], axis=0)
+    grad_tokens, r_query, r_key, r_value, r_out, r_extra = reduce_weights(
+        dq_in.reshape(Q_HALF, PAIR), dkv_in, normed, g_router + g_gain_m, sum_out,
+        pair.reshape(PAIR, MODEL_WIDTH), gain_a, grad_middle, full_q, full_kv,
+    )
     return (
         block_out,
         grad_tokens,
         r_query,
-        r_kv[:, :, 0].reshape(12, KV * HD),
-        r_kv[:, :, 1].reshape(12, KV * HD),
+        r_key,
+        r_value,
         r_out.T,
         r_extra[:, :EXPERT_COUNT],
         r_extra[:, EXPERT_COUNT],

time: 382 us -> 330 us (0.86)
  Pallas kernels: 285 us -> 267 us
  local copies, waits for them, and re-layouts: 33.6 us -> 18.4 us
  matrix products: 25.8 us -> 17.4 us
  other arithmetic: 19.4 us -> 11.5 us
    pallas_call x3, Pallas kernels: 177 us -> 161 us  [the longest x1 60.5 us: attend_back(): pl.pallas_call(attend_back_kernel, out_shape=[jax.ShapeDtypeStruct((4, HE...]
    dot_general x18 -> x14, matrix products: 20.5 us -> 13.8 us  [dot(): return lax.dot_general(a, b, (dims, ((), ())), preferred_element_type=F32)]
    unnamed x109 -> x61, local copies, waits for them, and re-layouts: 11.1 us -> 9.34 us
  transfers between devices with their start and end apart: 2 -> 2, of which waited for: 0 -> 0; matrix products, arithmetic and copies ran while one was open for 15% -> 8% of each run, Pallas kernels for 47% -> 49%
where the time goes in v4:
time: 330 us
  Pallas kernels  267 us (81%)
  local copies, waits for them, and re-layouts  18.4 us (6%)
  matrix products  17.4 us (5%)
  between operations  14.6 us (4%)
  other arithmetic  11.5 us (3%)
    pallas_call x1, Pallas kernels, experts(): pl.pallas_call(experts_kernel, out_shape=[back, back, jax.ShapeDtypeStruc...  62.8 us
    pallas_call x1, Pallas kernels, attend_back(): pl.pallas_call(attend_back_kernel, out_shape=[jax.ShapeDtypeStruct((4, HE...  60.5 us
    pallas_call x1, Pallas kernels, attend(): pl.pallas_call(attend_kernel, out_shape=[jax.ShapeDtypeStruct((4, HEAD_Q,...  56.6 us
    pallas_call x1, Pallas kernels, reduce_weights(): pl.pallas_call(reduce_kernel, out_shape=[jax.ShapeDtypeStruct(shape, F32)...  44.1 us
    pallas_call x1, Pallas kernels, gather_weights(): pl.pallas_call(gather_kernel, out_shape=[jax.ShapeDtypeStruct((4, 4, 4, 2...  43.5 us
    dot_general x14, matrix products, dot(): return lax.dot_general(a, b, (dims, ((), ())), preferred_element_type=F32)  13.8 us
    unnamed x61, local copies, waits for them, and re-layouts  9.34 us
  transfers between devices with their start and end apart: 2, of which 0 were waited for; matrix products, arithmetic and copies ran while one was open for 8% of the time, Pallas kernels for 49%

profile of v4, /device:TPU:1, one launch (start us, length us, event | category | flops | bytes accessed | tf_op | source)
XLA Modules:
  0.0 329.5 jit_solution(16540693858048770794)
XLA Ops:
  8.8 0.8 reshape.245
  12.2 1.2 copy.53
  15.0 43.5 %gather_weights.1 = (bf16[4,4,4,24,768]{4,3,2,1,0:T(8,128)(2,1)}, bf16[4,4,4,24,512]{4,3,2,1,0:T(8,128)(2,1)}, bf16[4,4,4,24,768]{4,3,2,1,0:T(8,128)(2,1)}, bf16...) custom-call(bf16[2,16,2176]{2,1,0:T(8,128)(2,1)} %fusion.18.pack, ...), custom_call_target="tpu_custom_call" | custom-call | tf_op jit(solution)/shard_map/gather_weights/pallas_call | solution.py:177
  58.6 1.1 pad_maximum_fusion
  63.3 1.5 convolution_convert_fusion.1
  65.2 1.3 convolution_convert_fusion.3.kv2
  66.9 1.6 convolution_convert_fusion.2
  68.5 56.6 %attend.1 = (bf16[4,192,256]{2,1,0:T(8,128)(2,1)}, bf16[16,256,128]{2,1,0:T(8,128)(2,1)}, bf16[8,192,128]{2,1,0:T(8,128)(2,1)}, f32[4,64,768]{2,1,0:T(8,128)}, f...) custom-call(bf16[4,192,256]{2,1,0:T(8,128)(2,1)} %bitcast.113, ...), custom_call_target="tpu_custom_call", output_to_operand_aliasing={{5}: (2, {})} | custom-call | tf_op jit(solution)/shard_map/attend/pallas_call | solution.py:371
  125.1 1.1 broadcast_select_fusion
  126.2 2.7 convolution_add_fusion.3
  129.0 1.0 multiply_reduce_fusion.1
  130.9 1.5 convolution_convert_fusion
  133.2 62.8 %experts.1 = (bf16[16,24,1536]{2,1,0:T(8,128)(2,1)}, bf16[16,24,1536]{2,1,0:T(8,128)(2,1)}, bf16[1536,1536]{1,0:T(8,128)(2,1)}) custom-call(bf16[16,24,1536]{2,1,0:T(8,128)(2,1)} %bitcast.93, f32[16,24,128]{2,1,0:T(8,128)} %broadcast_in_dim.34.gates, bf16[32,24,1536]{2,1,0:T(8,128)(2,1)} %get-tuple-element.50.cots, ...), custom_call_target="tpu_custom_call" | custom-call | tf_op jit(solution)/shard_map/experts/pallas_call | solution.py:565
  196.0 1.1 multiply_convert_fusion.normed
  197.7 1.2 fusion.3
  200.1 1.1 fusion.38
  201.2 1.3 copy-done.7
  205.8 60.5 %attend_back.1 = (bf16[4,192,256]{2,1,0:T(8,128)(2,1)}, bf16[16,256,128]{2,1,0:T(8,128)(2,1)}, bf16[3,4,4,24,256]{4,3,2,1,0:T(8,128)(2,1)}) custom-call(bf16[8,192,128]{2,1,0:T(8,128)(2,1)} %bitcast.108, bf16[128,1536]{1,0:T(8,128)(2,1)} %copy-done.14, bf16[768,128]{1,0:T(8,128)(2,1)} %bitcast.104, bf16[768,128]{1,0:T(8,128)(2,1)} %bitcast.102, ...), custom_call_target="tpu_custom_call" | custom-call | tf_op jit(solution)/shard_map/attend_back/pallas_call | solution.py:950
  266.9 2.4 convolution_add_fusion.g_moe
  269.2 44.1 %reduce_weights.1 = (f32[128,1536]{1,0:T(8,128)}, f32[12,1536]{1,0:T(8,128)}, f32[12,512]{1,0:T(8,128)}, f32[12,512]{1,0:T(8,128)}, f32[12,1536]{1,0:T(8,128)}, /*index=5*/f32[12,128]{1,0:T(8,128)}) custom-call(bf16[768,256]{1,0:T(8,128)(2,1)} %bitcast.112, bf16[16,256,128]{2,1,0:T(8,128)(2,1)} %get-tuple-element.59.dkv, ...), custom_call_target="tpu_custom_call" | custom-call | tf_op jit(solution)/shard_map/reduce_weights/pallas_call | solution.py:765
  313.3 1.5 slice_reduce_fusion
  314.8 2.7 convert_bitcast_fusion
  317.5 1.1 copy.54
  318.7 0.9 copy.69
  (120 shorter events, 20.3 us)
Async XLA Ops:
  7.2 51.3 %copy-start.17 = (bf16[384,512]{1,0:T(8,128)(2,1)S(1)}, bf16[384,512]{1,0:T(8,128)(2,1)}, u32[]{:S(2)}) copy-start(bf16[384,512]{1,0:T(8,128)(2,1)} %param.25) | copy-start | bytes 1179652
  7.2 51.3 %copy-start.18 = (bf16[384,512]{1,0:T(8,128)(2,1)S(1)}, bf16[384,512]{1,0:T(8,128)(2,1)}, u32[]{:S(2)}) copy-start(bf16[384,512]{1,0:T(8,128)(2,1)} %param.24) | copy-start | bytes 1179652
  7.2 125.2 %all-gather.2.cloned.1.call-start = ((), (), s32[]{:S(2)}) async-start(), calls=%async_computation.1 | async-start | bytes 5898240 | tf_op jit(solution)/shard_map/all_gather | solution.py:1048
  58.5 1.8 copy-start.22
  58.5 3.3 %copy-start.25 = (s32[128,2]{0,1:T(2,128)S(1)}, s32[128,2]{0,1:T(2,128)}, u32[]{:S(2)}) copy-start(s32[128,2]{0,1:T(2,128)} %param.16) | copy-start | bytes 3076
  58.5 3.5 %copy-start = (bf16[2,128,1536]{2,1,0:T(8,128)(2,1)S(1)}, bf16[2,128,1536]{2,1,0:T(8,128)(2,1)}, u32[]{:S(2)}) copy-start(bf16[2,128,1536]{2,1,0:T(8,128)(2,1)} %get-tuple-element.42) | copy-start | bytes 2359300
  59.6 2.7 copy-start.4
  59.6 3.7 %copy-start.3 = (bf16[128,1536]{1,0:T(8,128)(2,1)S(1)}, bf16[128,1536]{1,0:T(8,128)(2,1)}, u32[]{:S(2)}) copy-start(bf16[128,1536]{1,0:T(8,128)(2,1)} %param.27) | copy-start | bytes 1179652
  59.7 255.1 %reduce-scatter.2.cloned.1.call-start = ((), (), s32[]{:S(2)}) async-start(), calls=%async_computation.2 | async-start | bytes 5898240 | tf_op jit(solution)/shard_map/reduce_scatter | solution.py:1107
  63.3 1.8 copy-start.10
  63.3 1.8 copy-start.12
  65.1 1.8 copy-start.5
  68.5 57.7 %copy-start.13 = (bf16[128,1536]{1,0:T(8,128)(2,1)S(1)}, bf16[128,1536]{1,0:T(8,128)(2,1)}, u32[]{:S(2)}) copy-start(bf16[128,1536]{1,0:T(8,128)(2,1)} %tokens.1) | copy-start | bytes 1179652
  126.2 2.8 copy-start.9
  126.2 2.8 copy-start.8
  126.2 2.8 copy-start.6
  200.1 2.5 copy-start.7
  201.2 2.1 copy-start.14
  202.5 1.7 copy-start.1
  317.5 2.1 copy-start.20
  317.5 2.7 copy-start.24
  317.5 3.3 %copy-start.23 = (f32[12,512]{1,0:T(8,128)S(1)}, f32[12,512]{1,0:T(8,128)}, u32[]{:S(2)}) copy-start(f32[12,512]{1,0:T(8,128)} %get-tuple-element.149) | copy-start | bytes 73732
  317.5 3.9 %copy-start.19 = (f32[12,1536]{1,0:T(8,128)S(1)}, f32[12,1536]{1,0:T(8,128)}, u32[]{:S(2)}) copy-start(f32[12,1536]{1,0:T(8,128)} %get-tuple-element.65) | copy-start | bytes 221188
  317.5 4.6 %copy-start.21 = (f32[12,128]{1,0:T(8,128)S(1)}, f32[12,128]{1,0:T(8,128)}, u32[]{:S(2)}) copy-start(f32[12,128]{1,0:T(8,128)} %get-tuple-element.66) | copy-start | bytes 18436
  (4 other events, 4.7 us)
Sparse Core Ops, SparseCore 0:
  59.8 56.1 all-gather.1
  196.1 47.3 reduce-scatter.1

commit v5 on v4

--- a/solution.py
+++ b/solution.py
@@ -101,11 +101,13 @@
 
 
 def gather_kernel(
-    pack, tokens, segs, out0, out1, out2, out3, pair, seg_all,
-    sib, block, p_send, p_recv, l_sem, s_send, s_recv, sib_send, sib_recv,
+    w_query, w_key, w_value, w_out, extra, tokens, segs,
+    o_q, o_kv, out2, out3, pair, o_normed, q4, kv2, o_first,
+    pack, sib, block, w_q, w_kv, w_extra, rows, segments, normed,
+    p_send, p_recv, l_sem, s_send, s_recv, sib_send, sib_recv, o_sem,
 ):
     y, z, x, c = coords()
-    outs = (out0, out1, out2, out3)
+    outs = (w_q, w_kv, out2, w_extra)
     me = z * 8 + x * 2 + c
     sibling = dev(y, z, x, 1 - c)
 
@@ -116,19 +118,34 @@
     lax.fori_loop(1, 32, greet, 0)
     for step in STEPS:
         signal(axis_peer("y", step))
+    heads = []
+    for h in range(KV):
+        cols = slice(HD * h, HD * h + HD)
+        heads += [w_key[:, cols].astype(F32), w_value[:, cols].astype(F32)]
+    heads = jnp.concatenate(heads, axis=1).astype(BF)
+    for k in range(2):
+        parts = (
+            w_query[:, Q_HALF * k : Q_HALF * k + Q_HALF],
+            heads[:, KV_HALF * k : KV_HALF * k + KV_HALF],
+            w_out[:, Q_HALF * k : Q_HALF * k + Q_HALF],
+            extra[...],
+        )
+        for start, width, part in zip(STARTS, WIDTHS, parts):
+            pack[k, 0:12, start : start + width] = part
+            pack[k, 12:16, start : start + width] = jnp.zeros((4, width), BF)
     pl.semaphore_wait(pltpu.get_barrier_semaphore(), 34)
 
     first = remote(pack.at[1 - c], sib, sib_send.at[0], sib_recv.at[0], sibling)
     first.start()
-    second = remote(tokens, pair.at[c], sib_send.at[1], sib_recv.at[1], sibling)
+    second = remote(tokens, rows.at[c], sib_send.at[1], sib_recv.at[1], sibling)
     second.start()
-    own_rows = pltpu.make_async_copy(tokens, pair.at[c], l_sem.at[4])
+    own_rows = pltpu.make_async_copy(tokens, rows.at[c], l_sem.at[4])
     own_rows.start()
-    own_segs = pltpu.make_async_copy(segs, seg_all.at[me], l_sem.at[5])
+    own_segs = pltpu.make_async_copy(segs, segments.at[me], l_sem.at[5])
     own_segs.start()
 
     def spread(k, carry):
-        remote(segs, seg_all.at[me], s_send, s_recv, (y, (me + k) % 32)).start()
+        remote(segs, segments.at[me], s_send, s_recv, (y, (me + k) % 32)).start()
         return carry
 
     lax.fori_loop(1, 32, spread, 0)
@@ -161,31 +178,70 @@
         if phase == 0:
             for here in locals_:
                 here.wait()
+        if phase == 2:
+            own_segs.wait()
+            drain = remote(
+                segments.at[pl.ds(0, 31)], segments.at[pl.ds(0, 31)], s_send, s_recv, sibling
+            )
+            drain.wait_send()
+            drain.wait_recv()
+            places = segments[...].reshape(32, 128)
+            for zq in range(4):
+                t = (zq * 4 + x) * 2
+                mine = jnp.concatenate([segments[t], segments[t + 1]], axis=1)
+                begin = jnp.zeros((1, PAIR), jnp.int32)
+                for u in range(15):
+                    count = jnp.sum((places == u).astype(jnp.int32))
+                    begin = begin + jnp.where(mine > u, count, 0)
+                o_first[zq] = begin
+            second.wait()
+            own_rows.wait()
         for copy in copies:
             copy.wait()
-    second.wait()
-    own_rows.wait()
-    own_segs.wait()
-    drain = remote(
-        seg_all.at[pl.ds(0, 31)], seg_all.at[pl.ds(0, 31)], s_send, s_recv, sibling
-    )
-    drain.wait_send()
-    drain.wait_recv()
-
-
-def gather_weights(pack, tokens, segs):
+    stores = [
+        pltpu.make_async_copy(src, dst, o_sem.at[n])
+        for n, (src, dst) in enumerate(((w_q, o_q), (w_kv, o_kv), (w_extra, out3), (rows, pair)))
+    ]
+    for store in stores:
+        store.start()
+    gain = jnp.transpose(w_extra[...].reshape(MODEL_WIDTH, EXTRA).astype(F32))[EXPERT_COUNT : EXPERT_COUNT + 1]
+    for k in range(2):
+        values = rows[k].astype(F32)
+        normed[ROWS * k : ROWS * k + ROWS] = (values * inverse_rms(values) * gain).astype(BF)
+    last = pltpu.make_async_copy(normed, o_normed, o_sem.at[4])
+    last.start()
+    queries = dot(w_q[...].reshape(MODEL_WIDTH, Q_HALF), normed[...], ((0,), (1,))).astype(BF)
+    q4[...] = queries.reshape(4, HEAD_Q, PAIR)
+    kv2[...] = dot(normed[...], w_kv[...].reshape(MODEL_WIDTH, KV_HALF), ((1,), (0,))).astype(BF)
+    for store in stores:
+        store.wait()
+    last.wait()
+
+
+def gather_weights(w_query, w_key, w_value, w_out, extra, tokens, segs):
+    blocks = [(4, 4, 4, 24, width) for width in WIDTHS]
+    rows = (2, ROWS, MODEL_WIDTH)
+    flat = (PAIR, MODEL_WIDTH)
     return pl.pallas_call(
         gather_kernel,
-        out_shape=[jax.ShapeDtypeStruct((4, 4, 4, 24, width), BF) for width in WIDTHS]
+        out_shape=[jax.ShapeDtypeStruct(shape, BF) for shape in (*blocks, rows, flat)]
         + [
-            jax.ShapeDtypeStruct((2, ROWS, MODEL_WIDTH), BF),
-            jax.ShapeDtypeStruct((32, 1, 128), jnp.int32),
+            jax.ShapeDtypeStruct((4, HEAD_Q, PAIR), BF),
+            jax.ShapeDtypeStruct((PAIR, KV_HALF), BF),
+            jax.ShapeDtypeStruct((4, 1, PAIR), jnp.int32),
         ],
-        in_specs=[IN_VMEM, ANY, ANY],
-        out_specs=[ANY] * 6,
+        in_specs=[IN_VMEM] * 5 + [ANY, ANY],
+        out_specs=[ANY] * 6 + [IN_VMEM] * 3,
         scratch_shapes=[
+            pltpu.VMEM((2, 16, PACK), BF),
             pltpu.VMEM((16, PACK), BF),
             pltpu.VMEM((24, PACK), BF),
+            pltpu.VMEM(blocks[0], BF),
+            pltpu.VMEM(blocks[1], BF),
+            pltpu.VMEM(blocks[3], BF),
+            pltpu.VMEM(rows, BF),
+            pltpu.VMEM((32, 1, 128), jnp.int32),
+            pltpu.VMEM(flat, BF),
             pltpu.SemaphoreType.DMA((3, 7, 3)),
             pltpu.SemaphoreType.DMA((3, 7, 3)),
             pltpu.SemaphoreType.DMA((6,)),
@@ -193,10 +249,32 @@
             pltpu.SemaphoreType.DMA,
             pltpu.SemaphoreType.DMA((2,)),
             pltpu.SemaphoreType.DMA((2,)),
+            pltpu.SemaphoreType.DMA((5,)),
         ],
-        compiler_params=params(1),
+        compiler_params=params(1, 60 << 20),
         name="gather_weights",
-    )(pack, tokens, segs)
+    )(w_query, w_key, w_value, w_out, extra, tokens, segs)
+
+
+def offset(k):
+    dz = (k % 8) // 2
+    return dz, 2 * (k % 2) + (dz + k // 8) % 2
+
+
+def chip_to(k):
+    y, z, x, c = coords()
+    dz, dx = offset(k)
+    return (z + dz) % 4, (x + dx) % 4
+
+
+def chip_from(k):
+    y, z, x, c = coords()
+    dz, dx = offset(k)
+    return (z + 4 - dz) % 4, (x + 4 - dx) % 4
+
+
+def slot_block(k, core):
+    return (k // 8) * 16 + core * 8 + k % 8
 
 
 def plane_greet(y, me, c, sibling):
@@ -268,24 +346,25 @@
             copy.start()
             w_copies[part].append(copy)
 
+    def cots_copy(k):
+        tz, tx = chip_to(k)
+        return remote(
+            cots.at[tz * 4 + tx], c_all.at[slot_block(k, c)], c_send.at[k], c_recv.at[k], dev(y, tz, tx, c)
+        )
+
     def send_cots(k, carry):
-        t = (me + k) % 16
-        remote(
-            cots.at[t], c_all.at[c * 16 + me], c_send.at[k], c_recv.at[k], dev(y, t // 4, t % 4, c)
-        ).start()
+        cots_copy(k).start()
         return carry
 
     lax.fori_loop(1, 16, send_cots, 0)
-    own_cots = pltpu.make_async_copy(cots.at[me], c_all.at[c * 16 + me], l_sem.at[2])
+    own_cots = pltpu.make_async_copy(cots.at[me], c_all.at[slot_block(0, c)], l_sem.at[2])
     own_cots.start()
-    remote(cots.at[me], c_all.at[c * 16 + me], f_send, f_recv, sibling).start()
+    remote(cots.at[me], c_all.at[slot_block(0, c)], f_send, f_recv, sibling).start()
 
     def forward_cots(k, carry):
-        s = c * 16 + (me + 16 - k) % 16
-        t = (me + k) % 16
-        arrived = remote(cots.at[t], c_all.at[s], c_send.at[k], c_recv.at[k], dev(y, t // 4, t % 4, c))
+        arrived = cots_copy(k)
         arrived.wait_recv()
-        remote(c_all.at[s], c_all.at[s], f_send, f_recv, sibling).start()
+        remote(c_all.at[slot_block(k, c)], c_all.at[slot_block(k, c)], f_send, f_recv, sibling).start()
         arrived.wait_send()
         return carry
 
@@ -403,7 +482,7 @@
             pltpu.SemaphoreType.DMA((4, 2)),
             pltpu.SemaphoreType.DMA((4, 2)),
         ],
-        compiler_params=params(2, 56 << 20),
+        compiler_params=params(2, 60 << 20),
         name="attend",
     )(q4, kv2, half, cots, first)
 
@@ -431,101 +510,92 @@
         load.start()
     arrays = ((xs, x_all), (gates, t_all))
 
-    def scatter(a):
+    def arriving(a, k):
         src, dst = arrays[a]
-
+        tz, tx = chip_to(k)
+        return remote(
+            src.at[tz * 4 + tx], dst.at[slot_block(k, c)], send.at[a, k], recv.at[a, k], dev(y, tz, tx, c)
+        )
+
+    def steps_of(part):
+        return (1, 8) if part == 0 else (8, 16)
+
+    def scatter(a, part):
         def push(k, carry):
-            t = (me + k) % 16
-            remote(
-                src.at[t], dst.at[c * 16 + me], send.at[a, k], recv.at[a, k], dev(y, t // 4, t % 4, c)
-            ).start()
+            arriving(a, k).start()
             return carry
 
-        lax.fori_loop(1, 16, push, 0)
-        pltpu.make_async_copy(src.at[me], dst.at[c * 16 + me], l_sem.at[a]).start()
-        remote(src.at[me], dst.at[c * 16 + me], f_send.at[a], f_recv.at[a], sibling).start()
-
-    def hand_over(a):
+        lax.fori_loop(*steps_of(part), push, 0)
+        if part == 0:
+            src, dst = arrays[a]
+            pltpu.make_async_copy(src.at[me], dst.at[slot_block(0, c)], l_sem.at[a]).start()
+            remote(src.at[me], dst.at[slot_block(0, c)], f_send.at[a, 0], f_recv.at[a, 0], sibling).start()
+
+    def hand_over(a, part):
         src, dst = arrays[a]
 
         def forward(k, carry):
-            s = (me + 16 - k) % 16
-            t = (me + k) % 16
-            arrived = remote(
-                src.at[t], dst.at[c * 16 + s], send.at[a, k], recv.at[a, k], dev(y, t // 4, t % 4, c)
-            )
+            arrived = arriving(a, k)
             arrived.wait_recv()
-            remote(
-                dst.at[c * 16 + s], dst.at[c * 16 + s], f_send.at[a], f_recv.at[a], sibling
-            ).start()
+            block = dst.at[slot_block(k, c)]
+            remote(block, block, f_send.at[a, part], f_recv.at[a, part], sibling).start()
             arrived.wait_send()
             return carry
 
-        lax.fori_loop(1, 16, forward, 0)
-
-    def settle(a):
+        lax.fori_loop(*steps_of(part), forward, 0)
+
+    def settle(a, part):
         src, dst = arrays[a]
-        pltpu.make_async_copy(src.at[me], dst.at[c * 16 + me], l_sem.at[a]).wait()
-        half = pl.ds(0, 16)
-        drain = remote(dst.at[half], dst.at[half], f_send.at[a], f_recv.at[a], sibling)
+        if part == 0:
+            pltpu.make_async_copy(src.at[me], dst.at[slot_block(0, c)], l_sem.at[a]).wait()
+        some = dst.at[pl.ds(0, 8)]
+        drain = remote(some, some, f_send.at[a, part], f_recv.at[a, part], sibling)
         drain.wait_send()
         drain.wait_recv()
 
-    def swap(part, sib, a):
-        rows = pl.ds((1 - c) * 16, 16)
-        return remote(part.at[rows], sib, s_send.at[a], s_recv.at[a], sibling)
-
-    def give(part, sib, ret, a):
-        def add(t):
-            rows = c * 16 + t
-            part[rows] = (
-                part[rows].astype(F32) + sib[t].astype(F32)
-            ).astype(BF)
-            return part.at[rows]
+    def swap(mine, sib, a, part):
+        return remote(
+            mine.at[pl.ds(part * 16 + (1 - c) * 8, 8)], sib.at[pl.ds(part * 8, 8)],
+            s_send.at[a, part], s_recv.at[a, part], sibling,
+        )
+
+    def give(mine, sib, ret, a, part):
+        def add(k):
+            block = slot_block(k, c)
+            mine[block] = (mine[block].astype(F32) + sib[k].astype(F32)).astype(BF)
+            return mine.at[block]
 
         def push(k, carry):
-            t = (me + k) % 16
-            remote(add(t), ret.at[me], r_send.at[a], r_recv.at[a], dev(y, t // 4, t % 4, c)).start()
+            sz, sx = chip_from(k)
+            remote(add(k), ret.at[me], r_send.at[a], r_recv.at[a], dev(y, sz, sx, c)).start()
             return carry
 
-        lax.fori_loop(1, 16, push, 0)
-        pltpu.make_async_copy(add(me), ret.at[me], l_sem.at[2 + a]).start()
-
-    def given(part, ret, a):
-        pltpu.make_async_copy(part.at[c * 16 + me], ret.at[me], l_sem.at[2 + a]).wait()
+        lax.fori_loop(*steps_of(part), push, 0)
+        if part == 0:
+            pltpu.make_async_copy(add(0), ret.at[me], l_sem.at[2 + a]).start()
+
+    def given(mine, ret, a):
+        pltpu.make_async_copy(mine.at[slot_block(0, c)], ret.at[me], l_sem.at[2 + a]).wait()
         drain = remote(ret.at[pl.ds(0, 15)], ret.at[pl.ds(0, 15)], r_send.at[a], r_recv.at[a], sibling)
         drain.wait_send()
         drain.wait_recv()
 
-    def tile(n):
-        h = 1 - c if n == 0 else c
-        rows = 16 * SLOTS
-        return pl.ds(h * 16, 16), pl.ds(pl.multiple_of(h * rows, rows), rows)
-
-    scatter(0)
-    scatter(1)
-    hand_over(0)
-    hand_over(1)
-    settle(0)
-    settle(1)
-    for load in loads:
-        load.wait()
-    for n in range(2):
-        blocks, rows = tile(n)
-        rows_in = flat_rows(x_all[blocks])
-        both = dot(rows_in, w_all[:, : 2 * width], ((1,), (0,)))
+    half = 16 * SLOTS
+
+    def forward_pass(part):
+        blocks, rows = pl.ds(part * 16, 16), slice(part * half, part * half + half)
+        both = dot(flat_rows(x_all[blocks]), w_all[:, : 2 * width], ((1,), (0,)))
         gate_val, up_val = both[:, :width], both[:, width:]
         gate_v[rows] = gate_val
         up_v[rows] = up_val
         low = (gate_val * jax.nn.sigmoid(gate_val) * up_val).astype(BF)
         hidden[rows] = low
-        part_o[blocks] = dot(low, w_all[:, 2 * width :], ((1,), (1,))).astype(BF).reshape(16, SLOTS, MODEL_WIDTH)
-        if n == 0:
-            swap(part_o, sib_o, 0).start()
-    swap(part_o, sib_o, 0).wait()
-    give(part_o, sib_o, out_ret, 0)
-    for n in range(2):
-        blocks, rows = tile(n)
+        out = dot(low, w_all[:, 2 * width :], ((1,), (1,))).astype(BF)
+        part_o[blocks] = out.reshape(16, SLOTS, MODEL_WIDTH)
+        swap(part_o, sib_o, 0, part).start()
+
+    def backward_pass(part):
+        blocks, rows = pl.ds(part * 16, 16), slice(part * half, part * half + half)
         scale = jnp.concatenate([flat_rows(t_all[blocks])] * (MODEL_WIDTH // 128), axis=1)
         grad_expert = (flat_rows(g_all[blocks]).astype(F32) * scale).astype(BF)
         g_all[blocks] = grad_expert.reshape(16, SLOTS, MODEL_WIDTH)
@@ -537,12 +607,36 @@
         grad_up = (grad_hidden * gate_val * sig).astype(BF)
         grads = jnp.concatenate([grad_gate, grad_up], axis=1)
         g_both[rows] = grads
-        grad_rows = dot(grads, w_all[:, : 2 * width], ((1,), (1,)))
-        part_g[blocks] = grad_rows.astype(BF).reshape(16, SLOTS, MODEL_WIDTH)
-        if n == 0:
-            swap(part_g, sib_g, 1).start()
-    swap(part_g, sib_g, 1).wait()
-    give(part_g, sib_g, grad_ret, 1)
+        grad_rows = dot(grads, w_all[:, : 2 * width], ((1,), (1,))).astype(BF)
+        part_g[blocks] = grad_rows.reshape(16, SLOTS, MODEL_WIDTH)
+        swap(part_g, sib_g, 1, part).start()
+
+    scatter(0, 0)
+    scatter(1, 0)
+    scatter(0, 1)
+    scatter(1, 1)
+    for load in loads:
+        load.wait()
+    hand_over(0, 0)
+    settle(0, 0)
+    forward_pass(0)
+    hand_over(0, 1)
+    swap(part_o, sib_o, 0, 0).wait()
+    give(part_o, sib_o, out_ret, 0, 0)
+    settle(0, 1)
+    forward_pass(1)
+    hand_over(1, 0)
+    hand_over(1, 1)
+    settle(1, 0)
+    swap(part_o, sib_o, 0, 1).wait()
+    give(part_o, sib_o, out_ret, 0, 1)
+    backward_pass(0)
+    settle(1, 1)
+    swap(part_g, sib_g, 1, 0).wait()
+    give(part_g, sib_g, grad_ret, 1, 0)
+    backward_pass(1)
+    swap(part_g, sib_g, 1, 1).wait()
+    give(part_g, sib_g, grad_ret, 1, 1)
 
     def weight_grads(j, carry):
         cols = pl.ds(pl.multiple_of(j * 256, 256), 256)
@@ -585,15 +679,15 @@
             pltpu.SemaphoreType.DMA((4,)),
             pltpu.SemaphoreType.DMA((2, 16)),
             pltpu.SemaphoreType.DMA((2, 16)),
-            pltpu.SemaphoreType.DMA((2,)),
-            pltpu.SemaphoreType.DMA((2,)),
-            pltpu.SemaphoreType.DMA((2,)),
-            pltpu.SemaphoreType.DMA((2,)),
+            pltpu.SemaphoreType.DMA((2, 2)),
+            pltpu.SemaphoreType.DMA((2, 2)),
+            pltpu.SemaphoreType.DMA((2, 2)),
+            pltpu.SemaphoreType.DMA((2, 2)),
             pltpu.SemaphoreType.DMA((2,)),
             pltpu.SemaphoreType.DMA((2,)),
             pltpu.SemaphoreType.DMA,
         ],
-        compiler_params=params(6, 56 << 20),
+        compiler_params=params(6, 60 << 20),
         name="experts",
     )(xs, gates, cots, weights)
 
@@ -775,7 +869,7 @@
             pltpu.SemaphoreType.DMA((2,)),
             pltpu.SemaphoreType.DMA((2,)),
         ],
-        compiler_params=params(8, 58 << 20),
+        compiler_params=params(8, 60 << 20),
         name="reduce_weights",
     )(gq_t, dkv, normed, g_moe, s_out, pair, gain, grad_middle, w_q, w_kv)
 
@@ -980,7 +1074,7 @@
             pltpu.SemaphoreType.DMA((3, 3)),
             pltpu.SemaphoreType.DMA((3, 3)),
         ],
-        compiler_params=params(4, 58 << 20),
+        compiler_params=params(4, 60 << 20),
         name="attend_back",
     )(heads, branch, own_attn, other_attn, q_in, kv_in, first, ot, lse)
 
@@ -1000,10 +1094,6 @@
 
 def only_column(rows, column):
     return jnp.broadcast_to((jnp.arange(EXTRA) == column).astype(F32), (rows, EXTRA))
-
-
-def halves(matrix):
-    return matrix.reshape(12, 2, Q_HALF).transpose(1, 0, 2)
 
 
 def local(
@@ -1024,27 +1114,14 @@
 ):
     y, z, x, c = coords()
     width = w_gate.shape[1]
-    key_value = jnp.concatenate(
-        [w_key.reshape(12, 2, 4, HD), w_value.reshape(12, 2, 4, HD)], axis=3
-    ).reshape(12, 2, KV_HALF)
     extra = jnp.concatenate(
         [w_router, gain_attn[:, None], gain_moe[:, None], jnp.zeros((12, EXTRA - 18), BF)], axis=1
     )
-    pack = jnp.concatenate(
-        [
-            halves(w_query),
-            key_value.transpose(1, 0, 2),
-            halves(w_out.T),
-            jnp.broadcast_to(extra[None], (2, 12, EXTRA)),
-        ],
-        axis=2,
-    )
-    pack = jnp.pad(pack, ((0, 0), (0, 4), (0, 0)))
+    part_q, part_kv, part_out, part_extra, pair, normed, q4, keys_values, first = gather_weights(
+        w_query, w_key, w_value, w_out.T, extra, tokens, segment_ids
+    )
+    pair, w_gate, w_up, w_down = lax.optimization_barrier((pair, w_gate, w_up, w_down))
     w_experts = jnp.concatenate([w_gate, w_up, w_down.T], axis=1)
-    part_q, part_kv, part_out, part_extra, pair, seg_all = gather_weights(
-        pack, tokens, segment_ids
-    )
-    pair, w_experts = lax.optimization_barrier((pair, w_experts))
     full_experts = lax.all_gather(w_experts, "dp", axis=0, tiled=True)
     full_q = part_q.reshape(MODEL_WIDTH, Q_HALF)
     full_kv = part_kv.reshape(MODEL_WIDTH, KV_HALF)
@@ -1054,18 +1131,6 @@
     gain_a, gain_m = gains[0:1], gains[1:2]
     router = full_extra[:, :EXPERT_COUNT]
 
-    inputs2 = pair.reshape(PAIR, MODEL_WIDTH).astype(F32)
-    inverse_a = inverse_rms(inputs2)
-    normed = (inputs2 * inverse_a * gain_a).astype(BF)
-    q4 = dot(full_q, normed, ((0,), (1,))).astype(BF).reshape(4, HEAD_Q, PAIR)
-    keys_values = dot(normed, full_kv, ((1,), (0,))).astype(BF)
-    segs = seg_all.reshape(1, 4096)
-    counts = jnp.sum((segs < jnp.arange(16)[:, None]).astype(jnp.int32), axis=1)
-    row_segs = lax.dynamic_index_in_dim(seg_all.reshape(4, 4, PAIR), x, 1, keepdims=False)
-    first = jnp.sum(
-        jnp.where(row_segs[:, :, None] == jnp.arange(16), counts, 0), axis=2
-    )
-    first = first.reshape(4, 1, PAIR)
     chosen = (expert_ids[:, :, None] == jnp.arange(EXPERT_COUNT, dtype=jnp.int32)).astype(F32)
     used = jnp.sum(chosen, axis=1)
     earlier = (jnp.arange(ROWS)[:, None] > jnp.arange(ROWS)[None, :]).astype(BF)

time: 330 us -> 314 us (0.952)
  Pallas kernels: 267 us -> 260 us
  local copies, waits for them, and re-layouts: 18.4 us -> 14.4 us
    pallas_call x1, Pallas kernels: 62.8 us -> 51.1 us  [experts(): pl.pallas_call(experts_kernel, out_shape=[back, back, jax.ShapeDtypeStruc...]
    reshape x8 -> x0, local copies, waits for them, and re-layouts: 3.92 us -> none  [the longest x2 1.66 us: halves(): return matrix.reshape(12, 2, Q_HALF).transpose(1, 0, 2)]
    dot_general x14 -> x12, matrix products: 13.8 us -> 10.8 us  [dot(): return lax.dot_general(a, b, (dims, ((), ())), preferred_element_type=F32)]
    unnamed x61 -> x49, local copies, waits for them, and re-layouts: 9.34 us -> 8.71 us
  transfers between devices with their start and end apart: 2 -> 2, of which waited for: 0 -> 0; matrix products, arithmetic and copies ran while one was open for 8% -> 6% of each run, Pallas kernels for 49% -> 52%
where the time goes in v5:
time: 314 us
  Pallas kernels  260 us (83%)
  between operations  14.5 us (5%)
  local copies, waits for them, and re-layouts  14.4 us (5%)
  matrix products  14.4 us (5%)
  other arithmetic  10.2 us (3%)
    pallas_call x1, Pallas kernels, attend_back(): pl.pallas_call(attend_back_kernel, out_shape=[jax.ShapeDtypeStruct((4, HE...  60.6 us
    pallas_call x1, Pallas kernels, attend(): pl.pallas_call(attend_kernel, out_shape=[jax.ShapeDtypeStruct((4, HEAD_Q,...  57 us
    pallas_call x1, Pallas kernels, experts(): pl.pallas_call(experts_kernel, out_shape=[back, back, jax.ShapeDtypeStruc...  51.1 us
    pallas_call x1, Pallas kernels, gather_weights(): pl.pallas_call(gather_kernel, out_shape=[jax.ShapeDtypeStruct(shape, BF)...  46.6 us
    pallas_call x1, Pallas kernels, reduce_weights(): pl.pallas_call(reduce_kernel, out_shape=[jax.ShapeDtypeStruct(shape, F32)...  44.9 us
    dot_general x12, matrix products, dot(): return lax.dot_general(a, b, (dims, ((), ())), preferred_element_type=F32)  10.8 us
    unnamed x49, local copies, waits for them, and re-layouts  8.71 us
  transfers between devices with their start and end apart: 2, of which 0 were waited for; matrix products, arithmetic and copies ran while one was open for 6% of the time, Pallas kernels for 52%

profile of v5, /device:TPU:1, one launch (start us, length us, event | category | flops | bytes accessed | tf_op | source)
XLA Modules:
  0.0 313.8 jit_solution(17780386840696598386)
XLA Ops:
  8.8 1.4 maximum_maximum_fusion.extra
  10.2 46.6 %gather_weights.1 = (bf16[4,4,4,24,768]{4,3,2,1,0:T(8,128)(2,1)}, bf16[4,4,4,24,512]{4,3,2,1,0:T(8,128)(2,1)}, bf16[4,4,4,24,768]{4,3,2,1,0:T(8,128)(2,1)}, bf16...) custom-call(bf16[12,1536]{1,0:T(8,128)(2,1)} %w_query.1, ...), custom_call_target="tpu_custom_call" | custom-call | tf_op jit(solution)/shard_map/gather_weights/pallas_call | solution.py:225
  56.8 1.2 copy.45
  58.0 2.2 pad_maximum_fusion
  60.7 1.5 convolution_convert_fusion.1
  62.2 57.0 %attend.1 = (bf16[4,192,256]{2,1,0:T(8,128)(2,1)}, bf16[16,256,128]{2,1,0:T(8,128)(2,1)}, bf16[8,192,128]{2,1,0:T(8,128)(2,1)}, f32[4,64,768]{2,1,0:T(8,128)}, f...) custom-call(bf16[4,192,256]{2,1,0:T(8,128)(2,1)} %get-tuple-element., ...), custom_call_target="tpu_custom_call", output_to_operand_aliasing={{5}: (2, {})} | custom-call | tf_op jit(solution)/shard_map/attend/pallas_call | solution.py:450
  119.2 1.2 broadcast_select_fusion
  121.1 2.6 convolution_add_fusion.3
  123.7 1.0 multiply_reduce_fusion.1
  126.3 1.5 convolution_convert_fusion
  128.7 51.1 %experts.1 = (bf16[16,24,1536]{2,1,0:T(8,128)(2,1)}, bf16[16,24,1536]{2,1,0:T(8,128)(2,1)}, bf16[1536,1536]{1,0:T(8,128)(2,1)}) custom-call(bf16[16,24,1536]{2,1,0:T(8,128)(2,1)} %bitcast.72, f32[16,24,128]{2,1,0:T(8,128)} %broadcast_in_dim.21.gates, bf16[32,24,1536]{2,1,0:T(8,128)(2,1)} %get-tuple-element.53.cots, ...), custom_call_target="tpu_custom_call" | custom-call | tf_op jit(solution)/shard_map/experts/pallas_call | solution.py:659
  179.8 1.2 copy-done.1
  181.4 1.2 fusion
  183.8 1.2 fusion.27
  185.0 0.8 convolution_convert_fusion.2
  185.8 1.6 copy-done
  187.4 0.8 select_bitcast_fusion.1
  189.0 60.6 %attend_back.1 = (bf16[4,192,256]{2,1,0:T(8,128)(2,1)}, bf16[16,256,128]{2,1,0:T(8,128)(2,1)}, bf16[3,4,4,24,256]{4,3,2,1,0:T(8,128)(2,1)}) custom-call(bf16[8,192,128]{2,1,0:T(8,128)(2,1)} %bitcast.85, bf16[128,1536]{1,0:T(8,128)(2,1)} %copy-done.12, bf16[768,128]{1,0:T(8,128)(2,1)} %bitcast.82, bf16[768,128]{1,0:T(8,128)(2,1)} %bitcast.80, ...), custom_call_target="tpu_custom_call" | custom-call | tf_op jit(solution)/shard_map/attend_back/pallas_call | solution.py:1044
  250.2 2.4 convolution_add_fusion.g_moe
  252.6 44.9 %reduce_weights.1 = (f32[128,1536]{1,0:T(8,128)}, f32[12,1536]{1,0:T(8,128)}, f32[12,512]{1,0:T(8,128)}, f32[12,512]{1,0:T(8,128)}, f32[12,1536]{1,0:T(8,128)}, /*index=5*/f32[12,128]{1,0:T(8,128)}) custom-call(bf16[768,256]{1,0:T(8,128)(2,1)} %bitcast.88, bf16[16,256,128]{2,1,0:T(8,128)(2,1)} %get-tuple-element.65.dkv, ...), custom_call_target="tpu_custom_call" | custom-call | tf_op jit(solution)/shard_map/reduce_weights/pallas_call | solution.py:859
  297.5 1.5 slice_reduce_fusion
  299.0 2.8 convert_bitcast_fusion
  301.8 1.1 copy.46
  302.9 0.9 copy.54
  (86 shorter events, 11.0 us)
Async XLA Ops:
  7.2 120.7 %all-gather.2.cloned.1.call-start = ((), (), s32[]{:S(2)}) async-start(), calls=%async_computation.1 | async-start | bytes 5898240 | tf_op jit(solution)/shard_map/all_gather | solution.py:1125
  10.2 50.1 %copy-start.20 = (s32[128,2]{0,1:T(2,128)S(1)}, s32[128,2]{0,1:T(2,128)}, u32[]{:S(2)}) copy-start(s32[128,2]{0,1:T(2,128)} %param.16) | copy-start | bytes 3076
  58.0 2.7 copy-start.2
  60.3 238.7 %reduce-scatter.2.cloned.1.call-start = ((), (), s32[]{:S(2)}) async-start(), calls=%async_computation.2 | async-start | bytes 5898240 | tf_op jit(solution)/shard_map/reduce_scatter | solution.py:1172
  60.7 65.6 %copy-start.9 = (bf16[128,384]{1,0:T(8,128)(2,1)}, bf16[128,384]{1,0:T(8,128)(2,1)S(1)}, u32[]{:S(2)}) copy-start(bf16[128,384]{1,0:T(8,128)(2,1)S(1)} %fusion.15) | copy-start | bytes 294916
  62.2 58.9 %copy-start.11 = (bf16[128,1536]{1,0:T(8,128)(2,1)S(1)}, bf16[128,1536]{1,0:T(8,128)(2,1)}, u32[]{:S(2)}) copy-start(bf16[128,1536]{1,0:T(8,128)(2,1)} %tokens.1) | copy-start | bytes 1179652
  119.2 4.5 %copy-start.5 = (bf16[4,4,4,24,768]{4,3,2,1,0:T(8,128)(2,1)S(1)}, bf16[4,4,4,24,768]{4,3,2,1,0:T(8,128)(2,1)}, u32[]{:S(2)}) copy-start(bf16[4,4,4,24,768]{4,3,2,1,0:T(8,128)(2,1)} %get-tuple-element.51) | copy-start | bytes 7077892
  120.4 0.7 copy-start.8
  120.5 4.2 %copy-start.7 = (bf16[4,192,128]{2,1,0:T(8,128)(2,1)}, bf16[4,192,128]{2,1,0:T(8,128)(2,1)S(1)}, u32[]{:S(2)}) copy-start(bf16[4,192,128]{2,1,0:T(8,128)(2,1)S(1)} %get-tuple-element.126) | copy-start | bytes 589828
  123.7 1.0 copy-start.3
  179.8 1.3 copy-start.1
  181.4 1.3 copy-start.10
  181.4 1.3 copy-start.13
  181.4 1.7 copy-start.4
  183.1 1.8 copy-start.6
  185.0 3.3 %copy-start.12 = (bf16[128,1536]{1,0:T(8,128)(2,1)}, bf16[128,1536]{1,0:T(8,128)(2,1)S(1)}, u32[]{:S(2)}) copy-start(bf16[128,1536]{1,0:T(8,128)(2,1)S(1)} %get-tuple-element.118.branch) | copy-start | bytes 1179652
  185.0 2.4 copy-start
  299.0 4.0 %copy-start.14 = (f32[128,1536]{1,0:T(8,128)S(1)}, f32[128,1536]{1,0:T(8,128)}, u32[]{:S(2)}) copy-start(f32[128,1536]{1,0:T(8,128)} %get-tuple-element.151) | copy-start | bytes 2359300
  301.8 2.1 copy-start.16
  301.8 2.7 copy-start.19
  301.8 3.3 %copy-start.18 = (f32[12,512]{1,0:T(8,128)S(1)}, f32[12,512]{1,0:T(8,128)}, u32[]{:S(2)}) copy-start(f32[12,512]{1,0:T(8,128)} %get-tuple-element.154) | copy-start | bytes 73732
  301.8 3.9 %copy-start.15 = (f32[12,1536]{1,0:T(8,128)S(1)}, f32[12,1536]{1,0:T(8,128)}, u32[]{:S(2)}) copy-start(f32[12,1536]{1,0:T(8,128)} %get-tuple-element.75) | copy-start | bytes 221188
  301.8 4.6 %copy-start.17 = (f32[12,128]{1,0:T(8,128)S(1)}, f32[12,128]{1,0:T(8,128)}, u32[]{:S(2)}) copy-start(f32[12,128]{1,0:T(8,128)} %get-tuple-element.76) | copy-start | bytes 18436
Sparse Core Ops, SparseCore 0:
  60.4 56.2 all-gather.1
  179.9 48.3 reduce-scatter.1

commit v6 on v5

--- a/solution.py
+++ b/solution.py
@@ -8,7 +8,6 @@
 from jax.sharding import PartitionSpec as P
 
 MODEL_WIDTH = 1536
-HEADS = 24
 KV = 8
 HD = 64
 EXPERT_COUNT = 16
@@ -26,7 +25,6 @@
 EPS = 1e-05
 SCALE_QK = 0.125
 NEGATIVE = -1e30
-HIGH_PRECISION = lax.Precision.HIGHEST
 MESH = pl.DeviceIdType.MESH
 ANY = pl.BlockSpec(memory_space=pl.ANY)
 IN_VMEM = pl.BlockSpec(memory_space=pltpu.VMEM)
@@ -100,10 +98,39 @@
     ]
 
 
+def column_of(row):
+    return jnp.transpose(jnp.broadcast_to(row, (128, row.shape[1])))
+
+
+def slot_hits(ids):
+    lane = lax.broadcasted_iota(jnp.int32, (ROWS, 128), 1).astype(F32)
+    experts_of = [column_of(ids[k : k + 1].astype(F32)) for k in range(2)]
+    chosen = [jnp.where(lane == expert, 1.0, 0.0) for expert in experts_of]
+    row = lax.broadcasted_iota(jnp.int32, (ROWS, ROWS), 0)
+    earlier = jnp.where(row > lax.broadcasted_iota(jnp.int32, (ROWS, ROWS), 1), 1.0, 0.0).astype(BF)
+    before = dot(earlier, (chosen[0] + chosen[1]).astype(BF), ((1,), (0,)))
+    slot_lane = lax.broadcasted_iota(jnp.int32, (ROWS, EXPERT_COUNT * SLOTS), 1).astype(F32)
+    hits = []
+    for k in range(2):
+        place = jnp.sum(chosen[k] * before, axis=1, keepdims=True)
+        slot = jnp.where(place < EXPERT_CAPACITY, experts_of[k][:, :1] * SLOTS + place, -1.0)
+        hits.append(jnp.where(slot_lane == slot, 1.0, 0.0))
+    return chosen, hits
+
+
+def three_parts(values):
+    parts = []
+    for _ in range(3):
+        part = values.astype(BF)
+        parts.append(part)
+        values = values - part.astype(F32)
+    return parts
+
+
 def gather_kernel(
-    w_query, w_key, w_value, w_out, extra, tokens, segs,
-    o_q, o_kv, out2, out3, pair, o_normed, q4, kv2, o_first,
-    pack, sib, block, w_q, w_kv, w_extra, rows, segments, normed,
+    w_query, w_key, w_value, w_out, w_router, gain_a, gain_m, ids, cots, tokens, segs, w_gate, w_up, w_down,
+    o_q, o_kv, out2, out3, pair, o_normed, w_experts, q4, kv2, o_first, cot_slots,
+    pack, sib, block, w_q, w_kv, w_extra, rows, segments, normed, packed, down,
     p_send, p_recv, l_sem, s_send, s_recv, sib_send, sib_recv, o_sem,
 ):
     y, z, x, c = coords()
@@ -118,6 +145,23 @@
     lax.fori_loop(1, 32, greet, 0)
     for step in STEPS:
         signal(axis_peer("y", step))
+    expert_loads = [
+        pltpu.make_async_copy(w_gate, packed.at[:, 0:FF // 2], o_sem.at[5]),
+        pltpu.make_async_copy(w_up, packed.at[:, FF // 2 : FF], o_sem.at[6]),
+        pltpu.make_async_copy(w_down, down, o_sem.at[7]),
+    ]
+    for load in expert_loads:
+        load.start()
+    lane = lax.broadcasted_iota(jnp.int32, (12, EXTRA), 1)
+    square = lax.broadcasted_iota(jnp.int32, (12, 12), 0) == lax.broadcasted_iota(jnp.int32, (12, 12), 1)
+    extra = jnp.concatenate(
+        [w_router[...].astype(F32), jnp.zeros((12, EXTRA - EXPERT_COUNT), F32)], axis=1
+    )
+    for k, gain_row in enumerate((gain_a, gain_m)):
+        spread_row = jnp.broadcast_to(gain_row[...].astype(F32), (12, 12))
+        column = jnp.sum(jnp.where(square, spread_row, 0.0), axis=1, keepdims=True)
+        extra = jnp.where(lane == EXPERT_COUNT + k, column, extra)
+    extra = extra.astype(BF)
     heads = []
     for h in range(KV):
         cols = slice(HD * h, HD * h + HD)
@@ -128,7 +172,7 @@
             w_query[:, Q_HALF * k : Q_HALF * k + Q_HALF],
             heads[:, KV_HALF * k : KV_HALF * k + KV_HALF],
             w_out[:, Q_HALF * k : Q_HALF * k + Q_HALF],
-            extra[...],
+            extra,
         )
         for start, width, part in zip(STARTS, WIDTHS, parts):
             pack[k, 0:12, start : start + width] = part
@@ -194,6 +238,13 @@
                     count = jnp.sum((places == u).astype(jnp.int32))
                     begin = begin + jnp.where(mine > u, count, 0)
                 o_first[zq] = begin
+            chosen, hits = slot_hits(ids[...])
+            kept = dot((hits[0] + hits[1]).astype(BF), cots[...], ((0,), (0,))).astype(BF)
+            cot_slots[...] = kept.reshape(EXPERT_COUNT, SLOTS, MODEL_WIDTH)
+            for load in expert_loads:
+                load.wait()
+            packed[:, FF:] = jnp.transpose(down[...].astype(F32)).astype(BF)
+            pltpu.make_async_copy(packed, w_experts, o_sem.at[5]).start()
             second.wait()
             own_rows.wait()
         for copy in copies:
@@ -216,22 +267,25 @@
     for store in stores:
         store.wait()
     last.wait()
-
-
-def gather_weights(w_query, w_key, w_value, w_out, extra, tokens, segs):
+    pltpu.make_async_copy(packed, w_experts, o_sem.at[5]).wait()
+
+
+def gather_weights(vmem_args, hbm_args):
     blocks = [(4, 4, 4, 24, width) for width in WIDTHS]
     rows = (2, ROWS, MODEL_WIDTH)
     flat = (PAIR, MODEL_WIDTH)
+    experts_in = (MODEL_WIDTH // 4, 3 * FF // 2)
     return pl.pallas_call(
         gather_kernel,
-        out_shape=[jax.ShapeDtypeStruct(shape, BF) for shape in (*blocks, rows, flat)]
+        out_shape=[jax.ShapeDtypeStruct(shape, BF) for shape in (*blocks, rows, flat, experts_in)]
         + [
             jax.ShapeDtypeStruct((4, HEAD_Q, PAIR), BF),
             jax.ShapeDtypeStruct((PAIR, KV_HALF), BF),
             jax.ShapeDtypeStruct((4, 1, PAIR), jnp.int32),
+            jax.ShapeDtypeStruct((EXPERT_COUNT, SLOTS, MODEL_WIDTH), BF),
         ],
-        in_specs=[IN_VMEM] * 5 + [ANY, ANY],
-        out_specs=[ANY] * 6 + [IN_VMEM] * 3,
+        in_specs=[IN_VMEM] * len(vmem_args) + [ANY] * len(hbm_args),
+        out_specs=[ANY] * 7 + [IN_VMEM] * 4,
         scratch_shapes=[
             pltpu.VMEM((2, 16, PACK), BF),
             pltpu.VMEM((16, PACK), BF),
@@ -242,6 +296,8 @@
             pltpu.VMEM(rows, BF),
             pltpu.VMEM((32, 1, 128), jnp.int32),
             pltpu.VMEM(flat, BF),
+            pltpu.VMEM(experts_in, BF),
+            pltpu.VMEM((FF // 2, MODEL_WIDTH // 4), BF),
             pltpu.SemaphoreType.DMA((3, 7, 3)),
             pltpu.SemaphoreType.DMA((3, 7, 3)),
             pltpu.SemaphoreType.DMA((6,)),
@@ -249,11 +305,11 @@
             pltpu.SemaphoreType.DMA,
             pltpu.SemaphoreType.DMA((2,)),
             pltpu.SemaphoreType.DMA((2,)),
-            pltpu.SemaphoreType.DMA((5,)),
+            pltpu.SemaphoreType.DMA((8,)),
         ],
         compiler_params=params(1, 60 << 20),
         name="gather_weights",
-    )(w_query, w_key, w_value, w_out, extra, tokens, segs)
+    )(*vmem_args, *hbm_args)
 
 
 def offset(k):
@@ -277,18 +333,17 @@
     return (k // 8) * 16 + core * 8 + k % 8
 
 
-def plane_greet(y, me, c, sibling):
+def plane_greet():
+    y, z, x, c = coords()
+    me = z * 4 + x
+
     def greet(k, carry):
         t = (me + k) % 16
         signal(dev(y, t // 4, t % 4, c))
         return carry
 
     lax.fori_loop(1, 16, greet, 0)
-    if sibling is not None:
-        signal(sibling)
-        pl.semaphore_wait(pltpu.get_barrier_semaphore(), 16)
-    else:
-        pl.semaphore_wait(pltpu.get_barrier_semaphore(), 15)
+    signal(dev(y, z, x, 1 - c))
 
 
 KEYS = 1024
@@ -492,22 +547,48 @@
 
 
 def experts_kernel(
-    xs, gates, cots, weights, out_ret, grad_ret, d_all,
+    attn, tokens, extra, ids, cotangent, half_w, sib_w, cots, weights,
+    o_block, o_middle, o_branch, o_heads, o_moe, o_logits, o_gain, d_all,
     x_all, t_all, g_all, w_all, gate_v, up_v, hidden, g_both, part_o, part_g, sib_o, sib_g,
-    v_all,
+    v_all, wh, ws, xs, gates, out_ret, grad_ret, middle, moe_in,
     w_sem, l_sem, send, recv, f_send, f_recv, s_send, s_recv, r_send, r_recv, o_sem,
 ):
     y, z, x, c = coords()
     me = z * 4 + x
     width = hidden.shape[1]
     sibling = dev(y, z, x, 1 - c)
-    plane_greet(y, me, c, sibling)
     loads = [
         pltpu.make_async_copy(src, dst, w_sem.at[n])
-        for n, (src, dst) in enumerate(((weights, w_all), (cots, g_all)))
+        for n, (src, dst) in enumerate(((half_w, wh), (sib_w, ws), (weights, w_all), (cots, g_all)))
     ]
+    plane_greet()
     for load in loads:
         load.start()
+    chosen, hits = slot_hits(ids[...])
+    both_hits = (hits[0] + hits[1]).astype(BF)
+    flat_extra = extra[...].reshape(MODEL_WIDTH, EXTRA)
+    gain = jnp.transpose(flat_extra.astype(F32))[EXPERT_COUNT + 1 : EXPERT_COUNT + 2]
+    own = attn[pl.ds(c * 4, 4)].reshape(Q_HALF, ROWS)
+    other = attn[pl.ds((1 - c) * 4, 4)].reshape(Q_HALF, ROWS)
+    loads[0].wait()
+    loads[1].wait()
+    middle[...] = (
+        tokens[...].astype(F32)
+        + dot(own, wh[...].reshape(MODEL_WIDTH, Q_HALF), ((0,), (1,)))
+        + dot(other, ws[...].reshape(MODEL_WIDTH, Q_HALF), ((0,), (1,)))
+    )
+    inverse = inverse_rms(middle[...])
+    moe_in[...] = (middle[...] * inverse * gain).astype(BF)
+    logits = dot(moe_in[...], flat_extra, ((1,), (0,)))
+    picked = [jnp.sum(chosen[k] * logits, axis=1, keepdims=True) for k in range(2)]
+    most = jnp.maximum(picked[0], picked[1])
+    lifted = [jnp.exp(value - most) for value in picked]
+    share = [value / (lifted[0] + lifted[1]) for value in lifted]
+    slots_in = dot(both_hits, moe_in[...], ((0,), (0,))).astype(BF)
+    xs[...] = slots_in.reshape(EXPERT_COUNT, SLOTS, MODEL_WIDTH)
+    slot_gate = jnp.sum(hits[0] * share[0] + hits[1] * share[1], axis=0, keepdims=True)
+    gates[...] = column_of(slot_gate).reshape(EXPERT_COUNT, SLOTS, 128)
+    pl.semaphore_wait(pltpu.get_barrier_semaphore(), 16)
     arrays = ((xs, x_all), (gates, t_all))
 
     def arriving(a, k):
@@ -615,8 +696,8 @@
     scatter(1, 0)
     scatter(0, 1)
     scatter(1, 1)
-    for load in loads:
-        load.wait()
+    loads[2].wait()
+    loads[3].wait()
     hand_over(0, 0)
     settle(0, 0)
     forward_pass(0)
@@ -647,20 +728,49 @@
     lax.fori_loop(0, MODEL_WIDTH // 256, weight_grads, 0)
     store = pltpu.make_async_copy(v_all, d_all, o_sem)
     store.start()
+    given(part_o, out_ret, 0)
+    grad_out = cotangent[...].astype(F32)
+    rows_out = [dot(hits[k].astype(BF), flat_rows(out_ret[...]), ((1,), (0,))) for k in range(2)]
+    o_block[...] = (middle[...] + share[0] * rows_out[0] + share[1] * rows_out[1]).astype(BF)
+    pairs = [jnp.sum(grad_out * rows, axis=1, keepdims=True) for rows in rows_out]
+    mean = share[0] * pairs[0] + share[1] * pairs[1]
+    grad_logits = sum(chosen[k] * (share[k] * (pairs[k] - mean)) for k in range(2))
+    o_logits[...] = grad_logits
+    o_moe[...] = moe_in[...]
+    routed = sum(dot(part, flat_extra, ((1,), (1,))) for part in three_parts(grad_logits))
+    given(part_g, grad_ret, 1)
+    grad_moe = dot(both_hits, flat_rows(grad_ret[...]), ((1,), (0,))) + routed
+    o_gain[...] = jnp.sum(grad_moe * middle[...] * inverse, axis=0, keepdims=True)
+    grad_middle = grad_out + norm_backward(middle[...], inverse, gain, grad_moe)
+    o_middle[...] = grad_middle
+    branch = grad_middle.astype(BF)
+    o_branch[...] = branch
+    for core, weight in ((c, wh), (1 - c, ws)):
+        heads = dot(weight[...].reshape(MODEL_WIDTH, Q_HALF), branch, ((0,), (1,))).astype(BF)
+        o_heads[pl.ds(core * 4, 4)] = heads.reshape(4, HEAD_Q, ROWS)
     store.wait()
-    given(part_o, out_ret, 0)
-    given(part_g, grad_ret, 1)
-
-
-def experts(xs, gates, cots, weights):
+
+
+def experts(attn, tokens, extra, ids, cotangent, half_w, sib_w, cots, weights):
     rows = 32 * SLOTS
     width = weights.shape[1] // 3
-    back = jax.ShapeDtypeStruct((16, SLOTS, MODEL_WIDTH), BF)
+    slots = (16, SLOTS, MODEL_WIDTH)
+    flat = (ROWS, MODEL_WIDTH)
+    low = jax.ShapeDtypeStruct(flat, BF)
     return pl.pallas_call(
         experts_kernel,
-        out_shape=[back, back, jax.ShapeDtypeStruct(weights.shape, BF)],
-        in_specs=[ANY] * 4,
-        out_specs=[ANY] * 3,
+        out_shape=[
+            low,
+            jax.ShapeDtypeStruct(flat, F32),
+            low,
+            jax.ShapeDtypeStruct((8, HEAD_Q, ROWS), BF),
+            low,
+            jax.ShapeDtypeStruct((ROWS, 128), F32),
+            jax.ShapeDtypeStruct((1, MODEL_WIDTH), F32),
+            jax.ShapeDtypeStruct(weights.shape, BF),
+        ],
+        in_specs=[IN_VMEM] * 5 + [ANY] * 4,
+        out_specs=[IN_VMEM] * 7 + [ANY],
         scratch_shapes=[
             pltpu.VMEM((32, SLOTS, MODEL_WIDTH), BF),
             pltpu.VMEM((32, SLOTS, 128), F32),
@@ -675,7 +785,15 @@
             pltpu.VMEM((16, SLOTS, MODEL_WIDTH), BF),
             pltpu.VMEM((16, SLOTS, MODEL_WIDTH), BF),
             pltpu.VMEM(weights.shape, BF),
-            pltpu.SemaphoreType.DMA((2,)),
+            pltpu.VMEM(half_w.shape, BF),
+            pltpu.VMEM(half_w.shape, BF),
+            pltpu.VMEM(slots, BF),
+            pltpu.VMEM((EXPERT_COUNT, SLOTS, 128), F32),
+            pltpu.VMEM(slots, BF),
+            pltpu.VMEM(slots, BF),
+            pltpu.VMEM(flat, F32),
+            pltpu.VMEM(flat, BF),
+            pltpu.SemaphoreType.DMA((4,)),
             pltpu.SemaphoreType.DMA((4,)),
             pltpu.SemaphoreType.DMA((2, 16)),
             pltpu.SemaphoreType.DMA((2, 16)),
@@ -689,7 +807,7 @@
         ],
         compiler_params=params(6, 60 << 20),
         name="experts",
-    )(xs, gates, cots, weights)
+    )(attn, tokens, extra, ids, cotangent, half_w, sib_w, cots, weights)
 
 
 SUMS = tuple((n, start, width, order[::-1]) for n, start, width, order in FIRST_PARTS) + tuple(
@@ -699,7 +817,7 @@
 
 
 def reduce_kernel(
-    gq_t, dkv, normed, g_moe, s_out, pair, gain, grad_middle, w_q, w_kv,
+    gq_t, dkv, normed, moe_in, grad_logits, gain_m, s_out, pair, w_extra, grad_middle, w_q, w_kv,
     o_tokens, o_q, o_k, o_v, o_out, o_extra,
     v_q, v_kv, v_extra, wq, wkv, gkv, mine_part, give_part, sib_part, both, total, give, *rest,
 ):
@@ -797,16 +915,18 @@
             remote(give_part, sib_part, sib_send.at[0], sib_recv.at[0], sibling).start()
         else:
             mine_part[...] = part
-    column = jnp.transpose(jnp.broadcast_to(gain_sum, (EXTRA, MODEL_WIDTH)))
     lane = lax.broadcasted_iota(jnp.int32, (MODEL_WIDTH, EXTRA), 1)
-    extra = g_moe[...] + jnp.where(lane == EXPERT_COUNT, column, 0.0)
+    extra = sum(dot(moe_in[...], part, ((0,), (0,))) for part in three_parts(grad_logits[...]))
+    extra = jnp.where(lane == EXPERT_COUNT, column_of(gain_sum), extra)
+    extra = jnp.where(lane == EXPERT_COUNT + 1, column_of(gain_m[...]), extra)
+    gain = jnp.transpose(w_extra[...].reshape(MODEL_WIDTH, EXTRA).astype(F32))[EXPERT_COUNT : EXPERT_COUNT + 1]
     v_extra[...] = extra.astype(BF).reshape(4, 4, 4, 24, EXTRA)
     begin(0, 3)
     remote(give_part, sib_part, sib_send.at[0], sib_recv.at[0], sibling).wait()
     rows = pl.ds(pl.multiple_of(c * ROWS, ROWS), ROWS)
     values = pair[rows].astype(F32)
     o_tokens[...] = grad_middle[...] + norm_backward(
-        values, inverse_rms(values), gain[...], mine_part[...] + sib_part[...]
+        values, inverse_rms(values), gain, mine_part[...] + sib_part[...]
     )
 
     for part in range(LATE, parts):
@@ -839,7 +959,7 @@
     o_extra[...] = both[0, 0:12, STARTS[3] :] + both[1, 0:12, STARTS[3] :]
 
 
-def reduce_weights(gq_t, dkv, normed, g_moe, s_out, pair, gain, grad_middle, w_q, w_kv):
+def reduce_weights(*args):
     widths = [part[2] for part in SUMS]
     full = lambda width: pltpu.VMEM((4, 4, 4, 24, width), BF)
     rows = pltpu.VMEM((ROWS, MODEL_WIDTH), F32)
@@ -859,7 +979,7 @@
     return pl.pallas_call(
         reduce_kernel,
         out_shape=[jax.ShapeDtypeStruct(shape, F32) for shape in shapes],
-        in_specs=[IN_VMEM] * 8 + [ANY] * 2,
+        in_specs=[IN_VMEM] * 10 + [ANY] * 2,
         out_specs=[IN_VMEM] * 6,
         scratch_shapes=scratch
         + [
@@ -871,7 +991,7 @@
         ],
         compiler_params=params(8, 60 << 20),
         name="reduce_weights",
-    )(gq_t, dkv, normed, g_moe, s_out, pair, gain, grad_middle, w_q, w_kv)
+    )(*args)
 
 
 def wide_greet():
@@ -892,7 +1012,7 @@
 
 
 def attend_back_kernel(
-    heads, branch, own_attn, other_attn, q_in, kv_in, first_ref, ot_ref, lse_ref,
+    heads, branch, attn, q_in, kv_in, first_ref, ot_ref, lse_ref,
     dq_out, dkv_out, s_out,
     go, branch_sib, attn_sib, qs, gs, dq, dkv, dkv_low, dq_low,
     g_out, a_out,
@@ -914,7 +1034,7 @@
     lax.fori_loop(1, 8, push, 0)
     one = remote(branch, branch_sib, sib_send.at[0], sib_recv.at[0], sibling)
     one.start()
-    two = remote(other_attn, attn_sib, sib_send.at[1], sib_recv.at[1], sibling)
+    two = remote(attn.at[pl.ds((1 - c) * 4, 4)], attn_sib, sib_send.at[1], sib_recv.at[1], sibling)
     two.start()
     here = pltpu.make_async_copy(heads.at[j], go.at[j], l_sem.at[0])
     here.start()
@@ -926,7 +1046,9 @@
     two.wait()
 
     rows_b = jnp.concatenate([branch[...], branch_sib[...]], axis=0)
-    rows_a = jnp.concatenate([own_attn[...], attn_sib[...]], axis=1)
+    rows_a = jnp.concatenate(
+        [part.reshape(Q_HALF, ROWS) for part in (attn[pl.ds(c * 4, 4)], attn_sib[...])], axis=1
+    )
     for n in range(4):
         part = dot(rows_b[:, 384 * n : 384 * n + 384], rows_a, ((0,), (1,)))
         g_out[n] = part.astype(BF).reshape(4, 4, 24, Q_HALF)
@@ -1040,7 +1162,7 @@
     drain.wait_recv()
 
 
-def attend_back(heads, branch, own_attn, other_attn, q_in, kv_in, first, ot, lse):
+def attend_back(heads, branch, attn, q_in, kv_in, first, ot, lse):
     return pl.pallas_call(
         attend_back_kernel,
         out_shape=[
@@ -1048,12 +1170,12 @@
             jax.ShapeDtypeStruct((16, PAIR, 128), BF),
             jax.ShapeDtypeStruct((3, 4, 4, 24, 256), BF),
         ],
-        in_specs=[ANY] + [IN_VMEM] * 8,
+        in_specs=[ANY] + [IN_VMEM] * 7,
         out_specs=[ANY, ANY, IN_VMEM],
         scratch_shapes=[
             pltpu.VMEM((8, HEAD_Q, ROWS), BF),
             pltpu.VMEM((ROWS, MODEL_WIDTH), BF),
-            pltpu.VMEM((Q_HALF, ROWS), BF),
+            pltpu.VMEM((4, HEAD_Q, ROWS), BF),
             pltpu.VMEM((128, 3 * PAIR), BF),
             pltpu.VMEM((128, 3 * PAIR), BF),
             pltpu.VMEM((128, 3 * PAIR), F32),
@@ -1076,7 +1198,7 @@
         ],
         compiler_params=params(4, 60 << 20),
         name="attend_back",
-    )(heads, branch, own_attn, other_attn, q_in, kv_in, first, ot, lse)
+    )(heads, branch, attn, q_in, kv_in, first, ot, lse)
 
 
 def inverse_rms(values):
@@ -1086,14 +1208,6 @@
 def norm_backward(values, inverse, gain, grad_out):
     scaled = grad_out * gain
     return inverse * scaled - values * inverse**3 * jnp.mean(values * scaled, axis=-1, keepdims=True)
-
-
-def column_sums(left, right):
-    return lax.dot_general(left, right, (((0,), (0,)), ((), ())), precision=HIGH_PRECISION)
-
-
-def only_column(rows, column):
-    return jnp.broadcast_to((jnp.arange(EXTRA) == column).astype(F32), (rows, EXTRA))
 
 
 def local(
@@ -1112,92 +1226,27 @@
     w_down,
     cotangent,
 ):
-    y, z, x, c = coords()
     width = w_gate.shape[1]
-    extra = jnp.concatenate(
-        [w_router, gain_attn[:, None], gain_moe[:, None], jnp.zeros((12, EXTRA - 18), BF)], axis=1
-    )
-    part_q, part_kv, part_out, part_extra, pair, normed, q4, keys_values, first = gather_weights(
-        w_query, w_key, w_value, w_out.T, extra, tokens, segment_ids
-    )
-    pair, w_gate, w_up, w_down = lax.optimization_barrier((pair, w_gate, w_up, w_down))
-    w_experts = jnp.concatenate([w_gate, w_up, w_down.T], axis=1)
+    ids = expert_ids.T
+    part_q, part_kv, part_out, part_extra, pair, normed, w_experts, q4, keys_values, first, cot_slots = (
+        gather_weights(
+            (w_query, w_key, w_value, w_out.T, w_router, gain_attn[None], gain_moe[None], ids, cotangent),
+            (tokens, segment_ids, w_gate, w_up, w_down),
+        )
+    )
     full_experts = lax.all_gather(w_experts, "dp", axis=0, tiled=True)
-    full_q = part_q.reshape(MODEL_WIDTH, Q_HALF)
-    full_kv = part_kv.reshape(MODEL_WIDTH, KV_HALF)
-    full_extra = part_extra.reshape(MODEL_WIDTH, EXTRA)
-    picks = (jnp.arange(EXTRA)[None, :] == jnp.arange(8)[:, None] + EXPERT_COUNT).astype(BF)
-    gains = dot(picks, full_extra, ((1,), (1,)))
-    gain_a, gain_m = gains[0:1], gains[1:2]
-    router = full_extra[:, :EXPERT_COUNT]
-
-    chosen = (expert_ids[:, :, None] == jnp.arange(EXPERT_COUNT, dtype=jnp.int32)).astype(F32)
-    used = jnp.sum(chosen, axis=1)
-    earlier = (jnp.arange(ROWS)[:, None] > jnp.arange(ROWS)[None, :]).astype(BF)
-    before = dot(earlier, used.astype(BF), ((1,), (0,)))
-    place = jnp.sum(chosen * before[:, None, :], axis=-1)
-    slot = jnp.where(
-        place < EXPERT_CAPACITY, expert_ids * SLOTS + place.astype(jnp.int32), -1
-    )
-    hit = (slot.T[:, :, None] == jnp.arange(EXPERT_COUNT * SLOTS, dtype=jnp.int32)).astype(F32)
-    both = (hit[0] + hit[1]).astype(BF)
-    blocks = (EXPERT_COUNT, SLOTS, MODEL_WIDTH)
-    cot_slots = dot(both, cotangent, ((0,), (0,))).astype(BF)
     q_in, kv_in, attn, attn_t, lse, half_out, sib_out, cot_all = attend(
-        q4, keys_values, part_out, cot_slots.reshape(blocks), first
-    )
-    half_out = half_out.reshape(MODEL_WIDTH, Q_HALF)
-    sib_out = sib_out.reshape(MODEL_WIDTH, Q_HALF)
-    attn = attn.reshape(2, Q_HALF, ROWS)
-
-    own_attn = jnp.where(c == 0, attn[0], attn[1])
-    other_attn = jnp.where(c == 0, attn[1], attn[0])
-    inputs = tokens.astype(F32)
-    middle = (
-        inputs
-        + dot(own_attn, half_out, ((0,), (1,)))
-        + dot(other_attn, sib_out, ((0,), (1,)))
-    )
-    inverse_m = inverse_rms(middle)
-    moe_in = (middle * inverse_m * gain_m).astype(BF)
-    logits = dot(moe_in, router, ((1,), (0,)))
-    picked = jnp.sum(chosen * logits[:, None, :], axis=-1)
-    gates = jax.nn.softmax(picked, axis=-1)
-    slot_gate = jnp.sum(hit * gates.T[:, :, None], axis=(0, 1))
-    slots_in = dot(both, moe_in, ((0,), (0,))).astype(BF)
-    slot_gate = jnp.broadcast_to(slot_gate.reshape(EXPERT_COUNT, SLOTS, 1), (EXPERT_COUNT, SLOTS, 128))
-    out_ret, grad_ret, grad_experts = experts(
-        slots_in.reshape(blocks), slot_gate, cot_all, full_experts
+        q4, keys_values, part_out, cot_slots, first
+    )
+    block_out, grad_middle, branch, grad_heads, moe_in, grad_logits, gain_sum, grad_experts = experts(
+        attn, tokens, part_extra, ids, cotangent, half_out, sib_out, cot_all, full_experts
     )
     sum_experts = lax.psum_scatter(grad_experts, "dp", scatter_dimension=0, tiled=True)
-
-    grad_output = cotangent.astype(F32)
-    out_ret = out_ret.reshape(EXPERT_COUNT * SLOTS, MODEL_WIDTH)
-    grad_ret = grad_ret.reshape(EXPERT_COUNT * SLOTS, MODEL_WIDTH)
-    rows_out = [dot(hit[k].astype(BF), out_ret, ((1,), (0,))) for k in range(2)]
-    block_out = (middle + gates[:, 0:1] * rows_out[0] + gates[:, 1:2] * rows_out[1]).astype(BF)
-    grad_pair = jnp.stack([jnp.sum(grad_output * rows, axis=-1) for rows in rows_out], axis=-1)
-    grad_pick = gates * (grad_pair - jnp.sum(gates * grad_pair, axis=-1, keepdims=True))
-    grad_logits = jnp.sum(chosen * grad_pick[:, :, None], axis=1)
-    grad_moe_in = dot(both, grad_ret, ((1,), (0,))) + lax.dot_general(
-        grad_logits, router.astype(F32), (((1,), (1,)), ((), ())), precision=HIGH_PRECISION
-    )
-    g_router = column_sums(moe_in.astype(F32), jnp.pad(grad_logits, ((0, 0), (0, EXTRA - EXPERT_COUNT))))
-    g_gain_m = column_sums(grad_moe_in * middle * inverse_m, only_column(ROWS, EXPERT_COUNT + 1))
-    grad_middle = grad_output + norm_backward(middle, inverse_m, gain_m, grad_moe_in)
-    branch = grad_middle.astype(BF)
-    own_heads = dot(half_out, branch, ((0,), (1,))).astype(BF)
-    other_heads = dot(sib_out, branch, ((0,), (1,))).astype(BF)
-    grad_heads = jnp.stack(
-        [jnp.where(c == 0, own_heads, other_heads), jnp.where(c == 0, other_heads, own_heads)]
-    )
-    dq_in, dkv_in, sum_out = attend_back(
-        grad_heads.reshape(8, HEAD_Q, ROWS), branch, own_attn, other_attn, q_in, kv_in, first,
-        attn_t, lse,
-    )
+    dq_in, dkv_in, sum_out = attend_back(grad_heads, branch, attn, q_in, kv_in, first, attn_t, lse)
     grad_tokens, r_query, r_key, r_value, r_out, r_extra = reduce_weights(
-        dq_in.reshape(Q_HALF, PAIR), dkv_in, normed, g_router + g_gain_m, sum_out,
-        pair.reshape(PAIR, MODEL_WIDTH), gain_a, grad_middle, full_q, full_kv,
+        dq_in.reshape(Q_HALF, PAIR), dkv_in, normed, moe_in, grad_logits, gain_sum, sum_out,
+        pair.reshape(PAIR, MODEL_WIDTH), part_extra, grad_middle,
+        part_q.reshape(MODEL_WIDTH, Q_HALF), part_kv.reshape(MODEL_WIDTH, KV_HALF),
     )
     return (
         block_out,

time: 314 us -> 293 us (0.933)
  matrix products: 14.4 us -> 0 us
  Pallas kernels: 260 us -> 268 us
  other arithmetic: 10.2 us -> 2.8 us
  local copies, waits for them, and re-layouts: 14.4 us -> 7.38 us
    dot_general x15 -> x0, matrix products: 14.4 us -> none  [the longest x12 10.8 us: dot(): return lax.dot_general(a, b, (dims, ((), ())), preferred_element_type=F32)]
    pallas_call x1, Pallas kernels: 51.1 us -> 58.9 us  [experts(): pl.pallas_call(experts_kernel, out_shape=[low, jax.ShapeDtypeStruct(flat,...]
    concatenate x2 -> x0, other arithmetic: 3.62 us -> none  [the longest x1 2.25 us: local(): w_experts = jnp.concatenate([w_gate, w_up, w_down.T], axis=1)]
    unnamed x49 -> x22, local copies, waits for them, and re-layouts: 8.71 us -> 5.91 us
  transfers between devices with their start and end apart: 2 -> 2, of which waited for: 0 -> 0; matrix products, arithmetic and copies ran while one was open for 6% -> 1% of each run, Pallas kernels for 52% -> 55%
where the time goes in v6:
time: 293 us
  Pallas kernels  268 us (91%)
  between operations  14.1 us (5%)
  local copies, waits for them, and re-layouts  7.38 us (3%)
    pallas_call x1, Pallas kernels, attend_back(): pl.pallas_call(attend_back_kernel, out_shape=[jax.ShapeDtypeStruct((4, HE...  59.6 us
    pallas_call x1, Pallas kernels, experts(): pl.pallas_call(experts_kernel, out_shape=[low, jax.ShapeDtypeStruct(flat,...  58.9 us
    pallas_call x1, Pallas kernels, attend(): pl.pallas_call(attend_kernel, out_shape=[jax.ShapeDtypeStruct((4, HEAD_Q,...  57.1 us
    pallas_call x1, Pallas kernels, gather_weights(): pl.pallas_call(gather_kernel, out_shape=[jax.ShapeDtypeStruct(shape, BF)...  47.3 us
    pallas_call x1, Pallas kernels, reduce_weights(): pl.pallas_call(reduce_kernel, out_shape=[jax.ShapeDtypeStruct(shape, F32)...  45.2 us
    unnamed x22, local copies, waits for them, and re-layouts  5.91 us
  transfers between devices with their start and end apart: 2, of which 0 were waited for; matrix products, arithmetic and copies ran while one was open for 1% of the time, Pallas kernels for 55%

profile of v6, /device:TPU:1, one launch (start us, length us, event | category | flops | bytes accessed | tf_op | source)
XLA Modules:
  0.0 292.5 jit_solution(6689621537657509005)
XLA Ops:
  7.2 0.0 all-gather.2.cloned.1.call-start
  7.2 47.3 %gather_weights.1 = (bf16[4,4,4,24,768]{4,3,2,1,0:T(8,128)(2,1)}, bf16[4,4,4,24,512]{4,3,2,1,0:T(8,128)(2,1)}, bf16[4,4,4,24,768]{4,3,2,1,0:T(8,128)(2,1)}, bf16...) custom-call(bf16[12,1536]{1,0:T(8,128)(2,1)} %w_query.1, ...), custom_call_target="tpu_custom_call" | custom-call | tf_op jit(solution)/shard_map/gather_weights/pallas_call | solution.py:278
  54.5 0.0 all-gather.2.cloned.1.call-update
  54.6 0.0 reduce-scatter.2.cloned.1.call-start
  54.6 57.1 %attend.1 = (bf16[4,192,256]{2,1,0:T(8,128)(2,1)}, bf16[16,256,128]{2,1,0:T(8,128)(2,1)}, bf16[8,192,128]{2,1,0:T(8,128)(2,1)}, f32[4,64,768]{2,1,0:T(8,128)}, f...) custom-call(bf16[4,192,256]{2,1,0:T(8,128)(2,1)} %get-tuple-element., ...), custom_call_target="tpu_custom_call", output_to_operand_aliasing={{5}: (2, {})} | custom-call | tf_op jit(solution)/shard_map/attend/pallas_call | solution.py:505
  111.7 0.0 all-gather.2.cloned.1.call-done.weights
  111.7 58.9 %experts.1 = (bf16[128,1536]{1,0:T(8,128)(2,1)}, f32[128,1536]{1,0:T(8,128)}, bf16[128,1536]{1,0:T(8,128)(2,1)}, bf16[8,192,128]{2,1,0:T(8,128)(2,1)}, bf16[128,...) custom-call(bf16[8,192,128]{2,1,0:T(8,128)(2,1)} %get-tuple-element.53.attn, ...), custom_call_target="tpu_custom_call" | custom-call | tf_op jit(solution)/shard_map/experts/pallas_call | solution.py:760
  170.6 0.0 reduce-scatter.2.cloned.1.call-update
  170.6 59.6 %attend_back.1 = (bf16[4,192,256]{2,1,0:T(8,128)(2,1)}, bf16[16,256,128]{2,1,0:T(8,128)(2,1)}, bf16[3,4,4,24,256]{4,3,2,1,0:T(8,128)(2,1)}) custom-call(bf16[8,192,128]{2,1,0:T(8,128)(2,1)} %get-tuple-element.60.heads, bf16[128,1536]{1,0:T(8,128)(2,1)} %get-tuple-element.61.branch, bf16[8,192,128]{2,1,0:T(8,128)(2,1)} %get-tuple-element.53.attn, ...), custom_call_target="tpu_custom_call" | custom-call | tf_op jit(solution)/shard_map/attend_back/pallas_call | solution.py:1166
  230.2 45.2 %reduce_weights.1 = (f32[128,1536]{1,0:T(8,128)}, f32[12,1536]{1,0:T(8,128)}, f32[12,512]{1,0:T(8,128)}, f32[12,512]{1,0:T(8,128)}, f32[12,1536]{1,0:T(8,128)}, /*index=5*/f32[12,128]{1,0:T(8,128)}) custom-call(bf16[768,256]{1,0:T(8,128)(2,1)} %bitcast.15, bf16[16,256,128]{2,1,0:T(8,128)(2,1)} %get-tuple-element.67.dkv, ...), custom_call_target="tpu_custom_call" | custom-call | tf_op jit(solution)/shard_map/reduce_weights/pallas_call | solution.py:979
  275.5 1.5 slice_reduce_fusion
  276.9 2.8 convert_bitcast_fusion
  279.7 0.0 copy-start.4
  279.8 1.1 copy.28
  280.9 0.0 copy-done.1
  280.9 0.7 copy.37
  281.7 0.9 copy.38
  282.5 0.0 copy-done.3
  282.5 0.6 copy.39
  283.2 0.6 copy.40
  283.8 0.0 copy-done.5
  283.8 0.6 copy.41
  284.4 0.6 copy.42
  285.1 0.6 copy.43
  (11 shorter events, 0.0 us)
Async XLA Ops:
  7.2 104.5 %all-gather.2.cloned.1.call-start = ((), (), s32[]{:S(2)}) async-start(), calls=%async_computation.1 | async-start | bytes 5898240 | tf_op jit(solution)/shard_map/all_gather | solution.py:1237
  54.6 222.4 %reduce-scatter.2.cloned.1.call-start = ((), (), s32[]{:S(2)}) async-start(), calls=%async_computation.2 | async-start | bytes 5898240 | tf_op jit(solution)/shard_map/reduce_scatter | solution.py:1244
  276.9 4.0 %copy-start.1 = (bf16[128,1536]{1,0:T(8,128)(2,1)S(1)}, bf16[128,1536]{1,0:T(8,128)(2,1)}, u32[]{:S(2)}) copy-start(bf16[128,1536]{1,0:T(8,128)(2,1)} %get-tuple-element.125) | copy-start | bytes 1179652
  276.9 4.7 %copy-start = (f32[128,1536]{1,0:T(8,128)S(1)}, f32[128,1536]{1,0:T(8,128)}, u32[]{:S(2)}) copy-start(f32[128,1536]{1,0:T(8,128)} %get-tuple-element.126) | copy-start | bytes 2359300
  279.7 2.8 copy-start.3
  279.7 3.4 %copy-start.6 = (f32[12,512]{1,0:T(8,128)S(1)}, f32[12,512]{1,0:T(8,128)}, u32[]{:S(2)}) copy-start(f32[12,512]{1,0:T(8,128)} %get-tuple-element.128) | copy-start | bytes 73732
  279.7 4.1 %copy-start.5 = (f32[12,512]{1,0:T(8,128)S(1)}, f32[12,512]{1,0:T(8,128)}, u32[]{:S(2)}) copy-start(f32[12,512]{1,0:T(8,128)} %get-tuple-element.129) | copy-start | bytes 73732
  279.7 4.7 %copy-start.2 = (f32[12,1536]{1,0:T(8,128)S(1)}, f32[12,1536]{1,0:T(8,128)}, u32[]{:S(2)}) copy-start(f32[12,1536]{1,0:T(8,128)} %get-tuple-element.81) | copy-start | bytes 221188
  279.7 5.3 %copy-start.4 = (f32[12,128]{1,0:T(8,128)S(1)}, f32[12,128]{1,0:T(8,128)}, u32[]{:S(2)}) copy-start(f32[12,128]{1,0:T(8,128)} %get-tuple-element.82) | copy-start | bytes 18436
Sparse Core Ops, SparseCore 0:
  54.7 56.1 all-gather.1
  170.8 48.0 reduce-scatter.1
